TPU v7x, 32 devices: a whole 2x2x4 slice. The times are simulated.
32 devices in a mesh: dp: 8 (over y, x, core), seq: 4 (over z).
Axes of the slice: x: 2, y: 2, z: 4, core: 2. Of those that a mesh axis runs over, the one named last changes fastest.
Arguments:
- layer_input: bfloat16 [8, 2048, 768], P('dp', 'seq'), may hold values from -6 to 6
- cotangent: bfloat16 [8, 2048, 768], P('dp', 'seq'), may hold values from -6 to 6
- segment_ids: int32 [8, 2048], P('dp', 'seq'), may hold values from 0 to 8, as said below
- route_index: int32 [8, 3, 256], P('dp'), may hold values from 0 to 2047, as said below
- route_count: int32 [8, 3], P('dp'), may hold values from 128 to 256, as said below
- attn_gain: bfloat16 [768], P(('dp', 'seq')), may hold values from 0.5 to 1.5
- light_qkv: bfloat16 [768, 2304], P(('dp', 'seq')), may hold values from -0.21875 to 0.21875
- light_out: bfloat16 [768, 768], P(('dp', 'seq')), may hold values from -0.875 to 0.875
- heavy_qkv: bfloat16 [768, 2304], P(('dp', 'seq')), may hold values from -0.21875 to 0.21875
- heavy_out: bfloat16 [768, 768], P(('dp', 'seq')), may hold values from -0.875 to 0.875
- attn_router: bfloat16 [768], P(('dp', 'seq')), may hold values from -0.21875 to 0.21875
- ffn_gain: bfloat16 [768], P(('dp', 'seq')), may hold values from 0.5 to 1.5
- light_gate_up: bfloat16 [768, 2048], P(('dp', 'seq')), may hold values from -0.21875 to 0.21875
- light_down: bfloat16 [1024, 768], P(('dp', 'seq')), may hold values from -0.1875 to 0.1875
- heavy_gate_up: bfloat16 [768, 8192], P(('dp', 'seq')), may hold values from -0.21875 to 0.21875
- heavy_down: bfloat16 [4096, 768], P(('dp', 'seq')), may hold values from -0.1875 to 0.1875
- ffn_router: bfloat16 [768], P(('dp', 'seq')), may hold values from -0.21875 to 0.21875
Outputs:
- layer_output: bfloat16 [8, 2048, 768], P('dp', 'seq')
- input_grad: bfloat16 [8, 2048, 768], P('dp', 'seq')
- grad_attn_gain: float32 [768], P(('dp', 'seq'))
- grad_light_qkv: float32 [768, 2304], P(('dp', 'seq'))
- grad_light_out: float32 [768, 768], P(('dp', 'seq'))
- grad_heavy_qkv: float32 [768, 2304], P(('dp', 'seq'))
- grad_heavy_out: float32 [768, 768], P(('dp', 'seq'))
- grad_attn_router: float32 [768], P(('dp', 'seq'))
- grad_ffn_gain: float32 [768], P(('dp', 'seq'))
- grad_light_gate_up: float32 [768, 2048], P(('dp', 'seq'))
- grad_light_down: float32 [1024, 768], P(('dp', 'seq'))
- grad_heavy_gate_up: float32 [768, 8192], P(('dp', 'seq'))
- grad_heavy_down: float32 [4096, 768], P(('dp', 'seq'))
- grad_ffn_router: float32 [768], P(('dp', 'seq'))
Inputs may be any that keep to these rules, and one draw needn't show every extreme that they name: `segment_ids`: segment ids never fall along a row; in each row one segment begins within the first 512 tokens and ends within the last 512. `route_index`: for each row and set the first route_count slots hold distinct positions of the row in increasing order, later slots repeat the first position; every position of set 0 is also a position of set 1. `route_count`: in every draw each set has 256 live slots in some row; a row's count of set 1 is at least its count of set 0.
All inputs are finite; a program needn't handle non-finite values.
Results may differ from a plain program's by a relative error of at most 0.017.
Values may be sent and summed in bfloat16 or wider, within the bound.
No kernel may reach another device: no remote copies, remote signals or barrier semaphores. Data moves between devices by JAX's collectives and lax.ppermute only.
A program may use at most 256 MiB of HBM per device.

v0:
```python
import jax
import jax.numpy as jnp
from jax import lax
from jax.sharding import PartitionSpec as P

L_HEADS = 8
L_HEAD = 96
H_HEADS = 12
H_HEAD = 64
WINDOW = 128


epsilon = 1e-06
masked_score = -1e30
gelu_scale = 0.7978845608028654


def as_sent(x):
    return jax.tree.map(lambda a: a.astype(jnp.bfloat16) if a.dtype == jnp.float32 else a, x)


def extended_2(cells, sides, width):
    for axis, dim in sides:
        count = lax.axis_size(axis)
        ends = count - 1
        head = lax.slice_in_dim(cells, 0, width, axis=dim)
        tail = lax.slice_in_dim(cells, cells.shape[dim] - width, cells.shape[dim], axis=dim)
        cells = jnp.concatenate(
            [
                lax.ppermute(tail, axis, [(i, (i + 1) % count) for i in range(ends)]),
                cells,
                lax.ppermute(head, axis, [((i + 1) % count, i) for i in range(ends)]),
            ],
            axis=dim,
        )
    return cells


def rms_norm(values, gain_vec):
    return (
        values * lax.rsqrt(jnp.mean(values * values, axis=-1, keepdims=True) + epsilon) * gain_vec
    )


def gelu_tanh(values):
    return (
        0.5 * values * (1.0 + jnp.tanh(gelu_scale * (values + 0.044715 * values * values * values)))
    )


def sigmoid(values):
    return 1.0 / (1.0 + jnp.exp(-values))


def plain_unit(gate_part, up_part):
    return gelu_tanh(gate_part) * up_part


def gated_unit(gate_part, up_part, score_part):
    return sigmoid(score_part)[..., None] * gelu_tanh(gate_part) * up_part


def gate_mix(score_part, mixed_part):
    return sigmoid(score_part)[..., None] * mixed_part


def matmul(left_side, right_side):
    return jnp.einsum("...d,de->...e", left_side, right_side, preferred_element_type=jnp.float32)


def matmul_back(left_side, right_side):
    return jnp.einsum("...e,de->...d", left_side, right_side, preferred_element_type=jnp.float32)


def outer_sum(left_side, right_side):
    return jnp.einsum("...d,...e->de", left_side, right_side, preferred_element_type=jnp.float32)


def route_table(route_index, route_count, which_set, token_pos):
    slot_positions = route_index[:, which_set, :]
    is_live = jnp.arange(slot_positions.shape[1])[None, :] < route_count[:, which_set][:, None]
    matched = (slot_positions[:, :, None] == token_pos[None, None, :]) & is_live[:, :, None]
    return matched.astype(jnp.bfloat16)


def routed_rows(tables, sources):
    partial_rows = tuple(
        (
            jnp.einsum("rjt,rtd->rjd", routing, source, preferred_element_type=jnp.float32)
            for routing, source in zip(tables, sources)
        )
    )
    summed = jax.tree.map(
        lambda part: part.astype(jnp.float32),
        lax.psum_scatter(as_sent(partial_rows), "seq", scatter_dimension=1, tiled=True),
    )
    return tuple((member.astype(jnp.bfloat16) for member in summed))


def home_rows(tables, sources):
    gathered = jax.tree.map(
        lambda part, own: part.astype(own.dtype),
        lax.all_gather(as_sent(sources), "seq", axis=1, tiled=True),
        sources,
    )
    summed_rows = 0.0
    for routing, member in zip(tables, gathered):
        summed_rows = summed_rows + jnp.einsum(
            "rjt,rjd->rtd", routing, member, preferred_element_type=jnp.float32
        )
    return summed_rows


def light_scores(queries, extended, allowed):
    stretch_len, inner_dim = queries.shape
    head_q = queries.reshape(stretch_len, L_HEADS, L_HEAD)
    head_k = extended[:, :inner_dim].reshape(-1, L_HEADS, L_HEAD)
    scores = jnp.einsum(
        "qhe,khe->hqk", head_q, head_k, preferred_element_type=jnp.float32
    ) * L_HEAD ** (-0.5)
    return jnp.where(allowed[None], scores, masked_score)


def light_forward_row(packed):
    queries, extended, allowed = packed
    stretch_len, inner_dim = queries.shape
    scores = light_scores(queries, extended, allowed)
    head_v = extended[:, inner_dim:].reshape(-1, L_HEADS, L_HEAD)
    largest = jnp.max(scores, axis=-1, keepdims=True)
    raised = jnp.exp(scores - largest)
    row_sum = jnp.sum(raised, axis=-1, keepdims=True)
    soft_probs = (raised / row_sum).astype(jnp.bfloat16)
    mixed_out = jnp.einsum("hqk,khe->qhe", soft_probs, head_v, preferred_element_type=jnp.float32)
    return (
        mixed_out.reshape(stretch_len, inner_dim).astype(jnp.bfloat16),
        (largest + jnp.log(row_sum))[..., 0],
    )


def light_backward_row(packed):
    queries, extended, allowed, log_sum, grad_mixed = packed
    stretch_len, inner_dim = queries.shape
    head_scale = L_HEAD ** (-0.5)
    scores = light_scores(queries, extended, allowed)
    soft_probs = jnp.where(allowed[None], jnp.exp(scores - log_sum[..., None]), 0.0)
    head_q = queries.reshape(stretch_len, L_HEADS, L_HEAD)
    head_k = extended[:, :inner_dim].reshape(-1, L_HEADS, L_HEAD)
    head_v = extended[:, inner_dim:].reshape(-1, L_HEADS, L_HEAD)
    head_g = grad_mixed.reshape(stretch_len, L_HEADS, L_HEAD)
    grad_probs = jnp.einsum("qhe,khe->hqk", head_g, head_v, preferred_element_type=jnp.float32)
    inner_sum = jnp.sum(soft_probs * grad_probs, axis=-1, keepdims=True)
    grad_scores = (soft_probs * (grad_probs - inner_sum)).astype(jnp.bfloat16)
    grad_q = (
        jnp.einsum("hqk,khe->qhe", grad_scores, head_k, preferred_element_type=jnp.float32)
        * head_scale
    )
    grad_k = (
        jnp.einsum("hqk,qhe->khe", grad_scores, head_q, preferred_element_type=jnp.float32)
        * head_scale
    )
    grad_v = jnp.einsum(
        "hqk,qhe->khe", soft_probs.astype(jnp.bfloat16), head_g, preferred_element_type=jnp.float32
    )
    key_len = extended.shape[0]
    return (
        grad_q.reshape(stretch_len, inner_dim),
        jnp.concatenate(
            [grad_k.reshape(key_len, inner_dim), grad_v.reshape(key_len, inner_dim)], axis=-1
        ),
    )


def heavy_scores(heavy_q, heavy_kv_all, allowed):
    batch_rows, slot_count, heavy_width = heavy_q.shape
    head_q = heavy_q.reshape(batch_rows, slot_count, H_HEADS, H_HEAD)
    head_k = heavy_kv_all[..., :heavy_width].reshape(batch_rows, -1, H_HEADS, H_HEAD)
    scores = jnp.einsum(
        "rqhe,rkhe->rhqk", head_q, head_k, preferred_element_type=jnp.float32
    ) * H_HEAD ** (-0.5)
    return jnp.where(allowed[:, None], scores, masked_score)


def heavy_forward(heavy_q, heavy_kv_all, allowed):
    batch_rows, slot_count, heavy_width = heavy_q.shape
    scores = heavy_scores(heavy_q, heavy_kv_all, allowed)
    head_v = heavy_kv_all[..., heavy_width:].reshape(batch_rows, -1, H_HEADS, H_HEAD)
    largest = jnp.max(scores, axis=-1, keepdims=True)
    raised = jnp.exp(scores - largest)
    row_sum = jnp.sum(raised, axis=-1, keepdims=True)
    soft_probs = (raised / row_sum).astype(jnp.bfloat16)
    mixed_out = jnp.einsum(
        "rhqk,rkhe->rqhe", soft_probs, head_v, preferred_element_type=jnp.float32
    )
    return (
        mixed_out.reshape(batch_rows, slot_count, heavy_width),
        (largest + jnp.log(row_sum))[..., 0],
    )


def heavy_backward(heavy_q, heavy_kv_all, allowed, log_sum, grad_mixed):
    batch_rows, slot_count, heavy_width = heavy_q.shape
    head_scale = H_HEAD ** (-0.5)
    scores = heavy_scores(heavy_q, heavy_kv_all, allowed)
    soft_probs = jnp.where(allowed[:, None], jnp.exp(scores - log_sum[..., None]), 0.0)
    head_q = heavy_q.reshape(batch_rows, slot_count, H_HEADS, H_HEAD)
    head_k = heavy_kv_all[..., :heavy_width].reshape(batch_rows, -1, H_HEADS, H_HEAD)
    head_v = heavy_kv_all[..., heavy_width:].reshape(batch_rows, -1, H_HEADS, H_HEAD)
    head_g = grad_mixed.reshape(batch_rows, slot_count, H_HEADS, H_HEAD)
    grad_probs = jnp.einsum("rqhe,rkhe->rhqk", head_g, head_v, preferred_element_type=jnp.float32)
    inner_sum = jnp.sum(soft_probs * grad_probs, axis=-1, keepdims=True)
    grad_scores = (soft_probs * (grad_probs - inner_sum)).astype(jnp.bfloat16)
    grad_q = (
        jnp.einsum("rhqk,rkhe->rqhe", grad_scores, head_k, preferred_element_type=jnp.float32)
        * head_scale
    )
    grad_k = (
        jnp.einsum("rhqk,rqhe->rkhe", grad_scores, head_q, preferred_element_type=jnp.float32)
        * head_scale
    )
    grad_v = jnp.einsum(
        "rhqk,rqhe->rkhe",
        soft_probs.astype(jnp.bfloat16),
        head_g,
        preferred_element_type=jnp.float32,
    )
    key_count = heavy_kv_all.shape[1]
    grad_kv = jnp.concatenate(
        [
            grad_k.reshape(batch_rows, key_count, heavy_width),
            grad_v.reshape(batch_rows, key_count, heavy_width),
        ],
        axis=-1,
    )
    return (grad_q.reshape(batch_rows, slot_count, heavy_width), grad_kv)


def shards(
    layer_input,
    cotangent,
    segment_ids,
    route_index,
    route_count,
    attn_gain,
    light_qkv,
    light_out,
    heavy_qkv,
    heavy_out,
    attn_router,
    ffn_gain,
    light_gate_up,
    light_down,
    heavy_gate_up,
    heavy_down,
    ffn_router,
):
    batch_rows, stretch_len, model_width = layer_input.shape
    seq_groups = lax.axis_size("seq")
    stretch_pos = lax.axis_index("seq")
    routed_total = route_index.shape[2]
    slot_share = routed_total // seq_groups
    first_token = stretch_pos * stretch_len
    token_pos = first_token + jnp.arange(stretch_len, dtype=jnp.int32)
    attn_shards = (attn_gain, light_qkv, light_out, heavy_qkv, heavy_out, attn_router)
    ffn_shards = (ffn_gain, light_gate_up, light_down, heavy_gate_up, heavy_down, ffn_router)
    attn_full = (
        lax.all_gather(attn_shards[0], ("dp", "seq"), axis=0, tiled=True),
        lax.all_gather(attn_shards[1], ("dp", "seq"), axis=0, tiled=True),
        lax.all_gather(attn_shards[2], ("dp", "seq"), axis=0, tiled=True),
        lax.all_gather(attn_shards[3], ("dp", "seq"), axis=0, tiled=True),
        lax.all_gather(attn_shards[4], ("dp", "seq"), axis=0, tiled=True),
        lax.all_gather(attn_shards[5], ("dp", "seq"), axis=0, tiled=True),
    )
    ffn_full = (
        lax.all_gather(ffn_shards[0], ("dp", "seq"), axis=0, tiled=True),
        lax.all_gather(ffn_shards[1], ("dp", "seq"), axis=0, tiled=True),
        lax.all_gather(ffn_shards[2], ("dp", "seq"), axis=0, tiled=True),
        lax.all_gather(ffn_shards[3], ("dp", "seq"), axis=0, tiled=True),
        lax.all_gather(ffn_shards[4], ("dp", "seq"), axis=0, tiled=True),
        lax.all_gather(ffn_shards[5], ("dp", "seq"), axis=0, tiled=True),
    )
    seg_row = lax.all_gather(segment_ids, "seq", axis=1, tiled=True)
    input_wide = layer_input.astype(jnp.float32)
    gain_attn = attn_full[0].astype(jnp.float32)
    normed_attn = rms_norm(input_wide, gain_attn).astype(jnp.bfloat16)
    light_width = attn_full[2].shape[0]
    light_act = matmul(normed_attn, attn_full[1]).astype(jnp.bfloat16)
    queries = light_act[..., :light_width]
    extended = extended_2(light_act[..., light_width:], (("seq", 1),), WINDOW)
    seg_padded = jnp.pad(seg_row, ((0, 0), (WINDOW, WINDOW)), constant_values=-1)
    key_seg = lax.dynamic_slice_in_dim(seg_padded, first_token, stretch_len + 2 * WINDOW, 1)
    offsets = jnp.arange(stretch_len)[:, None] - (
        jnp.arange(stretch_len + 2 * WINDOW)[None, :] - WINDOW
    )
    in_reach = jnp.abs(offsets) <= WINDOW
    light_allowed = in_reach[None] & (segment_ids[:, :, None] == key_seg[:, None, :])
    light_mixed, light_lse = lax.map(light_forward_row, (queries, extended, light_allowed))
    light_branch = matmul(light_mixed, attn_full[2])
    heavy_width = attn_full[4].shape[0]
    table_q = route_table(route_index, route_count, 0, token_pos)
    table_kv = route_table(route_index, route_count, 1, token_pos)
    q_rows, kv_rows = routed_rows((table_q, table_kv), (normed_attn, normed_attn))
    heavy_q = matmul(q_rows, attn_full[3][:, :heavy_width]).astype(jnp.bfloat16)
    heavy_kv_own = matmul(kv_rows, attn_full[3][:, heavy_width:]).astype(jnp.bfloat16)
    heavy_kv_all = lax.all_gather(heavy_kv_own, "seq", axis=1, tiled=True)
    own_slots = lax.dynamic_slice_in_dim(
        route_index[:, 0, :], stretch_pos * slot_share, slot_share, 1
    )
    q_seg = jnp.take_along_axis(seg_row, own_slots, axis=1)
    kv_seg = jnp.take_along_axis(seg_row, route_index[:, 1, :], axis=1)
    kv_live = jnp.arange(routed_total)[None, :] < route_count[:, 1][:, None]
    heavy_allowed = (q_seg[:, :, None] == kv_seg[:, None, :]) & kv_live[:, None, :]
    heavy_mixed, heavy_lse = heavy_forward(heavy_q, heavy_kv_all, heavy_allowed)
    attn_score = jnp.einsum("rjd,d->rj", q_rows, attn_full[5], preferred_element_type=jnp.float32)
    gated_mixed = gate_mix(attn_score, heavy_mixed).astype(jnp.bfloat16)
    heavy_rows = matmul(gated_mixed, attn_full[4]).astype(jnp.bfloat16)
    heavy_branch = home_rows((table_q,), (heavy_rows,))
    midway = input_wide + light_branch + heavy_branch
    gain_ffn = ffn_full[0].astype(jnp.float32)
    normed_ffn = rms_norm(midway, gain_ffn).astype(jnp.bfloat16)
    light_hidden_width = ffn_full[2].shape[0]
    light_pre = matmul(normed_ffn, ffn_full[1])
    light_gate = light_pre[..., :light_hidden_width]
    light_up = light_pre[..., light_hidden_width:]
    light_hidden = plain_unit(light_gate, light_up).astype(jnp.bfloat16)
    light_ffn = matmul(light_hidden, ffn_full[2])
    heavy_hidden_width = ffn_full[4].shape[0]
    table_f = route_table(route_index, route_count, 2, token_pos)
    (ffn_rows,) = routed_rows((table_f,), (normed_ffn,))
    heavy_pre = matmul(ffn_rows, ffn_full[3])
    heavy_gate = heavy_pre[..., :heavy_hidden_width]
    heavy_up = heavy_pre[..., heavy_hidden_width:]
    ffn_score = jnp.einsum("rjd,d->rj", ffn_rows, ffn_full[5], preferred_element_type=jnp.float32)
    heavy_hidden = gated_unit(heavy_gate, heavy_up, ffn_score).astype(jnp.bfloat16)
    heavy_ffn_rows = matmul(heavy_hidden, ffn_full[4]).astype(jnp.bfloat16)
    heavy_ffn = home_rows((table_f,), (heavy_ffn_rows,))
    layer_output = (midway + light_ffn + heavy_ffn).astype(jnp.bfloat16)
    ffn_back = (
        lax.all_gather(ffn_shards[0], ("dp", "seq"), axis=0, tiled=True),
        lax.all_gather(ffn_shards[1], ("dp", "seq"), axis=0, tiled=True),
        lax.all_gather(ffn_shards[2], ("dp", "seq"), axis=0, tiled=True),
        lax.all_gather(ffn_shards[3], ("dp", "seq"), axis=0, tiled=True),
        lax.all_gather(ffn_shards[4], ("dp", "seq"), axis=0, tiled=True),
        lax.all_gather(ffn_shards[5], ("dp", "seq"), axis=0, tiled=True),
    )
    grad_top = cotangent.astype(jnp.float32)
    grad_light_down = outer_sum(light_hidden, cotangent)
    light_hidden_grad = matmul_back(cotangent, ffn_back[2]).astype(jnp.bfloat16)
    unused_light, light_pull = jax.vjp(plain_unit, light_gate, light_up)
    light_gate_grad, light_up_grad = light_pull(light_hidden_grad.astype(jnp.float32))
    light_pre_grad = jnp.concatenate([light_gate_grad, light_up_grad], axis=-1).astype(jnp.bfloat16)
    grad_light_gate_up = outer_sum(normed_ffn, light_pre_grad)
    normed_ffn_grad = matmul_back(light_pre_grad, ffn_back[1])
    (heavy_ffn_cot,) = routed_rows((table_f,), (cotangent,))
    grad_heavy_down = outer_sum(heavy_hidden, heavy_ffn_cot)
    heavy_hidden_grad = matmul_back(heavy_ffn_cot, ffn_back[4]).astype(jnp.bfloat16)
    unused_heavy, heavy_pull = jax.vjp(gated_unit, heavy_gate, heavy_up, ffn_score)
    heavy_gate_grad, heavy_up_grad, ffn_score_grad = heavy_pull(
        heavy_hidden_grad.astype(jnp.float32)
    )
    heavy_pre_grad = jnp.concatenate([heavy_gate_grad, heavy_up_grad], axis=-1).astype(jnp.bfloat16)
    grad_heavy_gate_up = outer_sum(ffn_rows, heavy_pre_grad)
    grad_ffn_router = jnp.einsum(
        "rjd,rj->d", ffn_rows.astype(jnp.float32), ffn_score_grad, precision=lax.Precision.HIGHEST
    )
    ffn_rows_grad = (
        matmul_back(heavy_pre_grad, ffn_back[3])
        + ffn_score_grad[..., None] * ffn_back[5].astype(jnp.float32)
    ).astype(jnp.bfloat16)
    normed_ffn_grad = normed_ffn_grad + home_rows((table_f,), (ffn_rows_grad,))
    unused_norm, ffn_norm_pull = jax.vjp(rms_norm, midway, gain_ffn)
    midway_norm_grad, grad_ffn_gain = ffn_norm_pull(normed_ffn_grad)
    midway_grad = grad_top + midway_norm_grad
    ffn_grads = (
        lax.psum_scatter(grad_ffn_gain, ("dp", "seq"), scatter_dimension=0, tiled=True),
        lax.psum_scatter(grad_light_gate_up, ("dp", "seq"), scatter_dimension=0, tiled=True),
        lax.psum_scatter(grad_light_down, ("dp", "seq"), scatter_dimension=0, tiled=True),
        lax.psum_scatter(grad_heavy_gate_up, ("dp", "seq"), scatter_dimension=0, tiled=True),
        lax.psum_scatter(grad_heavy_down, ("dp", "seq"), scatter_dimension=0, tiled=True),
        lax.psum_scatter(grad_ffn_router, ("dp", "seq"), scatter_dimension=0, tiled=True),
    )
    attn_back = (
        lax.all_gather(attn_shards[0], ("dp", "seq"), axis=0, tiled=True),
        lax.all_gather(attn_shards[1], ("dp", "seq"), axis=0, tiled=True),
        lax.all_gather(attn_shards[2], ("dp", "seq"), axis=0, tiled=True),
        lax.all_gather(attn_shards[3], ("dp", "seq"), axis=0, tiled=True),
        lax.all_gather(attn_shards[4], ("dp", "seq"), axis=0, tiled=True),
        lax.all_gather(attn_shards[5], ("dp", "seq"), axis=0, tiled=True),
    )
    attn_out_grad = midway_grad.astype(jnp.bfloat16)
    grad_light_out = outer_sum(light_mixed, attn_out_grad)
    light_mixed_grad = matmul_back(attn_out_grad, attn_back[2]).astype(jnp.bfloat16)
    again_act = matmul(normed_attn, attn_back[1]).astype(jnp.bfloat16)
    again_queries = again_act[..., :light_width]
    again_extended = extended_2(again_act[..., light_width:], (("seq", 1),), WINDOW)
    light_q_grad, light_ext_grad = lax.map(
        light_backward_row,
        (again_queries, again_extended, light_allowed, light_lse, light_mixed_grad),
    )
    rim_pair = jnp.concatenate(
        [light_ext_grad[:, :WINDOW], light_ext_grad[:, stretch_len + WINDOW :]], axis=1
    )
    rim_back = extended_2(rim_pair.astype(jnp.bfloat16), (("seq", 1),), WINDOW).astype(
        rim_pair.dtype
    )
    light_kv_grad = light_ext_grad[:, WINDOW : WINDOW + stretch_len]
    light_kv_grad = light_kv_grad.at[:, :WINDOW].add(rim_back[:, :WINDOW])
    light_kv_grad = light_kv_grad.at[:, stretch_len - WINDOW :].add(rim_back[:, 3 * WINDOW :])
    light_act_grad = jnp.concatenate([light_q_grad, light_kv_grad], axis=-1).astype(jnp.bfloat16)
    grad_light_qkv = outer_sum(normed_attn, light_act_grad)
    normed_attn_grad = matmul_back(light_act_grad, attn_back[1])
    (heavy_out_cot,) = routed_rows((table_q,), (attn_out_grad,))
    grad_heavy_out = outer_sum(gated_mixed, heavy_out_cot)
    gated_grad = matmul_back(heavy_out_cot, attn_back[4]).astype(jnp.bfloat16)
    unused_gate, gate_pull = jax.vjp(gate_mix, attn_score, heavy_mixed)
    attn_score_grad, heavy_mixed_grad = gate_pull(gated_grad.astype(jnp.float32))
    heavy_q_grad, heavy_kv_all_grad = heavy_backward(
        heavy_q, heavy_kv_all, heavy_allowed, heavy_lse, heavy_mixed_grad.astype(jnp.bfloat16)
    )
    heavy_kv_grad = lax.psum_scatter(
        heavy_kv_all_grad.astype(jnp.bfloat16), "seq", scatter_dimension=1, tiled=True
    )
    heavy_q_grad = heavy_q_grad.astype(jnp.bfloat16)
    grad_heavy_qkv = jnp.concatenate(
        [outer_sum(q_rows, heavy_q_grad), outer_sum(kv_rows, heavy_kv_grad)], axis=1
    )
    grad_attn_router = jnp.einsum(
        "rjd,rj->d", q_rows.astype(jnp.float32), attn_score_grad, precision=lax.Precision.HIGHEST
    )
    q_rows_grad = (
        matmul_back(heavy_q_grad, attn_back[3][:, :heavy_width])
        + attn_score_grad[..., None] * attn_back[5].astype(jnp.float32)
    ).astype(jnp.bfloat16)
    kv_rows_grad = matmul_back(heavy_kv_grad, attn_back[3][:, heavy_width:]).astype(jnp.bfloat16)
    normed_attn_grad = normed_attn_grad + home_rows(
        (table_q, table_kv), (q_rows_grad, kv_rows_grad)
    )
    unused_first, attn_norm_pull = jax.vjp(rms_norm, input_wide, gain_attn)
    input_norm_grad, grad_attn_gain = attn_norm_pull(normed_attn_grad)
    input_grad = (midway_grad + input_norm_grad).astype(jnp.bfloat16)
    attn_grads = (
        lax.psum_scatter(grad_attn_gain, ("dp", "seq"), scatter_dimension=0, tiled=True),
        lax.psum_scatter(grad_light_qkv, ("dp", "seq"), scatter_dimension=0, tiled=True),
        lax.psum_scatter(grad_light_out, ("dp", "seq"), scatter_dimension=0, tiled=True),
        lax.psum_scatter(grad_heavy_qkv, ("dp", "seq"), scatter_dimension=0, tiled=True),
        lax.psum_scatter(grad_heavy_out, ("dp", "seq"), scatter_dimension=0, tiled=True),
        lax.psum_scatter(grad_attn_router, ("dp", "seq"), scatter_dimension=0, tiled=True),
    )
    return (
        layer_output,
        input_grad,
        attn_grads[0],
        attn_grads[1],
        attn_grads[2],
        attn_grads[3],
        attn_grads[4],
        attn_grads[5],
        ffn_grads[0],
        ffn_grads[1],
        ffn_grads[2],
        ffn_grads[3],
        ffn_grads[4],
        ffn_grads[5],
    )


def solution(mesh):
    return jax.shard_map(
        shards,
        mesh=mesh,
        in_specs=(
            P("dp", "seq", None),
            P("dp", "seq", None),
            P("dp", "seq"),
            P("dp", None, None),
            P("dp", None),
            P(("dp", "seq")),
            P(("dp", "seq"), None),
            P(("dp", "seq"), None),
            P(("dp", "seq"), None),
            P(("dp", "seq"), None),
            P(("dp", "seq")),
            P(("dp", "seq")),
            P(("dp", "seq"), None),
            P(("dp", "seq"), None),
            P(("dp", "seq"), None),
            P(("dp", "seq"), None),
            P(("dp", "seq")),
        ),
        out_specs=(
            P("dp", "seq", None),
            P("dp", "seq", None),
            P(("dp", "seq")),
            P(("dp", "seq"), None),
            P(("dp", "seq"), None),
            P(("dp", "seq"), None),
            P(("dp", "seq"), None),
            P(("dp", "seq")),
            P(("dp", "seq")),
            P(("dp", "seq"), None),
            P(("dp", "seq"), None),
            P(("dp", "seq"), None),
            P(("dp", "seq"), None),
            P(("dp", "seq")),
        ),
        check_vma=False,
    )
```

profile of v0, /device:TPU:0, one launch (start us, length us, event | category | flops | bytes accessed | tf_op | source)
XLA Modules:
  0.0 1801.7 jit_solution(10396561440176845615)
XLA Ops:
  15.6 42.1 %all-reduce.10 = (bf16[768]{0:T(1024)(128)(2,1)S(1)}, bf16[768]{0:T(1024)(128)(2,1)S(1)}, bf16[768]{0:T(1024)(128)(2,1)S(1)}, bf16[768]{0:T(1024)(128)(2,1)}) all-reduce(bf16[768]{0:T(1024)(128)(2,1)S(1)} %dynamic-update-slice.9, bf16[768]{0:T(1024)(128)(2,1)S(1)} %dynamic-update-slice.10, ...), channel_id=1, replica_groups=mesh['dp'=8,'seq'=4] {'dp','seq'}, use_global_device_ids=true, to_apply=%add.1 | all-reduce | flops 3072 | bytes 12288
  96.9 42.7 %all-gather.15.cloned.1.call-done = bf16[768,2304]{1,0:T(8,128)(2,1)} async-done(((bf16[24,2304]{1,0:T(8,128)(2,1)}), bf16[768,2304]{1,0:T(8,128)(2,1)}) %all-gather.15.cloned.1.call-update) | async-done | bytes 3538960 | tf_op jit(solution)/shard_map/all_gather | solution.py:267
  145.4 56.0 %all-gather.19.cloned.1.call-done = bf16[768,2304]{1,0:T(8,128)(2,1)} async-done(((bf16[24,2304]{1,0:T(8,128)(2,1)}), bf16[768,2304]{1,0:T(8,128)(2,1)}) %all-gather.19.cloned.1.call-update) | async-done | bytes 3538960 | tf_op jit(solution)/shard_map/all_gather | solution.py:269
  205.5 18.6 %all-gather = bf16[256,1536]{1,0:T(8,128)(2,1)S(1)} all-gather(bf16[64,1536]{1,0:T(8,128)(2,1)S(1)} %convolution_convert_fusion.2), channel_id=2, replica_groups=mesh['dp'=8,'seq'=4] {'seq'}, dimensions={0}, use_global_device_ids=true | all-gather | bytes 983040 | tf_op jit(solution)/shard_map/all_gather | solution.py:304
  231.8 26.1 %all-gather.21.cloned.1.call-done = bf16[768,768]{1,0:T(8,128)(2,1)} async-done(((bf16[24,768]{1,0:T(8,128)(2,1)}), bf16[768,768]{1,0:T(8,128)(2,1)}) %all-gather.21.cloned.1.call-update) | async-done | bytes 1179664 | tf_op jit(solution)/shard_map/all_gather | solution.py:270
  259.7 16.0 all-gather.1
  295.6 18.4 %all-gather.17.cloned.1.call-done = bf16[768,768]{1,0:T(8,128)(2,1)} async-done(((bf16[24,768]{1,0:T(8,128)(2,1)}), bf16[768,768]{1,0:T(8,128)(2,1)}) %all-gather.17.cloned.1.call-update) | async-done | bytes 1179664 | tf_op jit(solution)/shard_map/all_gather | solution.py:268
  325.1 53.0 %all-gather.23.cloned.1.call-done = bf16[768,2048]{1,0:T(8,128)(2,1)} async-done(((bf16[24,2048]{1,0:T(8,128)(2,1)}), bf16[768,2048]{1,0:T(8,128)(2,1)}) %all-gather.23.cloned.1.call-update) | async-done | bytes 3145744 | tf_op jit(solution)/shard_map/all_gather | solution.py:275
  383.9 50.9 %all-gather.25.cloned.1.call-done = bf16[1024,768]{1,0:T(8,128)(2,1)} async-done(((bf16[32,768]{1,0:T(8,128)(2,1)}), bf16[1024,768]{1,0:T(8,128)(2,1)}) %all-gather.25.cloned.1.call-update) | async-done | bytes 1572880 | tf_op jit(solution)/shard_map/all_gather | solution.py:276
  446.0 86.4 %all-gather.27.cloned.1.call-done = bf16[768,8192]{1,0:T(8,128)(2,1)} async-done(((bf16[24,8192]{1,0:T(8,128)(2,1)}), bf16[768,8192]{1,0:T(8,128)(2,1)}) %all-gather.27.cloned.1.call-update) | async-done | bytes 12582928 | tf_op jit(solution)/shard_map/all_gather | solution.py:277
  540.7 62.7 %all-gather.29.cloned.1.call-done = bf16[4096,768]{1,0:T(8,128)(2,1)} async-done(((bf16[128,768]{1,0:T(8,128)(2,1)}), bf16[4096,768]{1,0:T(8,128)(2,1)}) %all-gather.29.cloned.1.call-update) | async-done | bytes 6291472 | tf_op jit(solution)/shard_map/all_gather | solution.py:278
  614.6 14.9 all-gather.3
  635.7 17.9 reduce-scatter.25.cloned.1.call-done
  795.6 14.6 all-gather.2
  814.8 15.2 all-gather.4
  831.5 14.2 all-gather.5
  847.8 40.6 %all-reduce.9 = (f32[768]{0:T(1024)S(1)}, f32[768]{0:T(1024)S(1)}, f32[768]{0:T(1024)S(1)}, f32[768]{0:T(1024)S(1)}) all-reduce(f32[768]{0:T(1024)S(1)} %get-tuple-element.82, f32[768]{0:T(1024)S(1)} %convolution_reduce_fusion.1, f32[768]{0:T(1024)S(1)} %copy-done.74, ...), channel_id=14, replica_groups=mesh['dp'=8,'seq'=4] {'dp','seq'}, use_global_device_ids=true, to_apply=%region_19.20.clone | all-reduce | flops 3072 | bytes 24576
  893.5 28.3 %reduce-scatter.35.cloned.1.call-done = f32[24,2048]{1,0:T(8,128)} async-done(((f32[768,2048]{1,0:T(8,128)}), f32[24,2048]{1,0:T(8,128)}) %reduce-scatter.35.cloned.1.call-update) | async-done | bytes 196624 | tf_op jit(solution)/shard_map/reduce_scatter | solution.py:375
  921.8 104.2 %reduce-scatter.29.cloned.1.call-done = f32[24,768]{1,0:T(8,128)} async-done(((f32[768,768]{1,0:T(8,128)}), f32[24,768]{1,0:T(8,128)}) %reduce-scatter.29.cloned.1.call-update) | async-done | bytes 73744 | tf_op jit(solution)/shard_map/reduce_scatter | solution.py:443
  1026.0 104.7 %reduce-scatter.33.cloned.1.call-done = f32[24,768]{1,0:T(8,128)} async-done(((f32[768,768]{1,0:T(8,128)}), f32[24,768]{1,0:T(8,128)}) %reduce-scatter.33.cloned.1.call-update) | async-done | bytes 73744 | tf_op jit(solution)/shard_map/reduce_scatter | solution.py:445
  1130.7 124.4 %reduce-scatter.27.cloned.1.call-done = f32[24,2304]{1,0:T(8,128)} async-done(((f32[768,2304]{1,0:T(8,128)}), f32[24,2304]{1,0:T(8,128)}) %reduce-scatter.27.cloned.1.call-update) | async-done | bytes 221200 | tf_op jit(solution)/shard_map/reduce_scatter | solution.py:442
  1255.1 125.5 %reduce-scatter.31.cloned.1.call-done = f32[24,2304]{1,0:T(8,128)} async-done(((f32[768,2304]{1,0:T(8,128)}), f32[24,2304]{1,0:T(8,128)}) %reduce-scatter.31.cloned.1.call-update) | async-done | bytes 221200 | tf_op jit(solution)/shard_map/reduce_scatter | solution.py:444
  1380.6 161.3 %reduce-scatter.41.cloned.1.call-done = f32[128,768]{1,0:T(8,128)} async-done(((f32[4096,768]{1,0:T(8,128)}), f32[128,768]{1,0:T(8,128)}) %reduce-scatter.41.cloned.1.call-update) | async-done | bytes 393232 | tf_op jit(solution)/shard_map/reduce_scatter | solution.py:378
  1541.9 252.5 %reduce-scatter.39.cloned.1.call-done = f32[24,8192]{1,0:T(8,128)} async-done(((f32[768,8192]{1,0:T(8,128)}), f32[24,8192]{1,0:T(8,128)}) %reduce-scatter.39.cloned.1.call-update) | async-done | bytes 786448 | tf_op jit(solution)/shard_map/reduce_scatter | solution.py:377
  (409 shorter events, 293.2 us)
Async XLA Ops:
  8.0 87.3 %reduce-scatter.17.cloned.1.call-start = ((), (), s32[]{:S(2)}) async-start(), calls=%async_computation.16 | async-start | bytes 491520 | tf_op jit(solution)/shard_map/reduce_scatter | solution.py:95
  75.3 64.3 %all-gather.15.cloned.1.call-start = ((), (), s32[]{:S(2)}) async-start(), calls=%async_computation.14 | async-start | bytes 3649536 | tf_op jit(solution)/shard_map/all_gather | solution.py:267
  75.9 125.6 %all-gather.19.cloned.1.call-start = ((), (), s32[]{:S(2)}) async-start(), calls=%async_computation.18 | async-start | bytes 3649536 | tf_op jit(solution)/shard_map/all_gather | solution.py:269
  76.4 126.8 %reduce-scatter.19.cloned.1.call-start = ((), (), s32[]{:S(2)}) async-start(), calls=%async_computation.17 | async-start | bytes 491520 | tf_op jit(solution)/shard_map/reduce_scatter | solution.py:95
  78.5 179.5 %all-gather.21.cloned.1.call-start = ((), (), s32[]{:S(2)}) async-start(), calls=%async_computation.19 | async-start | bytes 1216512 | tf_op jit(solution)/shard_map/all_gather | solution.py:270
  79.1 234.9 %all-gather.17.cloned.1.call-start = ((), (), s32[]{:S(2)}) async-start(), calls=%async_computation.15 | async-start | bytes 1216512 | tf_op jit(solution)/shard_map/all_gather | solution.py:268
  79.8 298.3 %all-gather.23.cloned.1.call-start = ((), (), s32[]{:S(2)}) async-start(), calls=%async_computation.20 | async-start | bytes 3244032 | tf_op jit(solution)/shard_map/all_gather | solution.py:275
  80.6 354.2 %all-gather.25.cloned.1.call-start = ((), (), s32[]{:S(2)}) async-start(), calls=%async_computation.21 | async-start | bytes 1622016 | tf_op jit(solution)/shard_map/all_gather | solution.py:276
  81.3 363.7 %reduce-scatter.21.cloned.1.call-start = ((), (), s32[]{:S(2)}) async-start(), calls=%async_computation.22 | async-start | bytes 491520 | tf_op jit(solution)/shard_map/reduce_scatter | solution.py:95
  227.8 48.0 %collective-permute-start = (bf16[1,128,1536]{2,1,0:T(8,128)(2,1)}, bf16[1,128,1536]{2,1,0:T(8,128)(2,1)}, u32[]{:S(2)}, u32[]{:S(2)}) collective-permute-start(bf16[1,128,1536]{2,1,0:T(8,128)(2,1)} %get-tuple-element.102), channel_id=1, source_target_pairs={{0,1},{1,2},{2,3},{4,5},{5,6},{6,7},{8,9},{9,10},{10,11},{12,13},{... | collective-permute-start | bytes 1179656 | tf_op jit(solution)/shard_map/ppermute | solution.py:30
  230.5 45.2 %collective-permute-start.1 = (bf16[1,128,1536]{2,1,0:T(8,128)(2,1)}, bf16[1,128,1536]{2,1,0:T(8,128)(2,1)}, u32[]{:S(2)}, u32[]{:S(2)}) collective-permute-start(bf16[1,128,1536]{2,1,0:T(8,128)(2,1)} %get-tuple-element.103), channel_id=1, source_target_pairs={{1,0},{2,1},{3,2},{5,4},{6,5},{7,6},{9,8},{10,9},{11,10},{13,12},{... | collective-permute-start | bytes 1179656 | tf_op jit(solution)/shard_map/ppermute | solution.py:32
  319.2 213.2 %all-gather.27.cloned.1.call-start = ((), (), s32[]{:S(2)}) async-start(), calls=%async_computation.23 | async-start | bytes 12976128 | tf_op jit(solution)/shard_map/all_gather | solution.py:277
  319.8 220.9 %reduce-scatter.23.cloned.1.call-start = ((), (), s32[]{:S(2)}) async-start(), calls=%async_computation.25 | async-start | bytes 491520 | tf_op jit(solution)/shard_map/reduce_scatter | solution.py:95
  321.8 281.6 %all-gather.29.cloned.1.call-start = ((), (), s32[]{:S(2)}) async-start(), calls=%async_computation.24 | async-start | bytes 6488064 | tf_op jit(solution)/shard_map/all_gather | solution.py:278
  322.3 331.3 %reduce-scatter.25.cloned.1.call-start = ((), (), s32[]{:S(2)}) async-start(), calls=%async_computation.26 | async-start | bytes 491520 | tf_op jit(solution)/shard_map/reduce_scatter | solution.py:95
  634.3 124.2 %reduce-scatter.43.cloned.1.call-start = ((), (), s32[]{:S(2)}) async-start(), calls=%async_computation.35 | async-start | bytes 983040
  671.3 222.2 %reduce-scatter.37.cloned.1.call-start = ((), (), s32[]{:S(2)}) async-start(), calls=%async_computation.32 | async-start | bytes 3244032 | tf_op jit(solution)/shard_map/reduce_scatter | solution.py:376
  675.6 246.3 %reduce-scatter.35.cloned.1.call-start = ((), (), s32[]{:S(2)}) async-start(), calls=%async_computation.31 | async-start | bytes 6488064 | tf_op jit(solution)/shard_map/reduce_scatter | solution.py:375
  681.9 344.1 %reduce-scatter.29.cloned.1.call-start = ((), (), s32[]{:S(2)}) async-start(), calls=%async_computation.28 | async-start | bytes 2433024 | tf_op jit(solution)/shard_map/reduce_scatter | solution.py:443
  692.5 438.1 %reduce-scatter.33.cloned.1.call-start = ((), (), s32[]{:S(2)}) async-start(), calls=%async_computation.30 | async-start | bytes 2433024 | tf_op jit(solution)/shard_map/reduce_scatter | solution.py:445
  725.3 529.7 %reduce-scatter.27.cloned.1.call-start = ((), (), s32[]{:S(2)}) async-start(), calls=%async_computation.27 | async-start | bytes 7299072 | tf_op jit(solution)/shard_map/reduce_scatter | solution.py:442
  752.8 627.8 %reduce-scatter.31.cloned.1.call-start = ((), (), s32[]{:S(2)}) async-start(), calls=%async_computation.29 | async-start | bytes 7299072 | tf_op jit(solution)/shard_map/reduce_scatter | solution.py:444
  766.9 775.0 %reduce-scatter.41.cloned.1.call-start = ((), (), s32[]{:S(2)}) async-start(), calls=%async_computation.34 | async-start | bytes 12976128 | tf_op jit(solution)/shard_map/reduce_scatter | solution.py:378
  774.4 1020.0 %reduce-scatter.39.cloned.1.call-start = ((), (), s32[]{:S(2)}) async-start(), calls=%async_computation.33 | async-start | bytes 25952256 | tf_op jit(solution)/shard_map/reduce_scatter | solution.py:377
  (111 other events, 1448.8 us)
Sparse Core Ops, SparseCore 0:
  75.4 19.8 reduce-scatter.16
  98.3 19.3 reduce-scatter.18
  319.3 19.4 reduce-scatter.20
  341.1 19.4 reduce-scatter.22
  634.5 19.1 reduce-scatter.24
  671.4 21.5 reduce-scatter.42
  700.0 100.9 reduce-scatter.36
  808.1 113.6 reduce-scatter.34
  927.7 98.2 reduce-scatter.28
  1032.5 98.0 reduce-scatter.32
  1136.9 118.0 reduce-scatter.26
  1262.1 118.4 reduce-scatter.30
  1387.2 154.6 reduce-scatter.40
  1549.9 244.4 reduce-scatter.38
Sparse Core Ops, SparseCore 1:
  78.6 61.0 all-gather.14
  142.3 59.1 all-gather.18
  204.1 53.8 all-gather.20
  260.8 53.1 all-gather.16
  316.9 61.2 all-gather.22
  381.1 53.7 all-gather.24
  437.9 94.4 all-gather.26
  535.6 67.7 all-gather.28
where the time goes:
time: 1810 us; the launch traced here: 1800 us
  waiting for transfers between devices  1340 us (74%)
  blocking collectives  188 us (10%)
  matrix products  167 us (9%)
  local copies, waits for them, and re-layouts  48 us (3%)
  other arithmetic  34.1 us (2%)
    reduce_scatter x1, waiting for transfers between devices, shards(): lax.psum_scatter(grad_heavy_gate_up, ('dp', 'seq'), scatter_dimension=0,...  253 us
    reduce_scatter x1, waiting for transfers between devices, shards(): lax.psum_scatter(grad_heavy_down, ('dp', 'seq'), scatter_dimension=0, til...  161 us
    reduce_scatter x1, waiting for transfers between devices, shards(): lax.psum_scatter(grad_heavy_qkv, ('dp', 'seq'), scatter_dimension=0, tile...  126 us
    reduce_scatter x1, waiting for transfers between devices, shards(): lax.psum_scatter(grad_light_qkv, ('dp', 'seq'), scatter_dimension=0, tile...  124 us
    reduce_scatter x1, waiting for transfers between devices, shards(): lax.psum_scatter(grad_heavy_out, ('dp', 'seq'), scatter_dimension=0, tile...  105 us
    reduce_scatter x1, waiting for transfers between devices, shards(): lax.psum_scatter(grad_light_out, ('dp', 'seq'), scatter_dimension=0, tile...  104 us
    all_gather x1, waiting for transfers between devices, shards(): lax.all_gather(ffn_shards[3], ('dp', 'seq'), axis=0, tiled=True)  86.4 us
    unnamed x2, blocking collectives  82.7 us
  transfers between devices with their start and end apart: 26, of which 19 were waited for; matrix products, arithmetic and copies ran while one was open for 11% of the time, Pallas kernels for 0%

commit v1 on v0

v1 whole, which is shorter than its diff:
```python
import jax
import jax.numpy as jnp
from jax import lax
from jax.experimental import pallas as pl
from jax.experimental.pallas import tpu as pltpu
from jax.sharding import PartitionSpec as P

L_HEADS = 8
L_HEAD = 96
H_HEADS = 12
H_HEAD = 64
WINDOW = 128
LANES = 128

epsilon = 1e-06
masked_score = -1e30
gelu_scale = 0.7978845608028654
bf16 = jnp.bfloat16
f32 = jnp.float32


def dma_moves(index, arrays, out_shapes, moves):
    def body(index_ref, *refs):
        ins, outs, sems = refs[: len(arrays)], refs[len(arrays) : -1], refs[-1]
        copies = [
            pltpu.make_async_copy(source(ins, index_ref), target(outs, index_ref), sems.at[k])
            for k, (source, target) in enumerate(moves)
        ]
        for copy in copies:
            copy.start()
        for copy in copies:
            copy.wait()

    return pl.pallas_call(
        body,
        out_shape=[jax.ShapeDtypeStruct(s, a) for s, a in out_shapes],
        in_specs=[pl.BlockSpec(memory_space=pltpu.SMEM)]
        + [pl.BlockSpec(memory_space=pl.ANY)] * len(arrays),
        out_specs=[pl.BlockSpec(memory_space=pltpu.VMEM)] * len(out_shapes),
        scratch_shapes=[pltpu.SemaphoreType.DMA((len(moves),))],
        compiler_params=pltpu.CompilerParams(vmem_limit_bytes=16 * 2**20),
    )(index, *arrays)


def dp_stages(count):
    if count == 8:
        return [
            lambda i: i ^ (2 + 2 * (i & 1)),
            lambda i: i ^ (4 - 2 * (i & 1)),
            lambda i: i ^ 1,
        ]
    masks = [1 << b for b in range(count.bit_length() - 1)][::-1]
    return [lambda i, m=m: i ^ m for m in masks]


def dp_sources(count):
    sources = [lambda i: i]
    for stage in dp_stages(count):
        sources = sources + [lambda i, f=f, stage=stage: f(stage(i)) for f in sources]
    return sources


def perm(count, stage):
    return [(i, stage(i)) for i in range(count)]


def seq_pieces(shard, count):
    return [shard] + [
        lax.ppermute(shard, "seq", [(i, i ^ k) for i in range(count)]) for k in range(1, count)
    ]


def gather_seq(shard):
    count, pos = lax.axis_size("seq"), lax.axis_index("seq")
    return place_seq(seq_pieces(shard, count), pos)


def place_seq(pieces, pos):
    count = len(pieces)
    order = jnp.stack([pos ^ k for k in range(count)]).astype(jnp.int32)
    moves = [
        (lambda ins, idx, k=k: ins[k], lambda outs, idx, k=k: outs[0].at[idx[k]])
        for k in range(count)
    ]
    shape = (count,) + pieces[0].shape
    return dma_moves(order, pieces, [(shape, pieces[0].dtype)], moves)[0]


def gather_dp(block, parts):
    count, me = lax.axis_size("dp"), lax.axis_index("dp")
    pieces = [block]
    for stage in dp_stages(count):
        pairs = perm(count, stage)
        pieces = pieces + [lax.ppermute(p, "dp", pairs) for p in pieces]
    order = jnp.stack([f(me) for f in dp_sources(count)]).astype(jnp.int32)
    moves, shapes = [], []
    for j, (shape, view) in enumerate(parts):
        shapes.append(((count,) + shape, block.dtype))
        for k in range(count):
            moves.append(
                (
                    lambda ins, idx, k=k, view=view: view(ins[k]),
                    lambda outs, idx, k=k, j=j: outs[j].at[idx[k]],
                )
            )
    return dma_moves(order, pieces, shapes, moves)


def scatter_dp(blocks):
    count, me = lax.axis_size("dp"), lax.axis_index("dp")
    order = jnp.stack([f(me) for f in dp_sources(count)]).astype(jnp.int32)
    half = count // 2
    shape = (half,) + blocks.shape[1:]
    moves = [
        (
            lambda ins, idx, k=k: ins[0].at[idx[k]],
            lambda outs, idx, k=k: outs[k // half].at[k % half],
        )
        for k in range(count)
    ]
    keep, send = dma_moves(order, [blocks], [(shape, bf16), (shape, bf16)], moves)
    for stage in dp_stages(count)[::-1]:
        got = lax.ppermute(send, "dp", perm(count, stage))
        total = keep.astype(f32) + got.astype(f32)
        half = half // 2
        if half:
            keep, send = total[:half].astype(bf16), total[half:].astype(bf16)
    return total[0]


def scatter_seq(blocks):
    count, pos = lax.axis_size("seq"), lax.axis_index("seq")
    sent = blocks.astype(bf16)
    total = lax.dynamic_index_in_dim(blocks, pos, 0, keepdims=False).astype(f32)
    for k in range(1, count):
        piece = lax.dynamic_index_in_dim(sent, pos ^ k, 0, keepdims=False)
        total = total + lax.ppermute(piece, "seq", [(i, i ^ k) for i in range(count)]).astype(f32)
    return total


def scatter_both(grad):
    dp, seq = lax.axis_size("dp"), lax.axis_size("seq")
    rows, columns = grad.shape
    blocks = grad.astype(bf16).reshape(dp, rows // dp, columns)
    mine = scatter_dp(blocks)
    return scatter_seq(mine.reshape(seq, rows // dp // seq, columns))


def sum_seq(part):
    count, mask = lax.axis_size("seq"), 1
    while mask < count:
        got = lax.ppermute(part, "seq", [(i, i ^ mask) for i in range(count)])
        part = (part.astype(f32) + got.astype(f32)).astype(bf16)
        mask *= 2
    return part


def after(value, *others):
    return lax.optimization_barrier((value,) + others)[0]


def inv_rms(values):
    return lax.rsqrt(jnp.mean(values * values, axis=-1, keepdims=True) + epsilon)


def norm_back(values, inv, scaled):
    inner = jnp.mean(scaled * values, axis=-1, keepdims=True)
    return inv * scaled - values * (inv * inv * inv) * inner


def gelu_both(v):
    inner = jnp.tanh(gelu_scale * (v + 0.044715 * v * v * v))
    value = 0.5 * v * (1.0 + inner)
    slope = 0.5 * (1.0 + inner) + 0.5 * v * (1.0 - inner * inner) * gelu_scale * (
        1.0 + 3.0 * 0.044715 * v * v
    )
    return value, slope


def sigmoid(values):
    return 1.0 / (1.0 + jnp.exp(-values))


def dot(a, b):
    return lax.dot_general(a, b, (((1,), (0,)), ((), ())), preferred_element_type=f32)


def dot_nt(a, b):
    return lax.dot_general(a, b, (((1,), (1,)), ((), ())), preferred_element_type=f32)


def dot_tn(a, b):
    return lax.dot_general(a, b, (((0,), (0,)), ((), ())), preferred_element_type=f32)


def route_table(slots, count, token_pos):
    live = jnp.arange(slots.shape[0]) < count
    return ((slots[:, None] == token_pos[None, :]) & live[:, None]).astype(bf16)


def heads(x, head):
    return x.reshape(x.shape[0], -1, head)


def attend(q, k, v, allowed, head):
    scores = jnp.einsum("qhe,khe->hqk", heads(q, head), heads(k, head), preferred_element_type=f32)
    scores = jnp.where(allowed[None], scores * head ** (-0.5), masked_score)
    largest = jnp.max(scores, axis=-1, keepdims=True)
    raised = jnp.exp(scores - largest)
    row_sum = jnp.sum(raised, axis=-1, keepdims=True)
    probs = (raised / row_sum).astype(bf16)
    mixed = jnp.einsum("hqk,khe->qhe", probs, heads(v, head), preferred_element_type=f32)
    return mixed.reshape(q.shape), largest + jnp.log(row_sum)


def attend_back(q, k, v, allowed, log_sum, grad, head):
    scale = head ** (-0.5)
    hq, hk, hv, hg = heads(q, head), heads(k, head), heads(v, head), heads(grad, head)
    scores = jnp.einsum("qhe,khe->hqk", hq, hk, preferred_element_type=f32) * scale
    probs = jnp.where(allowed[None], jnp.exp(scores - log_sum), 0.0)
    grad_probs = jnp.einsum("qhe,khe->hqk", hg, hv, preferred_element_type=f32)
    inner = jnp.sum(probs * grad_probs, axis=-1, keepdims=True)
    ds = (probs * (grad_probs - inner)).astype(bf16)
    grad_q = jnp.einsum("hqk,khe->qhe", ds, hk, preferred_element_type=f32) * scale
    grad_k = jnp.einsum("hqk,qhe->khe", ds, hq, preferred_element_type=f32) * scale
    grad_v = jnp.einsum("hqk,qhe->khe", probs.astype(bf16), hg, preferred_element_type=f32)
    grad_kv = jnp.concatenate([grad_k.reshape(k.shape), grad_v.reshape(k.shape)], axis=-1)
    return grad_q.reshape(q.shape).astype(bf16), grad_kv.astype(bf16)


def shards(
    layer_input,
    cotangent,
    segment_ids,
    route_index,
    route_count,
    attn_gain,
    light_qkv,
    light_out,
    heavy_qkv,
    heavy_out,
    attn_router,
    ffn_gain,
    light_gate_up,
    light_down,
    heavy_gate_up,
    heavy_down,
    ffn_router,
):
    dp, seq = lax.axis_size("dp"), lax.axis_size("seq")
    pos = lax.axis_index("seq")
    x_in, cot, seg = layer_input[0], cotangent[0], segment_ids[0]
    tokens, width = x_in.shape
    slots, counts = route_index[0], route_count[0]
    routed = slots.shape[1]
    token_pos = pos * tokens + jnp.arange(tokens, dtype=jnp.int32)
    table_q = route_table(slots[0], counts[0], token_pos)
    table_kv = route_table(slots[1], counts[1], token_pos)
    table_f = route_table(slots[2], counts[2], token_pos)

    marked = jnp.concatenate(
        [x_in, jnp.broadcast_to(seg.astype(bf16)[:, None], (tokens, LANES))], axis=1
    )
    left = lax.ppermute(marked[tokens - WINDOW :], "seq", [(i, i + 1) for i in range(seq - 1)])
    right = lax.ppermute(marked[:WINDOW], "seq", [(i + 1, i) for i in range(seq - 1)])
    kv_part = dot(table_kv, marked).astype(bf16)

    rows = light_qkv.shape[0]
    small = jnp.stack([attn_gain, attn_router, ffn_gain, ffn_router], axis=1)
    first = jnp.concatenate([light_qkv, jnp.pad(small, ((0, 0), (0, LANES - 4)))], axis=1)
    wide = light_qkv.shape[1]

    def full(parts):
        return [p.reshape(-1, p.shape[-1]) for p in parts]

    def whole_view(block):
        return [(block.shape, lambda r: r)]

    z_first = gather_seq(first)
    w_lqkv, small_all = full(
        gather_dp(
            z_first,
            [
                ((seq, rows, wide), lambda r: r.at[:, :, :wide]),
                ((seq, rows, LANES), lambda r: r.at[:, :, wide:]),
            ],
        )
    )
    kv_marked = sum_seq(kv_part)
    z_hqkv = gather_seq(after(heavy_qkv, z_first))
    (w_hqkv,) = full(gather_dp(z_hqkv, whole_view(z_hqkv)))
    z_outs = gather_seq(after(jnp.stack([light_out, heavy_out]), z_hqkv))
    w_lout, w_hout = full(
        gather_dp(
            z_outs,
            [((seq, rows, width), lambda r: r.at[:, 0]), ((seq, rows, width), lambda r: r.at[:, 1])],
        )
    )
    z_lgu = gather_seq(after(light_gate_up, z_outs))
    (w_lgu,) = full(gather_dp(z_lgu, whole_view(z_lgu)))
    z_down = gather_seq(after(light_down, z_lgu))
    (w_ldown,) = full(gather_dp(z_down, whole_view(z_down)))
    unit = heavy_down.shape[0]
    columns = heavy_gate_up.reshape(rows, 2 * dp, seq, unit)

    def hidden_columns(which):
        return lax.dynamic_index_in_dim(columns, which, 2, keepdims=False).reshape(rows, -1)

    own_columns = hidden_columns(pos)
    gu_pieces = [own_columns] + [
        lax.ppermute(
            after(hidden_columns(pos ^ k), z_lgu), "seq", [(i, i ^ k) for i in range(seq)]
        )
        for k in range(1, seq)
    ]
    z_hgu = place_seq(gu_pieces, pos)
    (w_hgu,) = full(gather_dp(z_hgu, whole_view(z_hgu)))
    (w_hdown,) = full(gather_dp(after(heavy_down, z_hgu), whole_view(heavy_down)))
    cot_rows = sum_seq(after(dot(table_f, cot).astype(bf16), z_outs))

    small_t = small_all[:, :4].T
    gain_attn = small_t[0].astype(f32)[None]
    router_attn = small_t[1][None]
    gain_ffn = small_t[2].astype(f32)[None]
    router_ffn = small_t[3][None]

    ext_marked = jnp.concatenate([left, marked, right], axis=0)
    ext_in = ext_marked[:, :width].astype(f32)
    ext_inv = inv_rms(ext_in)
    normed_ext = (ext_in * ext_inv * gain_attn).astype(bf16)
    normed = normed_ext[WINDOW : WINDOW + tokens]
    place = jnp.arange(tokens + 2 * WINDOW) - WINDOW
    outside = ((pos == 0) & (place < 0)) | ((pos == seq - 1) & (place >= tokens))
    key_seg = jnp.where(outside, -1.0, ext_marked[:, width].astype(f32))
    seg_f = seg.astype(f32)
    light_allowed = (jnp.abs(jnp.arange(tokens)[:, None] - place[None, :]) <= WINDOW) & (
        seg_f[:, None] == key_seg[None, :]
    )
    light_q = dot(normed, w_lqkv[:, :width]).astype(bf16)
    light_kv = dot(normed_ext, w_lqkv[:, width:]).astype(bf16)
    light_k, light_v = light_kv[:, :width], light_kv[:, width:]
    light_mixed, light_lse = attend(light_q, light_k, light_v, light_allowed, L_HEAD)
    light_mixed = light_mixed.astype(bf16)

    kv_in = kv_marked[:, :width].astype(f32)
    kv_inv = inv_rms(kv_in)
    kv_rows = (kv_in * kv_inv * gain_attn).astype(bf16)
    kv_seg = kv_marked[:, width].astype(f32)
    kv_live = jnp.arange(routed) < counts[1]
    q_rows = dot(table_q, normed).astype(bf16)
    q_seg = jnp.sum(table_q.astype(f32) * seg_f[None], axis=1)
    heavy_allowed = (q_seg[:, None] == kv_seg[None, :]) & kv_live[None, :]
    heavy_q = dot(q_rows, w_hqkv[:, :width]).astype(bf16)
    heavy_kv = dot(kv_rows, w_hqkv[:, width:]).astype(bf16)
    heavy_k, heavy_v = heavy_kv[:, :width], heavy_kv[:, width:]
    heavy_mixed, heavy_lse = attend(heavy_q, heavy_k, heavy_v, heavy_allowed, H_HEAD)
    gate = sigmoid(
        jnp.sum(q_rows.astype(f32) * router_attn.astype(f32), axis=1, keepdims=True)
    )
    gated = (gate * heavy_mixed).astype(bf16)
    heavy_rows = dot(gated, w_hout).astype(bf16)
    midway = x_in.astype(f32) + dot(light_mixed, w_lout) + dot_tn(table_q, heavy_rows)

    inv_ffn = inv_rms(midway)
    normed_ffn = (midway * inv_ffn * gain_ffn).astype(bf16)
    ffn_rows = sum_seq(dot(table_f, normed_ffn).astype(bf16))
    light_units = w_ldown.shape[0]
    light_pre = dot(normed_ffn, w_lgu)
    light_gate, light_up = light_pre[:, :light_units], light_pre[:, light_units:]
    light_act, light_slope = gelu_both(light_gate)
    light_hidden = (light_act * light_up).astype(bf16)
    light_ffn = dot(light_hidden, w_ldown)

    grad_light_down = dot_tn(light_hidden, cot)
    out_light_down = scatter_both(grad_light_down)
    hidden_grad = dot_nt(cot, w_ldown).astype(bf16).astype(f32)
    light_pre_grad = jnp.concatenate(
        [hidden_grad * light_up * light_slope, hidden_grad * light_act], axis=-1
    ).astype(bf16)
    out_light_gate_up = scatter_both(dot_tn(normed_ffn, light_pre_grad))
    normed_ffn_grad = dot_nt(light_pre_grad, w_lgu)

    heavy_units = w_hdown.shape[0]
    heavy_pre = dot(ffn_rows, w_hgu)
    heavy_gate, heavy_up = heavy_pre[:, :heavy_units], heavy_pre[:, heavy_units:]
    heavy_act, heavy_slope = gelu_both(heavy_gate)
    ffn_gate = sigmoid(
        jnp.sum(ffn_rows.astype(f32) * router_ffn.astype(f32), axis=1, keepdims=True)
    )
    heavy_hidden = (ffn_gate * heavy_act * heavy_up).astype(bf16)
    heavy_grad = dot_nt(cot_rows, w_hdown).astype(bf16).astype(f32)
    heavy_pre_grad = jnp.concatenate(
        [heavy_grad * ffn_gate * heavy_up * heavy_slope, heavy_grad * ffn_gate * heavy_act],
        axis=-1,
    ).astype(bf16)
    ffn_score_grad = (
        ffn_gate
        * (1.0 - ffn_gate)
        * jnp.sum(heavy_grad * heavy_act * heavy_up, axis=1, keepdims=True)
    )
    rows_grad_part = dot_nt(heavy_pre_grad, w_hgu) + ffn_score_grad * router_ffn.astype(f32)
    rows_grad = sum_seq(rows_grad_part.astype(bf16))
    heavy_out_rows = sum_seq(after(dot(heavy_hidden, w_hdown).astype(bf16), rows_grad))
    layer_output = (midway + light_ffn + dot_tn(table_f, heavy_out_rows)).astype(bf16)
    grad_ffn_router = jnp.sum(ffn_rows.astype(f32) * ffn_score_grad, axis=0)
    grad_hdown = dot_tn(heavy_hidden, cot_rows).astype(bf16)
    out_heavy_down = scatter_dp(grad_hdown.reshape(dp, unit, width))
    grad_hgu = dot_tn(ffn_rows, heavy_pre_grad).astype(bf16)
    hgu_mine = scatter_dp(grad_hgu.reshape(dp, width // dp, -1)).astype(bf16)
    hgu_mine = hgu_mine.reshape(seq, rows, -1)
    hgu_got = [lax.dynamic_index_in_dim(hgu_mine, pos, 0, keepdims=False)] + [
        lax.ppermute(
            lax.dynamic_index_in_dim(hgu_mine, pos ^ k, 0, keepdims=False),
            "seq",
            [(i, i ^ k) for i in range(seq)],
        )
        for k in range(1, seq)
    ]
    hgu_slices = place_seq(hgu_got, pos).reshape(seq, rows, 2 * dp, unit)
    out_heavy_gate_up = hgu_slices.transpose(1, 2, 0, 3).astype(f32).reshape(rows, -1)

    normed_ffn_grad = normed_ffn_grad + dot_tn(table_f, rows_grad)
    grad_ffn_gain = jnp.sum(normed_ffn_grad * midway * inv_ffn, axis=0)
    midway_grad = cot.astype(f32) + norm_back(midway, inv_ffn, normed_ffn_grad * gain_ffn)

    out_grad = midway_grad.astype(bf16)
    grad_lout = dot_tn(light_mixed, out_grad).astype(bf16)
    heavy_out_cot = dot(table_q, out_grad).astype(bf16)
    grad_hout = dot_tn(gated, heavy_out_cot).astype(bf16)
    outs_pair = jnp.stack(
        [grad_lout.reshape(dp, width // dp, width), grad_hout.reshape(dp, width // dp, width)],
        axis=1,
    )
    outs_mine = scatter_dp(outs_pair).reshape(2, seq, rows, width).transpose(1, 0, 2, 3)
    out_outs = scatter_seq(outs_mine)
    mixed_grad = dot_nt(out_grad, w_lout).astype(bf16)
    light_q_grad, light_kv_grad = attend_back(
        light_q, light_k, light_v, light_allowed, light_lse, mixed_grad, L_HEAD
    )
    grad_lqkv = jnp.concatenate(
        [dot_tn(normed, light_q_grad), dot_tn(normed_ext, light_kv_grad)], axis=1
    )
    out_light_qkv = scatter_both(grad_lqkv)
    ext_grad = dot_nt(light_kv_grad, w_lqkv[:, width:])

    gated_grad = dot_nt(heavy_out_cot, w_hout).astype(bf16).astype(f32)
    heavy_mixed_grad = (gate * gated_grad).astype(bf16)
    attn_score_grad = gate * (1.0 - gate) * jnp.sum(gated_grad * heavy_mixed, axis=1, keepdims=True)
    heavy_q_grad, heavy_kv_grad = attend_back(
        heavy_q, heavy_k, heavy_v, heavy_allowed, heavy_lse, heavy_mixed_grad, H_HEAD
    )
    grad_attn_router = jnp.sum(q_rows.astype(f32) * attn_score_grad, axis=0)
    q_rows_grad = (
        dot_nt(heavy_q_grad, w_hqkv[:, :width]) + attn_score_grad * router_attn.astype(f32)
    ).astype(bf16)
    kv_rows_grad = dot_nt(heavy_kv_grad, w_hqkv[:, width:])

    own_grad = (
        ext_grad[WINDOW : WINDOW + tokens]
        + dot_nt(light_q_grad, w_lqkv[:, :width])
        + dot_tn(table_q, q_rows_grad)
    )
    grad_attn_gain = (
        jnp.sum(own_grad * (ext_in * ext_inv)[WINDOW : WINDOW + tokens], axis=0)
        + jnp.sum(ext_grad[:WINDOW] * (ext_in * ext_inv)[:WINDOW], axis=0)
        + jnp.sum(ext_grad[WINDOW + tokens :] * (ext_in * ext_inv)[WINDOW + tokens :], axis=0)
        + jnp.sum(kv_rows_grad * (kv_in * kv_inv), axis=0)
    )
    small_grads = jnp.stack([grad_attn_gain, grad_attn_router, grad_ffn_gain, grad_ffn_router], 1)
    grad_hqkv = jnp.concatenate(
        [
            dot_tn(q_rows, heavy_q_grad),
            dot_tn(kv_rows, heavy_kv_grad),
            jnp.pad(small_grads, ((0, 0), (0, LANES - 4))),
        ],
        axis=1,
    )
    out_hqkv_small = scatter_both(grad_hqkv)
    out_small = out_hqkv_small[:, wide : wide + 4].T

    kv_total = sum_seq(kv_rows_grad.astype(bf16))
    from_right = lax.ppermute(
        ext_grad[WINDOW + tokens :].astype(bf16), "seq", [(i, i + 1) for i in range(seq - 1)]
    )
    from_left = lax.ppermute(
        ext_grad[:WINDOW].astype(bf16), "seq", [(i + 1, i) for i in range(seq - 1)]
    )
    edge = jnp.concatenate(
        [from_right.astype(f32), jnp.zeros((tokens - 2 * WINDOW, width), f32), from_left.astype(f32)]
    )
    total_grad = own_grad + edge + dot_tn(table_kv, kv_total)
    x_wide = x_in.astype(f32)
    input_grad = midway_grad + norm_back(
        x_wide, ext_inv[WINDOW : WINDOW + tokens], total_grad * gain_attn
    )

    return (
        layer_output[None],
        input_grad.astype(bf16)[None],
        out_small[0],
        out_light_qkv,
        out_outs[0],
        out_hqkv_small[:, :wide],
        out_outs[1],
        out_small[1],
        out_small[2],
        out_light_gate_up,
        out_light_down,
        out_heavy_gate_up,
        out_heavy_down,
        out_small[3],
    )


def solution(mesh):
    both = ("dp", "seq")
    vector, matrix, tokens = P(both), P(both, None), P("dp", "seq", None)
    return jax.shard_map(
        shards,
        mesh=mesh,
        in_specs=(
            tokens,
            tokens,
            P("dp", "seq"),
            P("dp", None, None),
            P("dp", None),
            vector,
            matrix,
            matrix,
            matrix,
            matrix,
            vector,
            vector,
            matrix,
            matrix,
            matrix,
            matrix,
            vector,
        ),
        out_specs=(
            tokens,
            tokens,
            vector,
            matrix,
            matrix,
            matrix,
            matrix,
            vector,
            vector,
            matrix,
            matrix,
            matrix,
            matrix,
            vector,
        ),
        check_vma=False,
    )
```

time: 1810 us -> 574 us (0.32)
  waiting for transfers between devices: 1340 us -> 181 us
  blocking collectives: 188 us -> 0 us
  starting transfers between devices: 8.88 us -> 126 us
  matrix products: 167 us -> 102 us
  Pallas kernels: 0 us -> 41.3 us
  other arithmetic: 34.1 us -> 53.1 us
    reduce_scatter x13 -> x0, waiting for transfers between devices: 929 us -> none  [the longest x1 253 us: shards(): lax.psum_scatter(grad_heavy_gate_up, ('dp', 'seq'), scatter_dimension=0,...]
    all_gather x8 -> x0, waiting for transfers between devices: 396 us -> none  [the longest x1 86.4 us: shards(): lax.all_gather(ffn_shards[3], ('dp', 'seq'), axis=0, tiled=True)]
    ppermute x4 -> x122, waiting for transfers between devices: 7.51 us -> 181 us  [the longest x12 68.2 us: sum_seq(): got = lax.ppermute(part, 'seq', [(i, i ^ mask) for i in range(count)])]
    ppermute x4 -> x122, starting transfers between devices: 7.37 us -> 126 us  [the longest x49 26.4 us: gather_dp(): pieces = pieces + [lax.ppermute(p, 'dp', pairs) for p in pieces]]
    all_gather x7 -> x0, blocking collectives: 106 us -> none  [the longest x5 75 us: home_rows(): lax.all_gather(as_sent(sources), 'seq', axis=1, tiled=True)]
    unnamed x2 -> x0, blocking collectives: 82.7 us -> none
    dot_general x53 -> x50, matrix products: 167 us -> 102 us  [the longest x14 22.7 us: dot(): lax.dot_general(a, b, (((1,), (0,)), ((), ())), preferred_element_type=f32)]
    pallas_call x0 -> x21, Pallas kernels: none -> 41.3 us  [dma_moves(): pl.pallas_call(body, out_shape=[jax.ShapeDtypeStruct(s, a) for s, a in ou...]
  transfers between devices with their start and end apart: 26 -> 122, of which waited for: 19 -> 41; matrix products, arithmetic and copies ran while one was open for 11% -> 34% of each run, Pallas kernels for 0% -> 7%
where the time goes in v1:
time: 574 us; the launch traced here: 564 us
  waiting for transfers between devices  181 us (32%)
  starting transfers between devices  126 us (22%)
  matrix products  102 us (18%)
  local copies, waits for them, and re-layouts  57.8 us (10%)
  other arithmetic  53.1 us (9%)
  Pallas kernels  41.3 us (7%)
    ppermute x12, waiting for transfers between devices, sum_seq(): got = lax.ppermute(part, 'seq', [(i, i ^ mask) for i in range(count)])  68.2 us
    pallas_call x21, Pallas kernels, dma_moves(): pl.pallas_call(body, out_shape=[jax.ShapeDtypeStruct(s, a) for s, a in ou...  41.3 us
    ppermute x21, waiting for transfers between devices, scatter_dp(): got = lax.ppermute(send, 'dp', perm(count, stage))  26.6 us
    ppermute x49, starting transfers between devices, gather_dp(): pieces = pieces + [lax.ppermute(p, 'dp', pairs) for p in pieces]  26.4 us
    ppermute x15, waiting for transfers between devices, scatter_seq(): lax.ppermute(piece, 'seq', [(i, i ^ k) for i in range(count)]).astype(f32)  24.7 us
    ppermute x15, waiting for transfers between devices, seq_pieces(): lax.ppermute(shard, 'seq', [(i, i ^ k) for i in range(count)])  23.3 us
    ppermute x15, starting transfers between devices, seq_pieces(): lax.ppermute(shard, 'seq', [(i, i ^ k) for i in range(count)])  22.9 us
    dot_general x14, matrix products, dot(): lax.dot_general(a, b, (((1,), (0,)), ((), ())), preferred_element_type=f32)  22.7 us
  transfers between devices with their start and end apart: 122, of which 41 were waited for; matrix products, arithmetic and copies ran while one was open for 34% of the time, Pallas kernels for 7%

profile of v1, /device:TPU:0, one launch (start us, length us, event | category | flops | bytes accessed | tf_op | source)
XLA Modules:
  0.0 564.2 jit_solution(18138324130767965083)
XLA Ops:
  2.5 5.1 collective-permute-start.4
  28.6 9.3 %collective-permute-done.14.refs_3_ = bf16[24,2304]{1,0:T(8,128)(2,1)S(1)} collective-permute-done((bf16[24,2304]{1,0:T(8,128)(2,1)S(1)}, bf16[24,2304]{1,0:T(8,128)(2,1)S(1)}, u32[]{:S(2)}, u32[]{:S(2)}) %collective-permute-start.14) | collective-permute-done | bytes 110624 | tf_op jit(solution)/shard_map/ppermute | solution.py:69
  53.7 4.4 collective-permute-done.36.refs_3_
  87.0 6.1 %collective-permute-done.57.refs_2_ = bf16[24,2048]{1,0:T(8,128)(2,1)S(1)} collective-permute-done((bf16[24,2048]{1,0:T(8,128)(2,1)S(1)}, bf16[24,2048]{1,0:T(8,128)(2,1)S(1)}, u32[]{:S(2)}, u32[]{:S(2)}) %collective-permute-start.57) | collective-permute-done | bytes 98336 | tf_op jit(solution)/shard_map/ppermute | solution.py:311
  120.7 6.2 %collective-permute-done.49.refs_3_ = bf16[4,32,768]{2,1,0:T(8,128)(2,1)S(1)} collective-permute-done((bf16[4,32,768]{2,1,0:T(8,128)(2,1)S(1)}, bf16[4,32,768]{2,1,0:T(8,128)(2,1)S(1)}, u32[]{:S(2)}, u32[]{:S(2)}) %collective-permute-start.49) | collective-permute-done | bytes 196640 | tf_op jit(solution)/shard_map/ppermute | solution.py:94
  130.3 8.6 %collective-permute-done.26 = bf16[256,896]{1,0:T(8,128)(2,1)S(1)} collective-permute-done((bf16[256,896]{1,0:T(8,128)(2,1)S(1)}, bf16[256,896]{1,0:T(8,128)(2,1)S(1)}, u32[]{:S(2)}, u32[]{:S(2)}) %collective-permute-start.26) | collective-permute-done | bytes 458784 | tf_op jit(solution)/shard_map/ppermute | solution.py:152
  191.2 5.7 %fusion.44 = bf16[8,96,512]{2,1,0:T(8,128)(2,1)} fusion(bf16[768,8,96]{0,2,1:T(8,128)(2,1)S(1)} %bitcast.321, f32[8,512,768]{2,1,0:T(8,128)S(1)} %get-tuple-element.146, f32[8,512]{1,0:T(8,128)S(1)} %fusion, f32[8,512]{1,0:T(8,128)S(1)} %get-tuple-element.145, pred[512,768]{1,0:T(8,128)(4,1)S(1)} %copy-done.44), kind=kOutput, calls=%fused_computation.110 | convolution fusion | flops 620101632 | bytes 14974976 | tf_op jit(solution)/shard_map/hqk,khe->qhe/dot_general | solution.py:212
  225.4 5.0 collective-permute-done.61.refs_3_
  237.0 5.0 collective-permute-done.54
  256.7 13.9 %collective-permute-done.55 = bf16[256,768]{1,0:T(8,128)(2,1)S(1)} collective-permute-done((bf16[256,768]{1,0:T(8,128)(2,1)S(1)}, bf16[256,768]{1,0:T(8,128)(2,1)S(1)}, u32[]{:S(2)}, u32[]{:S(2)}) %collective-permute-start.55) | collective-permute-done | bytes 393248 | tf_op jit(solution)/shard_map/ppermute | solution.py:152
  271.9 7.1 %collective-permute-done.74 = bf16[256,768]{1,0:T(8,128)(2,1)S(1)} collective-permute-done((bf16[256,768]{1,0:T(8,128)(2,1)S(1)}, bf16[256,768]{1,0:T(8,128)(2,1)S(1)}, u32[]{:S(2)}, u32[]{:S(2)}) %collective-permute-start.74) | collective-permute-done | bytes 393248 | tf_op jit(solution)/shard_map/ppermute | solution.py:152
  286.8 4.3 collective-permute-done.108
  309.5 7.4 %collective-permute-done.111 = bf16[32,768]{1,0:T(8,128)(2,1)S(1)} collective-permute-done((bf16[32,768]{1,0:T(8,128)(2,1)S(1)}, bf16[32,768]{1,0:T(8,128)(2,1)S(1)}, u32[]{:S(2)}, u32[]{:S(2)}) %collective-permute-start.111) | collective-permute-done | bytes 49184 | tf_op jit(solution)/shard_map/ppermute | solution.py:137
  336.4 6.5 %fusion.41 = bf16[8,96,768]{2,1,0:T(8,128)(2,1)S(1)} fusion(bf16[512,8,96]{0,2,1:T(8,128)(2,1)S(1)} %bitcast.338, f32[8,512,768]{2,1,0:T(8,128)} %copy-done.32, f32[8,512]{1,0:T(8,128)S(1)} %log_add_fusion.1, pred[512,768]{1,0:T(8,128)(4,1)S(1)} %copy-done.45), kind=kOutput, calls=%fused_computation.101 | convolution fusion | flops 617152512 | bytes 14958592 | tf_op jit(solution)/shard_map/hqk,qhe->khe/dot_general | solution.py:226
  343.0 10.8 %multiply_reduce_fusion = (f32[8,512]{1,0:T(8,128)S(1)}, f32[8,512,768]{2,1,0:T(8,128)}) fusion(f32[8,512,768]{2,1,0:T(8,128)} %copy-done.32, f32[8,512]{1,0:T(8,128)S(1)} %log_add_fusion.1, pred[512,768]{1,0:T(8,128)(4,1)S(1)} %copy-done.45, bf16[512,8,96]{0,2,1:T(8,128)(2,1)S(1)} %bitcast.339, bf16[768,8,96]{0,2,1:T(8,128)(2,1)S(1)} %bitcast.322), kind=kOutput, calls=%fused_computation.1 | convolution fusion | flops 619704320 | bytes 27557888 | tf_op jit(solution)/shard_map/qhe,khe->hqk/dot_general | solution.py:221
  353.8 7.0 %multiply_convert_fusion = bf16[8,512,768]{2,1,0:T(8,128)(2,1)S(1)} fusion(f32[8,512,768]{2,1,0:T(8,128)} %get-tuple-element.155, f32[8,512,768]{2,1,0:T(8,128)S(1)} %bitcast.308, f32[8,512]{1,0:T(8,128)S(1)} %get-tuple-element.154, f32[8,512]{1,0:T(8,128)S(1)} %log_add_fusion.1, pred[512,768]{1,0:T(8,128)(4,1)S(1)} %copy-done.45), kind=kLoop, calls=%fused_computation | loop fusion | flops 18874368 | bytes 31883264 | tf_op jit(solution)/shard_map/convert_element_type | solution.py:223
  421.3 4.5 collective-permute-done.81
  426.7 6.4 %collective-permute-done.121 = bf16[1,128,768]{2,1,0:T(8,128)(2,1)S(1)} collective-permute-done((bf16[1,128,768]{2,1,0:T(8,128)(2,1)S(1)}, bf16[1,128,768]{2,1,0:T(8,128)(2,1)S(1)}, u32[]{:S(2)}, u32[]{:S(2)}) %collective-permute-start.121) | collective-permute-done | bytes 196640 | tf_op jit(solution)/shard_map/ppermute | solution.py:123
  438.9 28.7 %collective-permute-done.82 = bf16[256,768]{1,0:T(8,128)(2,1)S(1)} collective-permute-done((bf16[256,768]{1,0:T(8,128)(2,1)S(1)}, bf16[256,768]{1,0:T(8,128)(2,1)S(1)}, u32[]{:S(2)}, u32[]{:S(2)}) %collective-permute-start.82) | collective-permute-done | bytes 393248 | tf_op jit(solution)/shard_map/ppermute | solution.py:152
  476.6 5.3 collective-permute-done.103
  510.5 6.4 %collective-permute-start.117 = (bf16[24,2048]{1,0:T(8,128)(2,1)S(1)}, bf16[24,2048]{1,0:T(8,128)(2,1)S(1)}, u32[]{:S(2)}, u32[]{:S(2)}) collective-permute-start(bf16[24,2048]{1,0:T(8,128)(2,1)S(1)} %get-tuple-element.117), channel_id=1, source_target_pairs={{0,2},{1,3},{2,0},{3,1},{4,6},{5,7},{6,4},{7,5},{8,10},{9,11},{10,... | collective-permute-start | bytes 294920 | tf_op jit(solution)/shard_map/ppermute | solution.py:412
  535.4 4.7 collective-permute-done.91
  545.3 4.7 collective-permute-start.86
  551.6 7.2 %collective-permute-done.93 = bf16[24,2304]{1,0:T(8,128)(2,1)S(1)} collective-permute-done((bf16[24,2304]{1,0:T(8,128)(2,1)S(1)}, bf16[24,2304]{1,0:T(8,128)(2,1)S(1)}, u32[]{:S(2)}, u32[]{:S(2)}) %collective-permute-start.93) | collective-permute-done | bytes 110624 | tf_op jit(solution)/shard_map/ppermute | solution.py:137
  (688 shorter events, 380.8 us)
Async XLA Ops:
  10.9 56.8 %collective-permute-start = (bf16[128,896]{1,0:T(8,128)(2,1)}, bf16[128,896]{1,0:T(8,128)(2,1)S(1)}, u32[]{:S(2)}, u32[]{:S(2)}) collective-permute-start(bf16[128,896]{1,0:T(8,128)(2,1)} %get-tuple-element.102), channel_id=1, source_target_pairs={{0,1},{1,2},{2,3},{4,5},{5,6},{6,7},{8,9},{9,10},{10,11},{12,13},{... | collective-permute-start | bytes 688136 | tf_op jit(solution)/shard_map/ppermute | solution.py:264
  19.4 60.5 %collective-permute-start.25 = (bf16[256,896]{1,0:T(8,128)(2,1)}, bf16[256,896]{1,0:T(8,128)(2,1)}, u32[]{:S(2)}, u32[]{:S(2)}) collective-permute-start(bf16[256,896]{1,0:T(8,128)(2,1)} %convolution_convert_fusion.16), channel_id=1, source_target_pairs={{0,1},{1,0},{2,3},{3,2},{4,5},{5,4},{6,7},{7,6},{8,9},{9,8},{10,11... | collective-permute-start | bytes 1376264 | tf_op jit(solution)/shard_map/ppermute | solution.py:152
  58.2 35.4 %collective-permute-start.8 = (bf16[4,24,2432]{2,1,0:T(8,128)(2,1)S(1)}, bf16[4,24,2432]{2,1,0:T(8,128)(2,1)S(1)}, u32[]{:S(2)}, u32[]{:S(2)}) collective-permute-start(bf16[4,24,2432]{2,1,0:T(8,128)(2,1)S(1)} %shard_map.272.refs_0_), channel_id=1, source_target_pairs={{0,4},{4,0},{8,12},{12,8},{16,20},{20,16},{24,28},{28,24},{1,5},{5... | collective-permute-start | bytes 1400840 | tf_op jit(solution)/shard_map/ppermute | solution.py:94
  154.3 42.6 %collective-permute-start.30 = (bf16[4,24,2304]{2,1,0:T(8,128)(2,1)S(1)}, bf16[4,24,2304]{2,1,0:T(8,128)(2,1)S(1)}, u32[]{:S(2)}, u32[]{:S(2)}) collective-permute-start(bf16[4,24,2304]{2,1,0:T(8,128)(2,1)S(1)} %shard_map.274.refs_0_), channel_id=1, source_target_pairs={{0,4},{4,0},{8,12},{12,8},{16,20},{20,16},{24,28},{28,24},{1,5},{5... | collective-permute-start | bytes 1327112 | tf_op jit(solution)/shard_map/ppermute | solution.py:94
  154.3 43.1 %collective-permute-start.37 = (bf16[4,24,2048]{2,1,0:T(8,128)(2,1)S(1)}, bf16[4,24,2048]{2,1,0:T(8,128)(2,1)}, u32[]{:S(2)}, u32[]{:S(2)}) collective-permute-start(bf16[4,24,2048]{2,1,0:T(8,128)(2,1)S(1)} %shard_map.278.refs_0_), channel_id=1, source_target_pairs={{0,8},{4,20},{8,0},{12,28},{16,24},{20,4},{24,16},{28,12},{1,9},{5... | collective-permute-start | bytes 1179656 | tf_op jit(solution)/shard_map/ppermute | solution.py:94
  155.1 44.3 %collective-permute-start.31 = (bf16[4,24,2304]{2,1,0:T(8,128)(2,1)}, bf16[4,24,2304]{2,1,0:T(8,128)(2,1)}, u32[]{:S(2)}, u32[]{:S(2)}) collective-permute-start(bf16[4,24,2304]{2,1,0:T(8,128)(2,1)} %collective-permute-done.27.refs_1_), channel_id=1, source_target_pairs={{0,4},{4,0},{8,12},{12,8},{16,20},{20,16},{24,28},{28,24},{1,5},{5... | collective-permute-start | bytes 1327112 | tf_op jit(solution)/shard_map/ppermute | solution.py:94
  155.2 43.2 %collective-permute-start.32 = (bf16[4,24,2304]{2,1,0:T(8,128)(2,1)}, bf16[4,24,2304]{2,1,0:T(8,128)(2,1)}, u32[]{:S(2)}, u32[]{:S(2)}) collective-permute-start(bf16[4,24,2304]{2,1,0:T(8,128)(2,1)} %collective-permute-done.28.refs_2_), channel_id=1, source_target_pairs={{0,4},{4,0},{8,12},{12,8},{16,20},{20,16},{24,28},{28,24},{1,5},{5... | collective-permute-start | bytes 1327112 | tf_op jit(solution)/shard_map/ppermute | solution.py:94
  155.7 45.0 %collective-permute-start.33 = (bf16[4,24,2304]{2,1,0:T(8,128)(2,1)}, bf16[4,24,2304]{2,1,0:T(8,128)(2,1)}, u32[]{:S(2)}, u32[]{:S(2)}) collective-permute-start(bf16[4,24,2304]{2,1,0:T(8,128)(2,1)} %collective-permute-done.29.refs_3_), channel_id=1, source_target_pairs={{0,4},{4,0},{8,12},{12,8},{16,20},{20,16},{24,28},{28,24},{1,5},{5... | collective-permute-start | bytes 1327112 | tf_op jit(solution)/shard_map/ppermute | solution.py:94
  224.4 27.6 %collective-permute-start.62 = (bf16[4,24,2048]{2,1,0:T(8,128)(2,1)S(1)}, bf16[4,24,2048]{2,1,0:T(8,128)(2,1)S(1)}, u32[]{:S(2)}, u32[]{:S(2)}) collective-permute-start(bf16[4,24,2048]{2,1,0:T(8,128)(2,1)S(1)} %shard_map.282.refs_0_), channel_id=1, source_target_pairs={{0,4},{4,0},{8,12},{12,8},{16,20},{20,16},{24,28},{28,24},{1,5},{5... | collective-permute-start | bytes 1179656 | tf_op jit(solution)/shard_map/ppermute | solution.py:94
  224.9 29.4 %collective-permute-start.63 = (bf16[4,24,2048]{2,1,0:T(8,128)(2,1)}, bf16[4,24,2048]{2,1,0:T(8,128)(2,1)S(1)}, u32[]{:S(2)}, u32[]{:S(2)}) collective-permute-start(bf16[4,24,2048]{2,1,0:T(8,128)(2,1)} %collective-permute-done.59.refs_1_), channel_id=1, source_target_pairs={{0,4},{4,0},{8,12},{12,8},{16,20},{20,16},{24,28},{28,24},{1,5},{5... | collective-permute-start | bytes 1179656 | tf_op jit(solution)/shard_map/ppermute | solution.py:94
  225.0 29.3 %collective-permute-start.64 = (bf16[4,24,2048]{2,1,0:T(8,128)(2,1)}, bf16[4,24,2048]{2,1,0:T(8,128)(2,1)S(1)}, u32[]{:S(2)}, u32[]{:S(2)}) collective-permute-start(bf16[4,24,2048]{2,1,0:T(8,128)(2,1)} %collective-permute-done.60.refs_2_), channel_id=1, source_target_pairs={{0,4},{4,0},{8,12},{12,8},{16,20},{20,16},{24,28},{28,24},{1,5},{5... | collective-permute-start | bytes 1179656 | tf_op jit(solution)/shard_map/ppermute | solution.py:94
  242.0 28.6 %collective-permute-start.55 = (bf16[256,768]{1,0:T(8,128)(2,1)S(1)}, bf16[256,768]{1,0:T(8,128)(2,1)S(1)}, u32[]{:S(2)}, u32[]{:S(2)}) collective-permute-start(bf16[256,768]{1,0:T(8,128)(2,1)S(1)} %add_convert_fusion.27), channel_id=1, source_target_pairs={{0,2},{1,3},{2,0},{3,1},{4,6},{5,7},{6,4},{7,5},{8,10},{9,11},{10,... | collective-permute-start | bytes 1179656 | tf_op jit(solution)/shard_map/ppermute | solution.py:152
  254.3 28.8 %collective-permute-start.107 = (bf16[4,128,768]{2,1,0:T(8,128)(2,1)S(1)}, bf16[4,128,768]{2,1,0:T(8,128)(2,1)S(1)}, u32[]{:S(2)}, u32[]{:S(2)}) collective-permute-start(bf16[4,128,768]{2,1,0:T(8,128)(2,1)S(1)} %get-tuple-element.65), channel_id=1, source_target_pairs={{0,4},{4,0},{8,12},{12,8},{16,20},{20,16},{24,28},{28,24},{1,5},{5... | collective-permute-start | bytes 2359304 | tf_op jit(solution)/shard_map/ppermute | solution.py:123
  254.3 155.2 %collective-permute-start.101 = (bf16[4,96,2048]{2,1,0:T(8,128)(2,1)}, bf16[4,96,2048]{2,1,0:T(8,128)(2,1)}, u32[]{:S(2)}, u32[]{:S(2)}) collective-permute-start(bf16[4,96,2048]{2,1,0:T(8,128)(2,1)} %get-tuple-element.63), channel_id=1, source_target_pairs={{0,4},{4,0},{8,12},{12,8},{16,20},{20,16},{24,28},{28,24},{1,5},{5... | collective-permute-start | bytes 4718600 | tf_op jit(solution)/shard_map/ppermute | solution.py:123
  309.0 65.0 %collective-permute-start.119 = (bf16[4,128,768]{2,1,0:T(8,128)(2,1)S(1)}, bf16[4,128,768]{2,1,0:T(8,128)(2,1)}, u32[]{:S(2)}, u32[]{:S(2)}) collective-permute-start(bf16[4,128,768]{2,1,0:T(8,128)(2,1)S(1)} %get-tuple-element.69), channel_id=1, source_target_pairs={{0,4},{4,0},{8,12},{12,8},{16,20},{20,16},{24,28},{28,24},{1,5},{5... | collective-permute-start | bytes 2359304 | tf_op jit(solution)/shard_map/ppermute | solution.py:123
  309.0 125.5 %collective-permute-start.113 = (bf16[4,96,2048]{2,1,0:T(8,128)(2,1)}, bf16[4,96,2048]{2,1,0:T(8,128)(2,1)}, u32[]{:S(2)}, u32[]{:S(2)}) collective-permute-start(bf16[4,96,2048]{2,1,0:T(8,128)(2,1)} %get-tuple-element.67), channel_id=1, source_target_pairs={{0,4},{4,0},{8,12},{12,8},{16,20},{20,16},{24,28},{28,24},{1,5},{5... | collective-permute-start | bytes 4718600 | tf_op jit(solution)/shard_map/ppermute | solution.py:123
  364.8 54.7 %collective-permute-start.77 = (bf16[256,768]{1,0:T(8,128)(2,1)}, bf16[256,768]{1,0:T(8,128)(2,1)}, u32[]{:S(2)}, u32[]{:S(2)}) collective-permute-start(bf16[256,768]{1,0:T(8,128)(2,1)} %convolution_convert_fusion.20), channel_id=1, source_target_pairs={{0,1},{1,0},{2,3},{3,2},{4,5},{5,4},{6,7},{7,6},{8,9},{9,8},{10,11... | collective-permute-start | bytes 1179656 | tf_op jit(solution)/shard_map/ppermute | solution.py:152
  376.3 41.9 %collective-permute-start.120 = (bf16[2,128,768]{2,1,0:T(8,128)(2,1)}, bf16[2,128,768]{2,1,0:T(8,128)(2,1)}, u32[]{:S(2)}, u32[]{:S(2)}) collective-permute-start(bf16[2,128,768]{2,1,0:T(8,128)(2,1)} %slice.396), channel_id=1, source_target_pairs={{0,16},{4,12},{8,24},{12,4},{16,0},{20,28},{24,8},{28,20},{1,17},{... | collective-permute-start | bytes 1179656 | tf_op jit(solution)/shard_map/ppermute | solution.py:123
  413.2 71.7 %collective-permute-start.95 = (bf16[4,2,96,768]{3,2,1,0:T(8,128)(2,1)S(1)}, bf16[4,2,96,768]{3,2,1,0:T(8,128)(2,1)S(1)}, u32[]{:S(2)}, u32[]{:S(2)}) collective-permute-start(bf16[4,2,96,768]{3,2,1,0:T(8,128)(2,1)S(1)} %copy-done.31), channel_id=1, source_target_pairs={{0,4},{4,0},{8,12},{12,8},{16,20},{20,16},{24,28},{28,24},{1,5},{5... | collective-permute-start | bytes 3538952 | tf_op jit(solution)/shard_map/ppermute | solution.py:123
  418.2 84.2 %collective-permute-start.89 = (bf16[4,96,2304]{2,1,0:T(8,128)(2,1)S(1)}, bf16[4,96,2304]{2,1,0:T(8,128)(2,1)S(1)}, u32[]{:S(2)}, u32[]{:S(2)}) collective-permute-start(bf16[4,96,2304]{2,1,0:T(8,128)(2,1)S(1)} %copy-done.29), channel_id=1, source_target_pairs={{0,4},{4,0},{8,12},{12,8},{16,20},{20,16},{24,28},{28,24},{1,5},{5... | collective-permute-start | bytes 5308424 | tf_op jit(solution)/shard_map/ppermute | solution.py:123
  419.5 53.2 %collective-permute-start.102 = (bf16[2,96,2048]{2,1,0:T(8,128)(2,1)S(1)}, bf16[2,96,2048]{2,1,0:T(8,128)(2,1)S(1)}, u32[]{:S(2)}, u32[]{:S(2)}) collective-permute-start(bf16[2,96,2048]{2,1,0:T(8,128)(2,1)S(1)} %slice.384), channel_id=1, source_target_pairs={{0,16},{4,12},{8,24},{12,4},{16,0},{20,28},{24,8},{28,20},{1,17},{... | collective-permute-start | bytes 2359304 | tf_op jit(solution)/shard_map/ppermute | solution.py:123
  433.1 37.0 %collective-permute-start.78 = (bf16[256,768]{1,0:T(8,128)(2,1)S(1)}, bf16[256,768]{1,0:T(8,128)(2,1)S(1)}, u32[]{:S(2)}, u32[]{:S(2)}) collective-permute-start(bf16[256,768]{1,0:T(8,128)(2,1)S(1)} %add_convert_fusion.21), channel_id=1, source_target_pairs={{0,2},{1,3},{2,0},{3,1},{4,6},{5,7},{6,4},{7,5},{8,10},{9,11},{10,... | collective-permute-start | bytes 1179656 | tf_op jit(solution)/shard_map/ppermute | solution.py:152
  434.5 33.2 %collective-permute-start.82 = (bf16[256,768]{1,0:T(8,128)(2,1)S(1)}, bf16[256,768]{1,0:T(8,128)(2,1)S(1)}, u32[]{:S(2)}, u32[]{:S(2)}) collective-permute-start(bf16[256,768]{1,0:T(8,128)(2,1)S(1)} %add_convert_fusion.19), channel_id=1, source_target_pairs={{0,2},{1,3},{2,0},{3,1},{4,6},{5,7},{6,4},{7,5},{8,10},{9,11},{10,... | collective-permute-start | bytes 1179656 | tf_op jit(solution)/shard_map/ppermute | solution.py:152
  467.7 28.3 %collective-permute-start.114 = (bf16[2,96,2048]{2,1,0:T(8,128)(2,1)S(1)}, bf16[2,96,2048]{2,1,0:T(8,128)(2,1)S(1)}, u32[]{:S(2)}, u32[]{:S(2)}) collective-permute-start(bf16[2,96,2048]{2,1,0:T(8,128)(2,1)S(1)} %slice.392), channel_id=1, source_target_pairs={{0,16},{4,12},{8,24},{12,4},{16,0},{20,28},{24,8},{28,20},{1,17},{... | collective-permute-start | bytes 2359304 | tf_op jit(solution)/shard_map/ppermute | solution.py:123
  (218 other events, 2252.5 us)

commit v2 on v1

v2 whole, which is shorter than its diff:
```python
import jax
import jax.numpy as jnp
from jax import lax
from jax.experimental import pallas as pl
from jax.experimental.pallas import tpu as pltpu
from jax.sharding import PartitionSpec as P

L_HEADS = 8
L_HEAD = 96
H_HEADS = 12
H_HEAD = 64
WINDOW = 128
LANES = 128

epsilon = 1e-06
masked_score = -1e30
gelu_scale = 0.7978845608028654
bf16 = jnp.bfloat16
f32 = jnp.float32


def dma_moves(index, arrays, out_shapes, moves):
    def body(index_ref, *refs):
        ins, outs, sems = refs[: len(arrays)], refs[len(arrays) : -1], refs[-1]
        copies = [
            pltpu.make_async_copy(source(ins, index_ref), target(outs, index_ref), sems.at[k])
            for k, (source, target) in enumerate(moves)
        ]
        for copy in copies:
            copy.start()
        for copy in copies:
            copy.wait()

    return pl.pallas_call(
        body,
        out_shape=[jax.ShapeDtypeStruct(s, a) for s, a in out_shapes],
        in_specs=[pl.BlockSpec(memory_space=pltpu.SMEM)]
        + [pl.BlockSpec(memory_space=pl.ANY)] * len(arrays),
        out_specs=[pl.BlockSpec(memory_space=pltpu.VMEM)] * len(out_shapes),
        scratch_shapes=[pltpu.SemaphoreType.DMA((len(moves),))],
        compiler_params=pltpu.CompilerParams(vmem_limit_bytes=16 * 2**20),
    )(index, *arrays)


def dp_stages(count):
    if count == 8:
        return [
            lambda i: i ^ (2 + 2 * (i & 1)),
            lambda i: i ^ (4 - 2 * (i & 1)),
            lambda i: i ^ 1,
        ]
    masks = [1 << b for b in range(count.bit_length() - 1)][::-1]
    return [lambda i, m=m: i ^ m for m in masks]


def dp_labels(count):
    labels = [()]
    for stage in range(len(dp_stages(count))):
        labels = labels + [label + (stage,) for label in labels]
    return labels


def dp_order():
    count, me = lax.axis_size("dp"), lax.axis_index("dp")
    stages = dp_stages(count)

    def source(label):
        at = me
        for stage in label[::-1]:
            at = stages[stage](at)
        return at

    return jnp.stack([source(label) for label in dp_labels(count)]).astype(jnp.int32)


def perm(count, stage):
    return [(i, stage(i)) for i in range(count)]


def perm_seq(count, k):
    return [(i, i ^ k) for i in range(count)]


def place_seq(pieces):
    count, pos = len(pieces), lax.axis_index("seq")
    order = jnp.stack([pos ^ k for k in range(count)]).astype(jnp.int32)
    moves = [
        (lambda ins, idx, k=k: ins[k], lambda outs, idx, k=k: outs[0].at[idx[k]])
        for k in range(count)
    ]
    shape = (count,) + pieces[0].shape
    return dma_moves(order, pieces, [(shape, pieces[0].dtype)], moves)[0]


def send_seq(piece_for):
    count = lax.axis_size("seq")
    return [lax.ppermute(piece_for(k), "seq", perm_seq(count, k)) for k in range(1, count)]


def wave(pieces, hops):
    count = lax.axis_size("dp")
    stages = dp_stages(count)
    for label in [p for p in pieces if len(p) == hops]:
        for stage in range(label[-1] + 1 if label else 0, len(stages)):
            pieces[label + (stage,)] = lax.ppermute(
                pieces[label], "dp", perm(count, stages[stage])
            )


def arrived(pieces, hops, last=None):
    final = len(dp_stages(lax.axis_size("dp"))) - 1
    return [p for p in pieces if len(p) == hops and (last or p[-1] != final)]


def fence(*values):
    return lax.optimization_barrier(values) if len(values) > 1 else values


def fence_pieces(groups, *values):
    flat = [pieces[label] for pieces, labels in groups for label in labels]
    out = fence(*values, *flat)
    rest = list(out[len(values) :])
    for pieces, labels in groups:
        for label in labels:
            pieces[label] = rest.pop(0)
    return out[: len(values)]


def place_dp(held, widths):
    pieces = [held[label] for label in dp_labels(lax.axis_size("dp"))]
    count = len(pieces)
    lead = pieces[0].shape[:-1]
    moves, shapes, low = [], [], 0
    for j, columns in enumerate(widths):
        shapes.append(((count,) + lead + (columns,), bf16))
        for k in range(count):
            moves.append(
                (
                    lambda ins, idx, k=k, low=low, columns=columns: ins[k].at[
                        ..., pl.ds(low, columns)
                    ],
                    lambda outs, idx, k=k, j=j: outs[j].at[idx[k]],
                )
            )
        low += columns
    return [p.reshape(-1, p.shape[-1]) for p in dma_moves(dp_order(), pieces, shapes, moves)]


def scatter_dp(grads):
    count = lax.axis_size("dp")
    half = count // 2
    rows = grads[0].shape[1]
    width = sum(g.shape[2] for g in grads)
    moves, low = [], 0
    for j, grad in enumerate(grads):
        columns = grad.shape[2]
        for k in range(count):
            moves.append(
                (
                    lambda ins, idx, k=k, j=j: ins[j].at[idx[k]],
                    lambda outs, idx, k=k, low=low, columns=columns: outs[k // half].at[
                        k % half, :, pl.ds(low, columns)
                    ],
                )
            )
        low += columns
    shape = (half, rows, width)
    keep, send = dma_moves(dp_order(), grads, [(shape, bf16), (shape, bf16)], moves)
    return Scatter(keep, send)


class Scatter:
    def __init__(self, keep, send):
        self.keep, self.left = keep, dp_stages(lax.axis_size("dp"))
        self.hop(send)

    def hop(self, send):
        count = lax.axis_size("dp")
        self.got = lax.ppermute(send, "dp", perm(count, self.left.pop()))

    def step(self):
        half = self.keep.shape[0] // 2
        wide = lambda part: part.astype(f32)
        send = (wide(self.keep[half:]) + wide(self.got[half:])).astype(bf16)
        self.keep = (wide(self.keep[:half]) + wide(self.got[:half])).astype(bf16)
        self.hop(send)

    def finish(self):
        while self.left:
            self.step()
        return self.keep[0].astype(f32) + self.got[0].astype(f32)


def fence_sums(sums, *values):
    out = fence(*values, *[s.got for s in sums])
    for s, got in zip(sums, out[len(values) :]):
        s.got = got
    return out[: len(values)]


def scatter_seq(blocks):
    count, pos = lax.axis_size("seq"), lax.axis_index("seq")
    sent = blocks.astype(bf16)
    total = lax.dynamic_index_in_dim(blocks, pos, 0, keepdims=False)
    for k in range(1, count):
        piece = lax.dynamic_index_in_dim(sent, pos ^ k, 0, keepdims=False)
        total = total + lax.ppermute(piece, "seq", perm_seq(count, k)).astype(f32)
    return total


def seq_masks():
    return [1 << b for b in range(lax.axis_size("seq").bit_length() - 1)]


def sum_hop(part, mask):
    got = lax.ppermute(part, "seq", perm_seq(lax.axis_size("seq"), mask))
    return (part.astype(f32) + got.astype(f32)).astype(bf16)


def sum_seq(part):
    for mask in seq_masks():
        part = sum_hop(part, mask)
    return part


def inv_rms(values):
    return lax.rsqrt(jnp.mean(values * values, axis=-1, keepdims=True) + epsilon)


def norm_back(values, inv, scaled):
    inner = jnp.mean(scaled * values, axis=-1, keepdims=True)
    return inv * scaled - values * (inv * inv * inv) * inner


def gelu_both(v):
    inner = jnp.tanh(gelu_scale * (v + 0.044715 * v * v * v))
    value = 0.5 * v * (1.0 + inner)
    slope = 0.5 * (1.0 + inner) + 0.5 * v * (1.0 - inner * inner) * gelu_scale * (
        1.0 + 3.0 * 0.044715 * v * v
    )
    return value, slope


def sigmoid(values):
    return 1.0 / (1.0 + jnp.exp(-values))


def dot(a, b):
    return lax.dot_general(a, b, (((1,), (0,)), ((), ())), preferred_element_type=f32)


def dot_nt(a, b):
    return lax.dot_general(a, b, (((1,), (1,)), ((), ())), preferred_element_type=f32)


def dot_tn(a, b):
    return lax.dot_general(a, b, (((0,), (0,)), ((), ())), preferred_element_type=f32)


def route_table(slots, count, token_pos):
    live = jnp.arange(slots.shape[0]) < count
    return ((slots[:, None] == token_pos[None, :]) & live[:, None]).astype(bf16)


def head_windows(width, head):
    found = []
    for low in range(0, width, head):
        first, last = low // LANES, (low + head - 1) // LANES
        found.append((first * LANES, (last + 1) * LANES, low - first * LANES))
    return found


def head_lanes(rows, low, high, offset, head):
    lane = lax.broadcasted_iota(jnp.int32, (rows, high - low), 1)
    return (lane >= offset) & (lane < offset + head)


def add_tiles(tiles, low, values):
    for t in range(values.shape[1] // LANES):
        part = values[:, t * LANES : (t + 1) * LANES]
        k = low // LANES + t
        tiles[k] = part if tiles[k] is None else tiles[k] + part


def attend(q, kv, q_seg, k_seg, head, block, reach, out_type):
    count, width = q.shape
    keys = kv.shape[0]
    span = block + 2 * reach if reach else keys
    windows = head_windows(width, head)
    scale = head ** (-0.5)

    def body(q_ref, kv_ref, q_seg_ref, k_seg_ref, out_ref, prob_ref):
        start = pl.multiple_of(pl.program_id(0) * block, block) if reach else 0
        rows = pl.ds(start, span)
        allowed = q_seg_ref[...] == k_seg_ref[:, rows]
        if reach:
            ahead = lax.broadcasted_iota(jnp.int32, (block, span), 1) - lax.broadcasted_iota(
                jnp.int32, (block, span), 0
            )
            allowed = allowed & (ahead >= 0) & (ahead <= 2 * reach)
        tiles = [None] * (width // LANES)
        for h, (low, high, offset) in enumerate(windows):
            mine = head_lanes(block, low, high, offset, head)
            q_head = jnp.where(mine, q_ref[:, low:high], 0)
            scores = dot_nt(q_head, kv_ref[rows, low:high]) * scale
            scores = jnp.where(allowed, scores, masked_score)
            raised = jnp.exp(scores - jnp.max(scores, axis=-1, keepdims=True))
            probs = (raised * (1.0 / jnp.sum(raised, axis=-1, keepdims=True))).astype(bf16)
            prob_ref[h] = probs
            mixed = dot(probs, kv_ref[rows, width + low : width + high])
            add_tiles(tiles, low, jnp.where(mine, mixed, 0.0))
        for t, tile in enumerate(tiles):
            out_ref[:, t * LANES : (t + 1) * LANES] = tile.astype(out_type)

    return pl.pallas_call(
        body,
        grid=(count // block,),
        in_specs=[
            pl.BlockSpec((block, width), lambda b: (b, 0)),
            pl.BlockSpec((keys, 2 * width), lambda b: (0, 0)),
            pl.BlockSpec((block, 1), lambda b: (b, 0)),
            pl.BlockSpec((1, keys), lambda b: (0, 0)),
        ],
        out_specs=[
            pl.BlockSpec((block, width), lambda b: (b, 0)),
            pl.BlockSpec((len(windows), block, span), lambda b: (0, b, 0)),
        ],
        out_shape=[
            jax.ShapeDtypeStruct((count, width), out_type),
            jax.ShapeDtypeStruct((len(windows), count, span), bf16),
        ],
        compiler_params=pltpu.CompilerParams(vmem_limit_bytes=32 * 2**20),
        cost_estimate=pl.CostEstimate(
            flops=4 * count * span * width,
            transcendentals=len(windows) * count * span,
            bytes_accessed=2 * (2 * count * width + 2 * keys * width + len(windows) * count * span),
        ),
    )(q, kv, q_seg[:, None], k_seg[None])


def attend_back(q, kv, probs, grad, head, block, reach):
    count, width = q.shape
    keys = kv.shape[0]
    span = block + 2 * reach if reach else keys
    windows = head_windows(width, head)
    scale = head ** (-0.5)

    def body(q_ref, kv_ref, prob_ref, grad_ref, q_grad_ref, kv_grad_ref, sums_ref):
        step = pl.program_id(0)

        @pl.when(step == 0)
        def _():
            sums_ref[...] = jnp.zeros_like(sums_ref)

        start = pl.multiple_of(step * block, block) if reach else 0
        rows = pl.ds(start, span)
        tiles = [None] * (width // LANES)
        for h, (low, high, offset) in enumerate(windows):
            mine = head_lanes(block, low, high, offset, head)
            q_head = jnp.where(mine, q_ref[:, low:high], 0)
            g_head = jnp.where(mine, grad_ref[:, low:high], 0)
            p_head = prob_ref[h]
            p_wide = p_head.astype(f32)
            p_grad = dot_nt(g_head, kv_ref[rows, width + low : width + high])
            inner = jnp.sum(p_wide * p_grad, axis=-1, keepdims=True)
            s_grad = (p_wide * (p_grad - inner)).astype(bf16)
            q_part = dot(s_grad, kv_ref[rows, low:high]) * scale
            add_tiles(tiles, low, jnp.where(mine, q_part, 0.0))
            sums_ref[rows, low:high] += dot_tn(s_grad, q_head) * scale
            sums_ref[rows, width + low : width + high] += dot_tn(p_head, g_head)
        for t, tile in enumerate(tiles):
            q_grad_ref[:, t * LANES : (t + 1) * LANES] = tile.astype(bf16)

        @pl.when(step == count // block - 1)
        def _():
            kv_grad_ref[...] = sums_ref[...].astype(bf16)

    return pl.pallas_call(
        body,
        grid=(count // block,),
        in_specs=[
            pl.BlockSpec((block, width), lambda b: (b, 0)),
            pl.BlockSpec((keys, 2 * width), lambda b: (0, 0)),
            pl.BlockSpec((len(windows), block, span), lambda b: (0, b, 0)),
            pl.BlockSpec((block, width), lambda b: (b, 0)),
        ],
        out_specs=[
            pl.BlockSpec((block, width), lambda b: (b, 0)),
            pl.BlockSpec((keys, 2 * width), lambda b: (0, 0)),
        ],
        out_shape=[
            jax.ShapeDtypeStruct((count, width), bf16),
            jax.ShapeDtypeStruct((keys, 2 * width), bf16),
        ],
        scratch_shapes=[pltpu.VMEM((keys, 2 * width), f32)],
        compiler_params=pltpu.CompilerParams(vmem_limit_bytes=40 * 2**20),
        cost_estimate=pl.CostEstimate(
            flops=8 * count * span * width,
            transcendentals=0,
            bytes_accessed=2 * (3 * count * width + 4 * keys * width + len(windows) * count * span),
        ),
    )(q, kv, probs, grad)


def shards(
    layer_input,
    cotangent,
    segment_ids,
    route_index,
    route_count,
    attn_gain,
    light_qkv,
    light_out,
    heavy_qkv,
    heavy_out,
    attn_router,
    ffn_gain,
    light_gate_up,
    light_down,
    heavy_gate_up,
    heavy_down,
    ffn_router,
):
    dp, seq = lax.axis_size("dp"), lax.axis_size("seq")
    pos = lax.axis_index("seq")
    x_in, cot, seg = layer_input[0], cotangent[0], segment_ids[0]
    tokens, width = x_in.shape
    slots, counts = route_index[0], route_count[0]
    routed = slots.shape[1]
    token_pos = pos * tokens + jnp.arange(tokens, dtype=jnp.int32)
    table_q = route_table(slots[0], counts[0], token_pos)
    table_kv = route_table(slots[1], counts[1], token_pos)
    table_f = route_table(slots[2], counts[2], token_pos)

    rows, wide = light_qkv.shape
    unit = heavy_down.shape[0]
    merged = lambda block: block.reshape(-1, block.shape[-1])
    hops = len(dp_stages(dp))

    small = jnp.stack([attn_gain, attn_router, ffn_gain, ffn_router], axis=1)
    first = jnp.concatenate([light_qkv, jnp.pad(small, ((0, 0), (0, LANES - 4)))], axis=1)
    got_first = send_seq(lambda k: first)
    marked = jnp.concatenate(
        [x_in, jnp.broadcast_to(seg.astype(bf16)[:, None], (tokens, LANES))], axis=1
    )
    left = lax.ppermute(marked[tokens - WINDOW :], "seq", [(i, i + 1) for i in range(seq - 1)])
    right = lax.ppermute(marked[:WINDOW], "seq", [(i + 1, i) for i in range(seq - 1)])
    kv_part = dot(table_kv, marked).astype(bf16)
    cot_part = dot(table_f, cot).astype(bf16)
    second = jnp.concatenate([heavy_qkv, light_out, heavy_out], axis=1)
    kv_part, cot_part, second, *got_first = fence(kv_part, cot_part, second, *got_first)

    first_held = {(): merged(place_seq([first] + got_first))}
    wave(first_held, 0)
    got_second = send_seq(lambda k: second)
    seq_left = seq_masks()
    kv_part = sum_hop(kv_part, seq_left.pop(0))
    for h in range(1, hops):
        fence_pieces([(first_held, arrived(first_held, h))])
        wave(first_held, h)
    w_lqkv, small_all = place_dp(first_held, [wide, LANES])

    small_t = small_all[:, :4].T
    gain_attn = small_t[0].astype(f32)[None]
    router_attn = small_t[1][None]
    gain_ffn = small_t[2].astype(f32)[None]
    router_ffn = small_t[3][None]

    ext_marked = jnp.concatenate([left, marked, right], axis=0)
    ext_in = ext_marked[:, :width].astype(f32)
    ext_inv = inv_rms(ext_in)
    normed_ext = (ext_in * ext_inv * gain_attn).astype(bf16)
    normed = normed_ext[WINDOW : WINDOW + tokens]
    place = jnp.arange(tokens + 2 * WINDOW) - WINDOW
    outside = ((pos == 0) & (place < 0)) | ((pos == seq - 1) & (place >= tokens))
    key_seg = jnp.where(outside, -1.0, ext_marked[:, width].astype(f32))
    seg_f = seg.astype(f32)
    light_q = dot(normed, w_lqkv[:, :width]).astype(bf16)
    light_kv = dot(normed_ext, w_lqkv[:, width:]).astype(bf16)
    z_second = merged(place_seq([second] + got_second))
    light_q, light_kv, kv_part, z_second = fence(light_q, light_kv, kv_part, z_second)
    second_held = {(): z_second}
    wave(second_held, 0)
    for mask in seq_left:
        kv_part = sum_hop(kv_part, mask)
    light_mixed, light_probs = attend(
        light_q, light_kv, seg_f, key_seg, L_HEAD, WINDOW, WINDOW, bf16
    )
    q_rows = dot(table_q, normed).astype(bf16)
    q_seg = jnp.sum(table_q.astype(f32) * seg_f[None], axis=1)
    columns = heavy_gate_up.reshape(rows, 2 * dp, seq, unit)
    light_mixed, q_rows, kv_marked, gate_up, columns, down = fence_pieces(
        [(second_held, arrived(second_held, 1))],
        light_mixed, q_rows, kv_part, light_gate_up, columns, light_down
    )

    for h in range(1, hops):
        wave(second_held, h)

    def gate_up_for(k):
        own = lax.dynamic_index_in_dim(columns, pos ^ k, 2, keepdims=False)
        return jnp.concatenate([gate_up, own.reshape(rows, -1)], axis=1)

    got_gate_up = send_seq(gate_up_for)
    got_down = send_seq(lambda k: down)
    w_hqkv, w_lout, w_hout = place_dp(second_held, [wide, width, width])

    kv_in = kv_marked[:, :width].astype(f32)
    kv_inv = inv_rms(kv_in)
    kv_rows = (kv_in * kv_inv * gain_attn).astype(bf16)
    kv_seg = jnp.where(jnp.arange(routed) < counts[1], kv_marked[:, width].astype(f32), -1.0)
    heavy_q = dot(q_rows, w_hqkv[:, :width]).astype(bf16)
    heavy_kv = dot(kv_rows, w_hqkv[:, width:]).astype(bf16)
    heavy_mixed, heavy_probs = attend(
        heavy_q, heavy_kv, q_seg, kv_seg, H_HEAD, min(routed, 256), 0, f32
    )
    gate = sigmoid(
        jnp.sum(q_rows.astype(f32) * router_attn.astype(f32), axis=1, keepdims=True)
    )
    gated = (gate * heavy_mixed).astype(bf16)
    heavy_rows = dot(gated, w_hout).astype(bf16)
    midway = x_in.astype(f32) + dot(light_mixed, w_lout) + dot_tn(table_q, heavy_rows)

    inv_ffn = inv_rms(midway)
    normed_ffn = (midway * inv_ffn * gain_ffn).astype(bf16)
    rows_part = dot(table_f, normed_ffn).astype(bf16)
    rows_part, normed_ffn, cot_part, *got = fence(
        rows_part, normed_ffn, cot_part, *got_gate_up, *got_down
    )
    got_gate_up, got_down = got[: seq - 1], got[seq - 1 :]
    gate_up_held = {(): merged(place_seq([gate_up_for(0)] + got_gate_up))}
    z_down = merged(place_seq([down] + got_down))
    if z_down.shape == heavy_down.shape:
        down_held = [{(): jnp.concatenate([z_down, heavy_down], axis=1)}]
    else:
        down_held = [{(): z_down}, {(): heavy_down}]
    ffn_held = [gate_up_held] + down_held
    for held in ffn_held:
        wave(held, 0)
    seq_left = seq_masks()
    rows_part = sum_hop(rows_part, seq_left.pop(0))
    rows_part, normed_ffn, cot_part = fence_pieces(
        [(held, arrived(held, 1)) for held in ffn_held], rows_part, normed_ffn, cot_part
    )
    for h in range(1, hops):
        for held in ffn_held:
            wave(held, h)
    for mask in seq_left:
        rows_part = sum_hop(rows_part, mask)
    w_lgu, w_hgu = place_dp(gate_up_held, [light_gate_up.shape[1], 2 * dp * unit])
    w_ldown, w_hdown = sum(
        [place_dp(held, [width] * (2 // len(down_held))) for held in down_held], []
    )
    ffn_rows, cot_part, normed_ffn = fence(rows_part, cot_part, normed_ffn)
    cot_rows = sum_seq(cot_part)

    by_dp = lambda grad: grad.reshape(dp, -1, grad.shape[1])
    light_units = w_ldown.shape[0]
    light_pre = dot(normed_ffn, w_lgu)
    light_gate, light_up = light_pre[:, :light_units], light_pre[:, light_units:]
    light_act, light_slope = gelu_both(light_gate)
    light_hidden = (light_act * light_up).astype(bf16)
    light_ffn = dot(light_hidden, w_ldown)
    grad_ldown = dot_tn(light_hidden, cot).astype(bf16)
    hidden_grad = dot_nt(cot, w_ldown).astype(bf16).astype(f32)
    light_pre_grad = jnp.concatenate(
        [hidden_grad * light_up * light_slope, hidden_grad * light_act], axis=-1
    ).astype(bf16)
    grad_lgu = dot_tn(normed_ffn, light_pre_grad).astype(bf16)
    normed_ffn_grad = dot_nt(light_pre_grad, w_lgu)
    ffn_rows, cot_rows, normed_ffn_grad, grad_ldown, grad_lgu = fence(
        ffn_rows, cot_rows, normed_ffn_grad, grad_ldown, grad_lgu
    )

    sum_light = [scatter_dp([by_dp(grad_lgu)]), scatter_dp([by_dp(grad_ldown)])]
    heavy_units = w_hdown.shape[0]
    heavy_pre = dot(ffn_rows, w_hgu)
    heavy_gate, heavy_up = heavy_pre[:, :heavy_units], heavy_pre[:, heavy_units:]
    heavy_act, heavy_slope = gelu_both(heavy_gate)
    ffn_gate = sigmoid(
        jnp.sum(ffn_rows.astype(f32) * router_ffn.astype(f32), axis=1, keepdims=True)
    )
    heavy_hidden = (ffn_gate * heavy_act * heavy_up).astype(bf16)
    heavy_grad = dot_nt(cot_rows, w_hdown).astype(bf16).astype(f32)
    heavy_pre_grad = jnp.concatenate(
        [heavy_grad * ffn_gate * heavy_up * heavy_slope, heavy_grad * ffn_gate * heavy_act],
        axis=-1,
    ).astype(bf16)
    ffn_score_grad = (
        ffn_gate
        * (1.0 - ffn_gate)
        * jnp.sum(heavy_grad * heavy_act * heavy_up, axis=1, keepdims=True)
    )
    rows_grad_part = dot_nt(heavy_pre_grad, w_hgu) + ffn_score_grad * router_ffn.astype(f32)
    rows_grad = rows_grad_part.astype(bf16)
    rows_grad, heavy_hidden, heavy_pre_grad, ffn_score_grad = fence_sums(
        sum_light, rows_grad, heavy_hidden, heavy_pre_grad, ffn_score_grad
    )
    seq_left = seq_masks()
    rows_grad = sum_hop(rows_grad, seq_left.pop(0))
    for s in sum_light:
        s.step()
    grad_ffn_router = jnp.sum(ffn_rows.astype(f32) * ffn_score_grad, axis=0)
    grad_hdown = dot_tn(heavy_hidden, cot_rows).astype(bf16)
    grad_hgu = dot_tn(ffn_rows, heavy_pre_grad).astype(bf16)
    out_part = dot(heavy_hidden, w_hdown).astype(bf16)
    rows_grad, grad_hdown, grad_hgu, out_part = fence_sums(
        sum_light, rows_grad, grad_hdown, grad_hgu, out_part
    )
    for mask in seq_left:
        rows_grad = sum_hop(rows_grad, mask)
    for s in sum_light:
        s.step()
    sum_heavy = [scatter_dp([by_dp(grad_hgu)]), scatter_dp([by_dp(grad_hdown)])]
    rows_grad, out_part = fence_sums(sum_light + sum_heavy, rows_grad, out_part)

    for s in sum_heavy:
        s.step()
    out_left = seq_masks()
    out_part = sum_hop(out_part, out_left.pop(0))
    lgu_mine = sum_light[0].finish().reshape(seq, rows, -1)
    ldown_mine = sum_light[1].finish().reshape(seq, -1, width)
    normed_ffn_grad = normed_ffn_grad + dot_tn(table_f, rows_grad)
    grad_ffn_gain = jnp.sum(normed_ffn_grad * midway * inv_ffn, axis=0)
    midway_grad = cot.astype(f32) + norm_back(midway, inv_ffn, normed_ffn_grad * gain_ffn)

    out_grad = midway_grad.astype(bf16)
    grad_lout = dot_tn(light_mixed, out_grad).astype(bf16)
    heavy_out_cot = dot(table_q, out_grad).astype(bf16)
    grad_hout = dot_tn(gated, heavy_out_cot).astype(bf16)
    gated_grad = dot_nt(heavy_out_cot, w_hout).astype(bf16).astype(f32)
    heavy_mixed_grad = (gate * gated_grad).astype(bf16)
    attn_score_grad = gate * (1.0 - gate) * jnp.sum(gated_grad * heavy_mixed, axis=1, keepdims=True)
    heavy_q_grad, heavy_kv_grad = attend_back(
        heavy_q, heavy_kv, heavy_probs, heavy_mixed_grad, H_HEAD, min(routed, 256), 0
    )
    grad_hq = dot_tn(q_rows, heavy_q_grad).astype(bf16)
    grad_hkv = dot_tn(kv_rows, heavy_kv_grad).astype(bf16)
    grad_attn_router = jnp.sum(q_rows.astype(f32) * attn_score_grad, axis=0)
    q_rows_grad = (
        dot_nt(heavy_q_grad, w_hqkv[:, :width]) + attn_score_grad * router_attn.astype(f32)
    ).astype(bf16)
    kv_rows_grad = dot_nt(heavy_kv_grad, w_hqkv[:, width:])
    mixed_grad = dot_nt(out_grad, w_lout).astype(bf16)
    mixed_grad, kv_send, out_part, lgu_mine, ldown_mine, *attn_grads = fence_sums(
        sum_heavy,
        mixed_grad,
        kv_rows_grad.astype(bf16),
        out_part,
        lgu_mine,
        ldown_mine,
        *[by_dp(g) for g in (grad_hq, grad_hkv, grad_lout, grad_hout)],
    )

    for s in sum_heavy:
        s.step()
    sum_attn = scatter_dp(attn_grads)
    for mask in out_left:
        out_part = sum_hop(out_part, mask)
    kv_left = seq_masks()
    kv_send = sum_hop(kv_send, kv_left.pop(0))
    light_q_grad, light_kv_grad = attend_back(
        light_q, light_kv, light_probs, mixed_grad, L_HEAD, WINDOW, WINDOW
    )
    light_q_grad, light_kv_grad, kv_send, out_part, lgu_mine, ldown_mine = fence_sums(
        sum_heavy + [sum_attn], light_q_grad, light_kv_grad, kv_send, out_part, lgu_mine, ldown_mine
    )
    sum_attn.step()
    for mask in kv_left:
        kv_send = sum_hop(kv_send, mask)
    out_light_down = scatter_seq(ldown_mine)
    hgu_mine = sum_heavy[0].finish().reshape(seq, rows, -1)
    out_heavy_down = sum_heavy[1].finish()
    ext_grad = dot_nt(light_kv_grad, w_lqkv[:, width:])

    own_grad = (
        ext_grad[WINDOW : WINDOW + tokens]
        + dot_nt(light_q_grad, w_lqkv[:, :width])
        + dot_tn(table_q, q_rows_grad)
    )
    grad_attn_gain = (
        jnp.sum(own_grad * (ext_in * ext_inv)[WINDOW : WINDOW + tokens], axis=0)
        + jnp.sum(ext_grad[:WINDOW] * (ext_in * ext_inv)[:WINDOW], axis=0)
        + jnp.sum(ext_grad[WINDOW + tokens :] * (ext_in * ext_inv)[WINDOW + tokens :], axis=0)
        + jnp.sum(kv_rows_grad * (kv_in * kv_inv), axis=0)
    )
    small_grads = jnp.stack([grad_attn_gain, grad_attn_router, grad_ffn_gain, grad_ffn_router], 1)
    grad_lqkv = [
        dot_tn(normed, light_q_grad).astype(bf16),
        dot_tn(normed_ext, light_kv_grad).astype(bf16),
        jnp.pad(small_grads, ((0, 0), (0, LANES - 4))).astype(bf16),
    ]
    *grad_lqkv, hgu_mine, lgu_mine, out_light_down = fence_sums(
        [sum_attn], *[by_dp(g) for g in grad_lqkv], hgu_mine, lgu_mine, out_light_down
    )
    sum_last = scatter_dp(grad_lqkv)
    both = jnp.concatenate([lgu_mine.astype(bf16), hgu_mine.astype(bf16)], axis=2)
    pick = lambda k: lax.dynamic_index_in_dim(both, pos ^ k, 0, keepdims=False)
    got = [pick(0)] + send_seq(pick)
    from_right = lax.ppermute(
        ext_grad[WINDOW + tokens :].astype(bf16), "seq", [(i, i + 1) for i in range(seq - 1)]
    )
    from_left = lax.ppermute(
        ext_grad[:WINDOW].astype(bf16), "seq", [(i + 1, i) for i in range(seq - 1)]
    )
    sum_last.step()
    attn_mine = sum_attn.finish().reshape(seq, rows, -1)
    attn_mine, kv_total, *got = fence_sums([sum_last], attn_mine, kv_send, *got)
    sum_last.step()
    heavy_outs = scatter_seq(attn_mine)
    light_cut = light_gate_up.shape[1]
    out_light_gate_up = sum(g[:, :light_cut].astype(f32) for g in got)
    slices = place_seq(got)[:, :, light_cut:].reshape(seq, rows, 2 * dp, unit)
    out_heavy_gate_up = slices.transpose(1, 2, 0, 3).astype(f32).reshape(rows, -1)
    layer_output = (midway + light_ffn + dot_tn(table_f, out_part)).astype(bf16)
    light_outs = scatter_seq(sum_last.finish().reshape(seq, rows, -1))
    out_small = light_outs[:, wide : wide + 4].T
    edge = jnp.concatenate(
        [from_right.astype(f32), jnp.zeros((tokens - 2 * WINDOW, width), f32), from_left.astype(f32)]
    )
    total_grad = own_grad + edge + dot_tn(table_kv, kv_total)
    x_wide = x_in.astype(f32)
    input_grad = midway_grad + norm_back(
        x_wide, ext_inv[WINDOW : WINDOW + tokens], total_grad * gain_attn
    )

    return (
        layer_output[None],
        input_grad.astype(bf16)[None],
        out_small[0],
        light_outs[:, :wide],
        heavy_outs[:, wide : wide + width],
        heavy_outs[:, :wide],
        heavy_outs[:, wide + width :],
        out_small[1],
        out_small[2],
        out_light_gate_up,
        out_light_down,
        out_heavy_gate_up,
        out_heavy_down,
        out_small[3],
    )


def solution(mesh):
    both = ("dp", "seq")
    vector, matrix, tokens = P(both), P(both, None), P("dp", "seq", None)
    return jax.shard_map(
        shards,
        mesh=mesh,
        in_specs=(
            tokens,
            tokens,
            P("dp", "seq"),
            P("dp", None, None),
            P("dp", None),
            vector,
            matrix,
            matrix,
            matrix,
            matrix,
            vector,
            vector,
            matrix,
            matrix,
            matrix,
            matrix,
            vector,
        ),
        out_specs=(
            tokens,
            tokens,
            vector,
            matrix,
            matrix,
            matrix,
            matrix,
            vector,
            vector,
            matrix,
            matrix,
            matrix,
            matrix,
            vector,
        ),
        check_vma=False,
    )
```

time: 574 us -> 482 us (0.84)
  matrix products: 102 us -> 54.3 us
  starting transfers between devices: 126 us -> 98.9 us
  Pallas kernels: 41.3 us -> 59 us
  local copies, waits for them, and re-layouts: 57.8 us -> 43.1 us
  waiting for transfers between devices: 181 us -> 169 us
  other arithmetic: 53.1 us -> 45.3 us
    dot_general x12 -> x0, matrix products: 40.9 us -> none  [the longest x2 11.8 us: attend_back(): grad_probs = jnp.einsum('qhe,khe->hqk', hg, hv, preferred_element_type=f32)]
    pallas_call x0 -> x4, Pallas kernels: none -> 31 us  [the longest x2 18.4 us: attend_back(): pl.pallas_call(body, grid=(count // block,), in_specs=[pl.BlockSpec((bloc...]
    ppermute x118 -> x82, starting transfers between devices: 116 us -> 87.2 us  [the longest x15 26.8 us: send_seq(): lax.ppermute(piece_for(k), 'seq', perm_seq(count, k))]
    pallas_call x21 -> x15, Pallas kernels: 41.3 us -> 28 us  [dma_moves(): pl.pallas_call(body, out_shape=[jax.ShapeDtypeStruct(s, a) for s, a in ou...]
    another operation x18 -> x2, other arithmetic: 13.3 us -> 1.05 us
    slice x23 -> x5, local copies, waits for them, and re-layouts: 14.4 us -> 4.14 us  [the longest x2 2.07 us: shards(): table_q = route_table(slots[0], counts[0], token_pos)]
    ppermute x118 -> x82, waiting for transfers between devices: 177 us -> 169 us  [the longest x12 81.9 us: sum_hop(): got = lax.ppermute(part, 'seq', perm_seq(lax.axis_size('seq'), mask))]
    add x12 -> x10, other arithmetic: 2.64 us -> 9.22 us  [the longest x6 5.45 us: finish(): return self.keep[0].astype(f32) + self.got[0].astype(f32)]
  transfers between devices with their start and end apart: 122 -> 86, of which waited for: 41 -> 28; matrix products, arithmetic and copies ran while one was open for 34% -> 16% of each run, Pallas kernels for 7% -> 9%
where the time goes in v2:
time: 482 us; the launch traced here: 473 us
  waiting for transfers between devices  169 us (35%)
  starting transfers between devices  98.9 us (21%)
  Pallas kernels  59 us (12%)
  matrix products  54.3 us (11%)
  other arithmetic  45.3 us (9%)
  local copies, waits for them, and re-layouts  43.1 us (9%)
    ppermute x12, waiting for transfers between devices, sum_hop(): got = lax.ppermute(part, 'seq', perm_seq(lax.axis_size('seq'), mask))  81.9 us
    pallas_call x15, Pallas kernels, dma_moves(): pl.pallas_call(body, out_shape=[jax.ShapeDtypeStruct(s, a) for s, a in ou...  28 us
    ppermute x15, starting transfers between devices, send_seq(): lax.ppermute(piece_for(k), 'seq', perm_seq(count, k))  26.8 us
    ppermute x15, waiting for transfers between devices, send_seq(): lax.ppermute(piece_for(k), 'seq', perm_seq(count, k))  25.3 us
    ppermute x28, waiting for transfers between devices, wave(): lax.ppermute(pieces[label], 'dp', perm(count, stages[stage]))  23.7 us
    ppermute x18, waiting for transfers between devices, hop(): self.got = lax.ppermute(send, 'dp', perm(count, self.left.pop()))  23.1 us
    unnamed x271, local copies, waits for them, and re-layouts  22.9 us
    dot_general x15, matrix products, dot_tn(): lax.dot_general(a, b, (((0,), (0,)), ((), ())), preferred_element_type=f32)  22.1 us
  transfers between devices with their start and end apart: 86, of which 28 were waited for; matrix products, arithmetic and copies ran while one was open for 16% of the time, Pallas kernels for 9%

profile of v2, /device:TPU:0, one launch (start us, length us, event | category | flops | bytes accessed | tf_op | source)
XLA Modules:
  0.0 473.3 jit_solution(5944135912144919719)
XLA Ops:
  23.7 4.6 collective-permute-start
  39.8 4.4 collective-permute-done.13.refs_1_
  44.3 6.8 %collective-permute-done.14.refs_2_ = bf16[24,3840]{1,0:T(8,128)(2,1)S(1)} collective-permute-done((bf16[24,3840]{1,0:T(8,128)(2,1)S(1)}, bf16[24,3840]{1,0:T(8,128)(2,1)S(1)}, u32[]{:S(2)}, u32[]{:S(2)}) %collective-permute-start.14) | collective-permute-done | bytes 184352 | tf_op jit(solution)/shard_map/ppermute | solution.py:97
  78.5 10.6 %shard_map.275 = (bf16[512,768]{1,0:T(8,128)(2,1)S(1)}, bf16[8,512,384]{2,1,0:T(8,128)(2,1)S(1)}) custom-call(bf16[512,768]{1,0:T(8,128)(2,1)S(1)} %convolution_convert_fusion.14.q_ref, bf16[768,1536]{1,0:T(8,128)(2,1)S(1)} %convolution_convert_fusion.4.kv_ref, f32[512,1]{1,0:T(8,128)S(1)} %copy.68.q_seg_ref, f32[1,768]{1,0:T(1,128)S(1)} %or_select_fusion.k_seg_ref), custom_call_target="tpu_custom_call" | custom-call | flops 603979776 | bytes 7077888 | tf_op jit(solution)/shard_map/pallas_call | solution.py:315
  97.4 7.7 %collective-permute-done.19.refs_3_ = bf16[96,3840]{1,0:T(8,128)(2,1)S(1)} collective-permute-done((bf16[96,3840]{1,0:T(8,128)(2,1)}, bf16[96,3840]{1,0:T(8,128)(2,1)S(1)}, u32[]{:S(2)}, u32[]{:S(2)}) %collective-permute-start.19) | collective-permute-done | bytes 737312 | tf_op jit(solution)/shard_map/ppermute | solution.py:105
  132.7 5.5 %collective-permute-done.26.refs_3_ = bf16[24,4096]{1,0:T(8,128)(2,1)S(1)} collective-permute-done((bf16[24,4096]{1,0:T(8,128)(2,1)S(1)}, bf16[24,4096]{1,0:T(8,128)(2,1)S(1)}, u32[]{:S(2)}, u32[]{:S(2)}) %collective-permute-start.26) | collective-permute-done | bytes 196640 | tf_op jit(solution)/shard_map/ppermute | solution.py:97
  149.9 5.7 %collective-permute-done.30 = bf16[256,768]{1,0:T(8,128)(2,1)S(1)} collective-permute-done((bf16[256,768]{1,0:T(8,128)(2,1)S(1)}, bf16[256,768]{1,0:T(8,128)(2,1)S(1)}, u32[]{:S(2)}, u32[]{:S(2)}) %collective-permute-start.30) | collective-permute-done | bytes 393248 | tf_op jit(solution)/shard_map/ppermute | solution.py:216
  155.7 12.5 %collective-permute-done.33.refs_1_ = bf16[128,1536]{1,0:T(8,128)(2,1)S(1)} collective-permute-done((bf16[128,1536]{1,0:T(8,128)(2,1)S(1)}, bf16[128,1536]{1,0:T(8,128)(2,1)S(1)}, u32[]{:S(2)}, u32[]{:S(2)}) %collective-permute-start.33) | collective-permute-done | bytes 393248 | tf_op jit(solution)/shard_map/ppermute | solution.py:105
  174.5 14.5 %collective-permute-done.35 = bf16[256,768]{1,0:T(8,128)(2,1)S(1)} collective-permute-done((bf16[256,768]{1,0:T(8,128)(2,1)S(1)}, bf16[256,768]{1,0:T(8,128)(2,1)S(1)}, u32[]{:S(2)}, u32[]{:S(2)}) %collective-permute-start.35) | collective-permute-done | bytes 393248 | tf_op jit(solution)/shard_map/ppermute | solution.py:216
  191.2 9.5 %collective-permute-done.46 = bf16[256,768]{1,0:T(8,128)(2,1)S(1)} collective-permute-done((bf16[256,768]{1,0:T(8,128)(2,1)S(1)}, bf16[256,768]{1,0:T(8,128)(2,1)S(1)}, u32[]{:S(2)}, u32[]{:S(2)}) %collective-permute-start.46) | collective-permute-done | bytes 393248 | tf_op jit(solution)/shard_map/ppermute | solution.py:216
  204.3 17.5 %collective-permute-done.47 = bf16[256,768]{1,0:T(8,128)(2,1)S(1)} collective-permute-done((bf16[256,768]{1,0:T(8,128)(2,1)S(1)}, bf16[256,768]{1,0:T(8,128)(2,1)S(1)}, u32[]{:S(2)}, u32[]{:S(2)}) %collective-permute-start.47) | collective-permute-done | bytes 393248 | tf_op jit(solution)/shard_map/ppermute | solution.py:216
  248.7 4.6 collective-permute-done.50
  253.4 7.9 %collective-permute-done.52 = bf16[2,128,768]{2,1,0:T(8,128)(2,1)S(1)} collective-permute-done((bf16[2,128,768]{2,1,0:T(8,128)(2,1)S(1)}, bf16[2,128,768]{2,1,0:T(8,128)(2,1)S(1)}, u32[]{:S(2)}, u32[]{:S(2)}) %collective-permute-start.52) | collective-permute-done | bytes 393248 | tf_op jit(solution)/shard_map/ppermute | solution.py:179
  272.3 12.7 %collective-permute-done.53 = bf16[256,768]{1,0:T(8,128)(2,1)S(1)} collective-permute-done((bf16[256,768]{1,0:T(8,128)(2,1)S(1)}, bf16[256,768]{1,0:T(8,128)(2,1)S(1)}, u32[]{:S(2)}, u32[]{:S(2)}) %collective-permute-start.53) | collective-permute-done | bytes 393248 | tf_op jit(solution)/shard_map/ppermute | solution.py:216
  293.9 4.7 shard_map.286
  308.6 5.7 %collective-permute-done.58 = bf16[256,768]{1,0:T(8,128)(2,1)S(1)} collective-permute-done((bf16[256,768]{1,0:T(8,128)(2,1)S(1)}, bf16[256,768]{1,0:T(8,128)(2,1)S(1)}, u32[]{:S(2)}, u32[]{:S(2)}) %collective-permute-start.58) | collective-permute-done | bytes 393248 | tf_op jit(solution)/shard_map/ppermute | solution.py:216
  314.4 7.4 %collective-permute-done.60 = bf16[2,128,768]{2,1,0:T(8,128)(2,1)S(1)} collective-permute-done((bf16[2,128,768]{2,1,0:T(8,128)(2,1)S(1)}, bf16[2,128,768]{2,1,0:T(8,128)(2,1)S(1)}, u32[]{:S(2)}, u32[]{:S(2)}) %collective-permute-start.60) | collective-permute-done | bytes 393248 | tf_op jit(solution)/shard_map/ppermute | solution.py:179
  333.5 13.7 %shard_map.287 = (bf16[512,768]{1,0:T(8,128)(2,1)S(1)}, bf16[768,1536]{1,0:T(8,128)(2,1)S(1)}) custom-call(bf16[512,768]{1,0:T(8,128)(2,1)S(1)} %copy-done.5, bf16[768,1536]{1,0:T(8,128)(2,1)S(1)} %convolution_convert_fusion.4.kv_ref, bf16[8,512,384]{2,1,0:T(8,128)(2,1)S(1)} %copy-done.3, bf16[512,768]{1,0:T(8,128)(2,1)S(1)} %convolution_convert_fusion.13.grad_ref), custom_call_target="tpu_custom_call" | custom-call | flops 1207959552 | bytes 10223616 | tf_op jit(solution)/shard_map/pallas_call | solution.py:378
  372.6 5.1 %add_convert_fusion = (bf16[2,96,3840]{2,1,0:T(8,128)(2,1)}, bf16[2,96,3840]{2,1,0:T(8,128)(2,1)}) fusion(bf16[4,96,3840]{2,1,0:T(8,128)(2,1)} %copy-done.47, bf16[4,96,3840]{2,1,0:T(8,128)(2,1)} %copy-done.8), kind=kLoop, calls=%fused_computation.7 | loop fusion | flops 5898240 | bytes 8847360 | tf_op jit(solution)/shard_map/convert_element_type | solution.py:184
  387.8 4.6 collective-permute-start.66
  400.0 5.2 %collective-permute-done.73 = bf16[256,768]{1,0:T(8,128)(2,1)S(1)} collective-permute-done((bf16[256,768]{1,0:T(8,128)(2,1)}, bf16[256,768]{1,0:T(8,128)(2,1)S(1)}, u32[]{:S(2)}, u32[]{:S(2)}) %collective-permute-start.73) | collective-permute-done | bytes 393248 | tf_op jit(solution)/shard_map/ppermute | solution.py:216
  407.1 4.9 %collective-permute-start.74 = (bf16[24,4096]{1,0:T(8,128)(2,1)S(1)}, bf16[24,4096]{1,0:T(8,128)(2,1)S(1)}, u32[]{:S(2)}, u32[]{:S(2)}) collective-permute-start(bf16[24,4096]{1,0:T(8,128)(2,1)S(1)} %get-tuple-element.303), channel_id=1, source_target_pairs={{0,1},{1,0},{2,3},{3,2},{4,5},{5,4},{6,7},{7,6},{8,9},{9,8},{10,11... | collective-permute-start | bytes 589832 | tf_op jit(solution)/shard_map/ppermute | solution.py:97
  421.1 8.1 %collective-permute-done.75.refs_2_ = bf16[24,4096]{1,0:T(8,128)(2,1)S(1)} collective-permute-done((bf16[24,4096]{1,0:T(8,128)(2,1)S(1)}, bf16[24,4096]{1,0:T(8,128)(2,1)S(1)}, u32[]{:S(2)}, u32[]{:S(2)}) %collective-permute-start.75) | collective-permute-done | bytes 196640 | tf_op jit(solution)/shard_map/ppermute | solution.py:97
  447.7 8.2 %collective-permute-done.84 = bf16[24,3840]{1,0:T(8,128)(2,1)} collective-permute-done((bf16[24,3840]{1,0:T(8,128)(2,1)}, bf16[24,3840]{1,0:T(8,128)(2,1)}, u32[]{:S(2)}, u32[]{:S(2)}) %collective-permute-start.84) | collective-permute-done | bytes 184352 | tf_op jit(solution)/shard_map/ppermute | solution.py:207
  (593 shorter events, 277.7 us)
Async XLA Ops:
  69.0 24.3 %collective-permute-start.17 = (bf16[96,3840]{1,0:T(8,128)(2,1)}, bf16[96,3840]{1,0:T(8,128)(2,1)}, u32[]{:S(2)}, u32[]{:S(2)}) collective-permute-start(bf16[96,3840]{1,0:T(8,128)(2,1)} %bitcast.26.refs_0_), channel_id=1, source_target_pairs={{0,8},{4,20},{8,0},{12,28},{16,24},{20,4},{24,16},{28,12},{1,9},{5... | collective-permute-start | bytes 2211848 | tf_op jit(solution)/shard_map/ppermute | solution.py:105
  69.6 23.7 %collective-permute-start.18 = (bf16[96,3840]{1,0:T(8,128)(2,1)}, bf16[96,3840]{1,0:T(8,128)(2,1)}, u32[]{:S(2)}, u32[]{:S(2)}) collective-permute-start(bf16[96,3840]{1,0:T(8,128)(2,1)} %bitcast.26.refs_0_), channel_id=1, source_target_pairs={{0,16},{4,12},{8,24},{12,4},{16,0},{20,28},{24,8},{28,20},{1,17},{... | collective-permute-start | bytes 2211848 | tf_op jit(solution)/shard_map/ppermute | solution.py:105
  69.6 22.4 %collective-permute-start.16 = (bf16[256,896]{1,0:T(8,128)(2,1)}, bf16[256,896]{1,0:T(8,128)(2,1)}, u32[]{:S(2)}, u32[]{:S(2)}) collective-permute-start(bf16[256,896]{1,0:T(8,128)(2,1)} %add_convert_fusion.14), channel_id=1, source_target_pairs={{0,2},{1,3},{2,0},{3,1},{4,6},{5,7},{6,4},{7,5},{8,10},{9,11},{10,... | collective-permute-start | bytes 1376264 | tf_op jit(solution)/shard_map/ppermute | solution.py:216
  78.4 28.7 %collective-permute-start.20 = (bf16[96,3840]{1,0:T(8,128)(2,1)}, bf16[96,3840]{1,0:T(8,128)(2,1)S(1)}, u32[]{:S(2)}, u32[]{:S(2)}) collective-permute-start(bf16[96,3840]{1,0:T(8,128)(2,1)} %bitcast.26.refs_0_), channel_id=1, source_target_pairs={{0,4},{4,0},{8,12},{12,8},{16,20},{20,16},{24,28},{28,24},{1,5},{5... | collective-permute-start | bytes 2211848 | tf_op jit(solution)/shard_map/ppermute | solution.py:105
  95.7 33.5 %collective-permute-start.27 = (bf16[32,768]{1,0:T(8,128)(2,1)}, bf16[32,768]{1,0:T(8,128)(2,1)}, u32[]{:S(2)}, u32[]{:S(2)}) collective-permute-start(bf16[32,768]{1,0:T(8,128)(2,1)} %refs_0_), channel_id=1, source_target_pairs={{0,1},{1,0},{2,3},{3,2},{4,5},{5,4},{6,7},{7,6},{8,9},{9,8},{10,11... | collective-permute-start | bytes 147464 | tf_op jit(solution)/shard_map/ppermute | solution.py:97
  107.1 25.5 %collective-permute-start.28 = (bf16[32,768]{1,0:T(8,128)(2,1)}, bf16[32,768]{1,0:T(8,128)(2,1)}, u32[]{:S(2)}, u32[]{:S(2)}) collective-permute-start(bf16[32,768]{1,0:T(8,128)(2,1)} %refs_0_), channel_id=1, source_target_pairs={{0,2},{1,3},{2,0},{3,1},{4,6},{5,7},{6,4},{7,5},{8,10},{9,11},{10,... | collective-permute-start | bytes 147464 | tf_op jit(solution)/shard_map/ppermute | solution.py:97
  107.1 25.5 %collective-permute-start.29 = (bf16[32,768]{1,0:T(8,128)(2,1)}, bf16[32,768]{1,0:T(8,128)(2,1)}, u32[]{:S(2)}, u32[]{:S(2)}) collective-permute-start(bf16[32,768]{1,0:T(8,128)(2,1)} %refs_0_), channel_id=1, source_target_pairs={{0,3},{1,2},{2,1},{3,0},{4,7},{5,6},{6,5},{7,4},{8,11},{9,10},{10,... | collective-permute-start | bytes 147464 | tf_op jit(solution)/shard_map/ppermute | solution.py:97
  110.7 22.0 %collective-permute-start.24 = (bf16[24,4096]{1,0:T(8,128)(2,1)}, bf16[24,4096]{1,0:T(8,128)(2,1)S(1)}, u32[]{:S(2)}, u32[]{:S(2)}) collective-permute-start(bf16[24,4096]{1,0:T(8,128)(2,1)} %get-tuple-element.328), channel_id=1, source_target_pairs={{0,1},{1,0},{2,3},{3,2},{4,5},{5,4},{6,7},{7,6},{8,9},{9,8},{10,11... | collective-permute-start | bytes 589832 | tf_op jit(solution)/shard_map/ppermute | solution.py:97
  111.3 21.4 %collective-permute-start.25 = (bf16[24,4096]{1,0:T(8,128)(2,1)}, bf16[24,4096]{1,0:T(8,128)(2,1)}, u32[]{:S(2)}, u32[]{:S(2)}) collective-permute-start(bf16[24,4096]{1,0:T(8,128)(2,1)} %get-tuple-element.326), channel_id=1, source_target_pairs={{0,2},{1,3},{2,0},{3,1},{4,6},{5,7},{6,4},{7,5},{8,10},{9,11},{10,... | collective-permute-start | bytes 589832 | tf_op jit(solution)/shard_map/ppermute | solution.py:97
  140.3 28.0 %collective-permute-start.31 = (bf16[96,4096]{1,0:T(8,128)(2,1)S(1)}, bf16[96,4096]{1,0:T(8,128)(2,1)S(1)}, u32[]{:S(2)}, u32[]{:S(2)}) collective-permute-start(bf16[96,4096]{1,0:T(8,128)(2,1)S(1)} %bitcast.215), channel_id=1, source_target_pairs={{0,8},{4,20},{8,0},{12,28},{16,24},{20,4},{24,16},{28,12},{1,9},{5... | collective-permute-start | bytes 2359304 | tf_op jit(solution)/shard_map/ppermute | solution.py:105
  142.0 26.3 %collective-permute-start.32 = (bf16[96,4096]{1,0:T(8,128)(2,1)S(1)}, bf16[96,4096]{1,0:T(8,128)(2,1)S(1)}, u32[]{:S(2)}, u32[]{:S(2)}) collective-permute-start(bf16[96,4096]{1,0:T(8,128)(2,1)S(1)} %bitcast.216), channel_id=1, source_target_pairs={{0,16},{4,12},{8,24},{12,4},{16,0},{20,28},{24,8},{28,20},{1,17},{... | collective-permute-start | bytes 2359304 | tf_op jit(solution)/shard_map/ppermute | solution.py:105
  168.3 20.7 %collective-permute-start.35 = (bf16[256,768]{1,0:T(8,128)(2,1)S(1)}, bf16[256,768]{1,0:T(8,128)(2,1)S(1)}, u32[]{:S(2)}, u32[]{:S(2)}) collective-permute-start(bf16[256,768]{1,0:T(8,128)(2,1)S(1)} %add_convert_fusion.32), channel_id=1, source_target_pairs={{0,2},{1,3},{2,0},{3,1},{4,6},{5,7},{6,4},{7,5},{8,10},{9,11},{10,... | collective-permute-start | bytes 1179656 | tf_op jit(solution)/shard_map/ppermute | solution.py:216
  190.1 31.7 %collective-permute-start.37 = (bf16[96,4096]{1,0:T(8,128)(2,1)S(1)}, bf16[96,4096]{1,0:T(8,128)(2,1)S(1)}, u32[]{:S(2)}, u32[]{:S(2)}) collective-permute-start(bf16[96,4096]{1,0:T(8,128)(2,1)S(1)} %bitcast.217), channel_id=1, source_target_pairs={{0,4},{4,0},{8,12},{12,8},{16,20},{20,16},{24,28},{28,24},{1,5},{5... | collective-permute-start | bytes 2359304 | tf_op jit(solution)/shard_map/ppermute | solution.py:105
  190.7 31.1 %collective-permute-start.38 = (bf16[96,4096]{1,0:T(8,128)(2,1)S(1)}, bf16[96,4096]{1,0:T(8,128)(2,1)S(1)}, u32[]{:S(2)}, u32[]{:S(2)}) collective-permute-start(bf16[96,4096]{1,0:T(8,128)(2,1)S(1)} %collective-permute-done.31.refs_1_), channel_id=1, source_target_pairs={{0,4},{4,0},{8,12},{12,8},{16,20},{20,16},{24,28},{28,24},{1,5},{5... | collective-permute-start | bytes 2359304 | tf_op jit(solution)/shard_map/ppermute | solution.py:105
  190.9 31.0 %collective-permute-start.39 = (bf16[96,4096]{1,0:T(8,128)(2,1)S(1)}, bf16[96,4096]{1,0:T(8,128)(2,1)S(1)}, u32[]{:S(2)}, u32[]{:S(2)}) collective-permute-start(bf16[96,4096]{1,0:T(8,128)(2,1)S(1)} %collective-permute-done.32.refs_2_), channel_id=1, source_target_pairs={{0,4},{4,0},{8,12},{12,8},{16,20},{20,16},{24,28},{28,24},{1,5},{5... | collective-permute-start | bytes 2359304 | tf_op jit(solution)/shard_map/ppermute | solution.py:105
  200.7 21.2 %collective-permute-start.40 = (bf16[96,4096]{1,0:T(8,128)(2,1)S(1)}, bf16[96,4096]{1,0:T(8,128)(2,1)S(1)}, u32[]{:S(2)}, u32[]{:S(2)}) collective-permute-start(bf16[96,4096]{1,0:T(8,128)(2,1)S(1)} %collective-permute-done.36.refs_3_), channel_id=1, source_target_pairs={{0,4},{4,0},{8,12},{12,8},{16,20},{20,16},{24,28},{28,24},{1,5},{5... | collective-permute-start | bytes 2359304 | tf_op jit(solution)/shard_map/ppermute | solution.py:105
  200.8 20.9 %collective-permute-start.47 = (bf16[256,768]{1,0:T(8,128)(2,1)S(1)}, bf16[256,768]{1,0:T(8,128)(2,1)S(1)}, u32[]{:S(2)}, u32[]{:S(2)}) collective-permute-start(bf16[256,768]{1,0:T(8,128)(2,1)S(1)} %add_convert_fusion.30), channel_id=1, source_target_pairs={{0,2},{1,3},{2,0},{3,1},{4,6},{5,7},{6,4},{7,5},{8,10},{9,11},{10,... | collective-permute-start | bytes 1179656 | tf_op jit(solution)/shard_map/ppermute | solution.py:216
  263.4 23.4 %collective-permute-start.56 = (bf16[4,96,2048]{2,1,0:T(8,128)(2,1)S(1)}, bf16[4,96,2048]{2,1,0:T(8,128)(2,1)S(1)}, u32[]{:S(2)}, u32[]{:S(2)}) collective-permute-start(bf16[4,96,2048]{2,1,0:T(8,128)(2,1)S(1)} %get-tuple-element.209), channel_id=1, source_target_pairs={{0,4},{4,0},{8,12},{12,8},{16,20},{20,16},{24,28},{28,24},{1,5},{5... | collective-permute-start | bytes 4718600 | tf_op jit(solution)/shard_map/ppermute | solution.py:179
  263.5 21.6 %collective-permute-start.53 = (bf16[256,768]{1,0:T(8,128)(2,1)S(1)}, bf16[256,768]{1,0:T(8,128)(2,1)S(1)}, u32[]{:S(2)}, u32[]{:S(2)}) collective-permute-start(bf16[256,768]{1,0:T(8,128)(2,1)S(1)} %add_convert_fusion.28), channel_id=1, source_target_pairs={{0,2},{1,3},{2,0},{3,1},{4,6},{5,7},{6,4},{7,5},{8,10},{9,11},{10,... | collective-permute-start | bytes 1179656 | tf_op jit(solution)/shard_map/ppermute | solution.py:216
  325.2 25.6 %collective-permute-start.65 = (bf16[4,96,3840]{2,1,0:T(8,128)(2,1)S(1)}, bf16[4,96,3840]{2,1,0:T(8,128)(2,1)S(1)}, u32[]{:S(2)}, u32[]{:S(2)}) collective-permute-start(bf16[4,96,3840]{2,1,0:T(8,128)(2,1)S(1)} %get-tuple-element.236), channel_id=1, source_target_pairs={{0,4},{4,0},{8,12},{12,8},{16,20},{20,16},{24,28},{28,24},{1,5},{5... | collective-permute-start | bytes 8847368 | tf_op jit(solution)/shard_map/ppermute | solution.py:179
  330.1 20.6 %collective-permute-start.62 = (bf16[256,768]{1,0:T(8,128)(2,1)S(1)}, bf16[256,768]{1,0:T(8,128)(2,1)S(1)}, u32[]{:S(2)}, u32[]{:S(2)}) collective-permute-start(bf16[256,768]{1,0:T(8,128)(2,1)S(1)} %add_convert_fusion.23), channel_id=1, source_target_pairs={{0,2},{1,3},{2,0},{3,1},{4,6},{5,7},{6,4},{7,5},{8,10},{9,11},{10,... | collective-permute-start | bytes 1179656 | tf_op jit(solution)/shard_map/ppermute | solution.py:216
  370.3 22.0 %collective-permute-start.68 = (bf16[32,768]{1,0:T(8,128)(2,1)}, bf16[32,768]{1,0:T(8,128)(2,1)}, u32[]{:S(2)}, u32[]{:S(2)}) collective-permute-start(bf16[32,768]{1,0:T(8,128)(2,1)} %get-tuple-element.322), channel_id=1, source_target_pairs={{0,1},{1,0},{2,3},{3,2},{4,5},{5,4},{6,7},{7,6},{8,9},{9,8},{10,11... | collective-permute-start | bytes 147464 | tf_op jit(solution)/shard_map/ppermute | solution.py:207
  384.8 20.4 %collective-permute-start.73 = (bf16[256,768]{1,0:T(8,128)(2,1)}, bf16[256,768]{1,0:T(8,128)(2,1)S(1)}, u32[]{:S(2)}, u32[]{:S(2)}) collective-permute-start(bf16[256,768]{1,0:T(8,128)(2,1)} %add_convert_fusion.20), channel_id=1, source_target_pairs={{0,2},{1,3},{2,0},{3,1},{4,6},{5,7},{6,4},{7,5},{8,10},{9,11},{10,... | collective-permute-start | bytes 1179656 | tf_op jit(solution)/shard_map/ppermute | solution.py:216
  434.5 23.5 %collective-permute-start.79 = (bf16[1,96,2432]{2,1,0:T(8,128)(2,1)}, bf16[1,96,2432]{2,1,0:T(8,128)(2,1)}, u32[]{:S(2)}, u32[]{:S(2)}) collective-permute-start(bf16[1,96,2432]{2,1,0:T(8,128)(2,1)} %add_convert_fusion.11), channel_id=1, source_target_pairs={{0,8},{4,20},{8,0},{12,28},{16,24},{20,4},{24,16},{28,12},{1,9},{5... | collective-permute-start | bytes 1400840 | tf_op jit(solution)/shard_map/ppermute | solution.py:179
  (196 other events, 1892.7 us)

commit v3 on v2

--- a/solution.py
+++ b/solution.py
@@ -81,55 +81,25 @@
     return [(i, i ^ k) for i in range(count)]
 
 
-def place_seq(pieces):
-    count, pos = len(pieces), lax.axis_index("seq")
-    order = jnp.stack([pos ^ k for k in range(count)]).astype(jnp.int32)
-    moves = [
-        (lambda ins, idx, k=k: ins[k], lambda outs, idx, k=k: outs[0].at[idx[k]])
-        for k in range(count)
-    ]
-    shape = (count,) + pieces[0].shape
-    return dma_moves(order, pieces, [(shape, pieces[0].dtype)], moves)[0]
-
-
-def send_seq(piece_for):
-    count = lax.axis_size("seq")
-    return [lax.ppermute(piece_for(k), "seq", perm_seq(count, k)) for k in range(1, count)]
-
-
-def wave(pieces, hops):
-    count = lax.axis_size("dp")
-    stages = dp_stages(count)
-    for label in [p for p in pieces if len(p) == hops]:
-        for stage in range(label[-1] + 1 if label else 0, len(stages)):
-            pieces[label + (stage,)] = lax.ppermute(
-                pieces[label], "dp", perm(count, stages[stage])
-            )
-
-
-def arrived(pieces, hops, last=None):
-    final = len(dp_stages(lax.axis_size("dp"))) - 1
-    return [p for p in pieces if len(p) == hops and (last or p[-1] != final)]
-
-
 def fence(*values):
     return lax.optimization_barrier(values) if len(values) > 1 else values
 
 
-def fence_pieces(groups, *values):
-    flat = [pieces[label] for pieces, labels in groups for label in labels]
-    out = fence(*values, *flat)
-    rest = list(out[len(values) :])
-    for pieces, labels in groups:
-        for label in labels:
-            pieces[label] = rest.pop(0)
-    return out[: len(values)]
-
-
-def place_dp(held, widths):
-    pieces = [held[label] for label in dp_labels(lax.axis_size("dp"))]
-    count = len(pieces)
-    lead = pieces[0].shape[:-1]
+def gate(value, *others):
+    return lax.optimization_barrier((value,) + others)[0] if others else value
+
+
+def seq_order(steps):
+    pos = lax.axis_index("seq")
+    return jnp.stack([pos ^ k for k in steps]).astype(jnp.int32)
+
+
+def place_seq(pieces, widths=None):
+    return place(pieces, seq_order(range(len(pieces))), widths or [pieces[0].shape[-1]])
+
+
+def place(pieces, order, widths):
+    count, lead = len(pieces), pieces[0].shape[:-1]
     moves, shapes, low = [], [], 0
     for j, columns in enumerate(widths):
         shapes.append(((count,) + lead + (columns,), bf16))
@@ -143,7 +113,53 @@
                 )
             )
         low += columns
-    return [p.reshape(-1, p.shape[-1]) for p in dma_moves(dp_order(), pieces, shapes, moves)]
+    return [p.reshape(-1, p.shape[-1]) for p in dma_moves(order, pieces, shapes, moves)]
+
+
+def fold(block, rows):
+    count, width = block.shape[-2:]
+    extra = count - rows
+    if not extra:
+        return block
+    if rows % 8 or extra % 8 or extra < 0 or rows % extra or width % (rows // extra * LANES):
+        return block.reshape(block.shape[:-2] + (rows, -1))
+    groups = jnp.split(block[..., rows:, :], rows // extra, axis=-1)
+    return jnp.concatenate([block[..., :rows, :], jnp.concatenate(groups, axis=-2)], axis=-1)
+
+
+def unfold(block, count, width):
+    rows = block.shape[-2]
+    extra = count - rows
+    if not extra:
+        return block
+    if rows % 8 or extra % 8 or extra < 0 or rows % extra or width % (rows // extra * LANES):
+        return block.reshape(block.shape[:-2] + (count, width))
+    groups = jnp.split(block[..., width:], rows // extra, axis=-2)
+    return jnp.concatenate([block[..., :width], jnp.concatenate(groups, axis=-1)], axis=-2)
+
+
+def send_seq(piece_for, every=1):
+    count = lax.axis_size("seq")
+    steps = range(every, count, every)
+    return [lax.ppermute(piece_for(k), "seq", perm_seq(count, k)) for k in steps]
+
+
+def wave(pieces, hops, *after):
+    count = lax.axis_size("dp")
+    stages = dp_stages(count)
+    for label in [p for p in pieces if len(p) == hops]:
+        later = range(label[-1] + 1 if label else 0, len(stages))
+        if len(later):
+            pieces[label] = gate(pieces[label], *after)
+        for stage in later:
+            pieces[label + (stage,)] = lax.ppermute(
+                pieces[label], "dp", perm(count, stages[stage])
+            )
+
+
+def place_dp(held, widths, *after):
+    pieces = [held[label] for label in dp_labels(lax.axis_size("dp"))]
+    return place(pieces, gate(dp_order(), *after), widths)
 
 
 def scatter_dp(grads):
@@ -178,49 +194,108 @@
         count = lax.axis_size("dp")
         self.got = lax.ppermute(send, "dp", perm(count, self.left.pop()))
 
-    def step(self):
+    def step(self, *after):
+        self.keep = gate(self.keep, *after)
         half = self.keep.shape[0] // 2
         wide = lambda part: part.astype(f32)
         send = (wide(self.keep[half:]) + wide(self.got[half:])).astype(bf16)
         self.keep = (wide(self.keep[:half]) + wide(self.got[:half])).astype(bf16)
         self.hop(send)
 
-    def finish(self):
-        while self.left:
-            self.step()
-        return self.keep[0].astype(f32) + self.got[0].astype(f32)
-
-
-def fence_sums(sums, *values):
-    out = fence(*values, *[s.got for s in sums])
-    for s, got in zip(sums, out[len(values) :]):
-        s.got = got
-    return out[: len(values)]
-
-
-def scatter_seq(blocks):
-    count, pos = lax.axis_size("seq"), lax.axis_index("seq")
-    sent = blocks.astype(bf16)
-    total = lax.dynamic_index_in_dim(blocks, pos, 0, keepdims=False)
-    for k in range(1, count):
-        piece = lax.dynamic_index_in_dim(sent, pos ^ k, 0, keepdims=False)
-        total = total + lax.ppermute(piece, "seq", perm_seq(count, k)).astype(f32)
-    return total
-
-
-def seq_masks():
-    return [1 << b for b in range(lax.axis_size("seq").bit_length() - 1)]
-
-
-def sum_hop(part, mask):
-    got = lax.ppermute(part, "seq", perm_seq(lax.axis_size("seq"), mask))
-    return (part.astype(f32) + got.astype(f32)).astype(bf16)
-
-
-def sum_seq(part):
-    for mask in seq_masks():
-        part = sum_hop(part, mask)
-    return part
+    def finish(self, *after):
+        while len(self.left):
+            self.step(*after)
+        return gate(self.keep, *after)[0].astype(f32) + self.got[0].astype(f32)
+
+
+def pick_seq(blocks):
+    pos = lax.axis_index("seq")
+    return lambda k: lax.dynamic_index_in_dim(blocks, pos ^ k, 0, keepdims=False)
+
+
+class Sum:
+    def __init__(self, part, *after, pair=False):
+        self.masks = [1 << b for b in range(lax.axis_size("seq").bit_length() - 1)]
+        if pair:
+            self.masks = self.masks[:1]
+        self.part = gate(part, *after)
+        self.send()
+
+    def send(self):
+        pairs = perm_seq(lax.axis_size("seq"), self.masks.pop(0))
+        self.got = lax.ppermute(self.part, "seq", pairs)
+
+    def add(self, *after):
+        part = gate(self.part, *after)
+        self.part = (part.astype(f32) + self.got.astype(f32)).astype(bf16)
+        if self.masks:
+            self.send()
+
+    def finish(self, *after):
+        while self.masks:
+            self.add(*after)
+        self.add(*after)
+        return self.part
+
+
+def split_columns(odd, weights, chunk):
+    rows, width = weights.shape
+    pairs = width // (2 * chunk)
+
+    def body(odd_ref, weights_ref, own_ref, other_ref):
+        def copy(own, other):
+            for j in range(pairs):
+                at = pl.ds(j * chunk, chunk)
+                own[:, at] = weights_ref[:, pl.ds(2 * j * chunk, chunk)]
+                other[:, at] = weights_ref[:, pl.ds((2 * j + 1) * chunk, chunk)]
+
+        @pl.when(odd_ref[0] == 0)
+        def _():
+            copy(own_ref, other_ref)
+
+        @pl.when(odd_ref[0] == 1)
+        def _():
+            copy(other_ref, own_ref)
+
+    return pl.pallas_call(
+        body,
+        in_specs=[pl.BlockSpec(memory_space=pltpu.SMEM), pl.BlockSpec(memory_space=pltpu.VMEM)],
+        out_specs=[pl.BlockSpec(memory_space=pltpu.VMEM)] * 2,
+        out_shape=[jax.ShapeDtypeStruct((rows, width // 2), weights.dtype)] * 2,
+    )(odd, weights)
+
+
+def join_columns(odd, pieces, chunk):
+    rows, width = pieces[0].shape
+    count = len(pieces)
+
+    def body(odd_ref, *refs):
+        out_ref = refs[-1]
+
+        def fill(first, second):
+            for j in range(width // chunk):
+                at = pl.ds(j * chunk, chunk)
+                for side, group in enumerate((first, second)):
+                    total = group[0][:, at].astype(f32)
+                    for ref in group[1:]:
+                        total = total + ref[:, at].astype(f32)
+                    out_ref[:, pl.ds((2 * j + side) * chunk, chunk)] = total
+
+        @pl.when(odd_ref[0] == 0)
+        def _():
+            fill(refs[0:count:2], refs[1:count:2])
+
+        @pl.when(odd_ref[0] == 1)
+        def _():
+            fill(refs[1:count:2], refs[0:count:2])
+
+    return pl.pallas_call(
+        body,
+        in_specs=[pl.BlockSpec(memory_space=pltpu.SMEM)]
+        + [pl.BlockSpec(memory_space=pltpu.VMEM)] * count,
+        out_specs=pl.BlockSpec(memory_space=pltpu.VMEM),
+        out_shape=jax.ShapeDtypeStruct((rows, 2 * width), f32),
+    )(odd, *pieces)
 
 
 def inv_rms(values):
@@ -433,31 +508,36 @@
     table_f = route_table(slots[2], counts[2], token_pos)
 
     rows, wide = light_qkv.shape
-    unit = heavy_down.shape[0]
+    unit, light_unit = heavy_down.shape[0], light_down.shape[0]
+    light_cut, half = light_gate_up.shape[1], seq // 2
     merged = lambda block: block.reshape(-1, block.shape[-1])
+    by_dp = lambda grad: grad.reshape(dp, -1, grad.shape[1])
+    by_seq = lambda mine: mine.reshape(seq, rows, -1)
     hops = len(dp_stages(dp))
+    odd = pos & 1
+    fold_width = width * light_unit // rows
 
     small = jnp.stack([attn_gain, attn_router, ffn_gain, ffn_router], axis=1)
     first = jnp.concatenate([light_qkv, jnp.pad(small, ((0, 0), (0, LANES - 4)))], axis=1)
     got_first = send_seq(lambda k: first)
+    light_ffn_own = jnp.concatenate([light_gate_up, fold(light_down, rows)], axis=1)
+    light_ffn_all = lax.all_gather(light_ffn_own, ("dp", "seq"), axis=0, tiled=True)
     marked = jnp.concatenate(
         [x_in, jnp.broadcast_to(seg.astype(bf16)[:, None], (tokens, LANES))], axis=1
     )
     left = lax.ppermute(marked[tokens - WINDOW :], "seq", [(i, i + 1) for i in range(seq - 1)])
     right = lax.ppermute(marked[:WINDOW], "seq", [(i + 1, i) for i in range(seq - 1)])
     kv_part = dot(table_kv, marked).astype(bf16)
-    cot_part = dot(table_f, cot).astype(bf16)
-    second = jnp.concatenate([heavy_qkv, light_out, heavy_out], axis=1)
-    kv_part, cot_part, second, *got_first = fence(kv_part, cot_part, second, *got_first)
-
-    first_held = {(): merged(place_seq([first] + got_first))}
+    own_gu, other_gu = split_columns(odd[None], heavy_gate_up, unit)
+    first_held = {(): place_seq([first] + got_first)[0]}
     wave(first_held, 0)
+
+    others = fence(heavy_qkv, light_out, heavy_out, *got_first)[:3]
+    second = jnp.concatenate(others, axis=1)
+    sum_kv = Sum(kv_part, *got_first)
     got_second = send_seq(lambda k: second)
-    seq_left = seq_masks()
-    kv_part = sum_hop(kv_part, seq_left.pop(0))
     for h in range(1, hops):
-        fence_pieces([(first_held, arrived(first_held, h))])
-        wave(first_held, h)
+        wave(first_held, h, second)
     w_lqkv, small_all = place_dp(first_held, [wide, LANES])
 
     small_t = small_all[:, :4].T
@@ -471,90 +551,59 @@
     ext_inv = inv_rms(ext_in)
     normed_ext = (ext_in * ext_inv * gain_attn).astype(bf16)
     normed = normed_ext[WINDOW : WINDOW + tokens]
-    place = jnp.arange(tokens + 2 * WINDOW) - WINDOW
-    outside = ((pos == 0) & (place < 0)) | ((pos == seq - 1) & (place >= tokens))
+    place_of = jnp.arange(tokens + 2 * WINDOW) - WINDOW
+    outside = ((pos == 0) & (place_of < 0)) | ((pos == seq - 1) & (place_of >= tokens))
     key_seg = jnp.where(outside, -1.0, ext_marked[:, width].astype(f32))
     seg_f = seg.astype(f32)
     light_q = dot(normed, w_lqkv[:, :width]).astype(bf16)
     light_kv = dot(normed_ext, w_lqkv[:, width:]).astype(bf16)
-    z_second = merged(place_seq([second] + got_second))
-    light_q, light_kv, kv_part, z_second = fence(light_q, light_kv, kv_part, z_second)
-    second_held = {(): z_second}
+    cot_part = dot(table_f, cot).astype(bf16)
+
+    (second_z,) = place_seq([gate(second, light_kv, light_q)] + got_second)
+    second_held = {(): second_z}
     wave(second_held, 0)
-    for mask in seq_left:
-        kv_part = sum_hop(kv_part, mask)
+    sum_kv.add(light_kv)
     light_mixed, light_probs = attend(
-        light_q, light_kv, seg_f, key_seg, L_HEAD, WINDOW, WINDOW, bf16
+        gate(light_q, second_z, sum_kv.part), light_kv, seg_f, key_seg, L_HEAD, WINDOW, WINDOW, bf16
     )
     q_rows = dot(table_q, normed).astype(bf16)
     q_seg = jnp.sum(table_q.astype(f32) * seg_f[None], axis=1)
-    columns = heavy_gate_up.reshape(rows, 2 * dp, seq, unit)
-    light_mixed, q_rows, kv_marked, gate_up, columns, down = fence_pieces(
-        [(second_held, arrived(second_held, 1))],
-        light_mixed, q_rows, kv_part, light_gate_up, columns, light_down
-    )
 
     for h in range(1, hops):
-        wave(second_held, h)
-
-    def gate_up_for(k):
-        own = lax.dynamic_index_in_dim(columns, pos ^ k, 2, keepdims=False)
-        return jnp.concatenate([gate_up, own.reshape(rows, -1)], axis=1)
-
-    got_gate_up = send_seq(gate_up_for)
-    got_down = send_seq(lambda k: down)
-    w_hqkv, w_lout, w_hout = place_dp(second_held, [wide, width, width])
-
+        wave(second_held, h, light_mixed)
+    kv_marked = sum_kv.finish(light_mixed)
+    own_gu, other_gu = fence(own_gu, other_gu, light_mixed)[:2]
+    got_gu = send_seq(lambda k: other_gu if k & 1 else own_gu)
+    got_down = send_seq(lambda k: gate(heavy_down, light_mixed), 2)
+    w_hqkv, w_lout, w_hout = place_dp(second_held, [wide, width, width], light_mixed)
     kv_in = kv_marked[:, :width].astype(f32)
-    kv_inv = inv_rms(kv_in)
-    kv_rows = (kv_in * kv_inv * gain_attn).astype(bf16)
+    kv_rows = (kv_in * inv_rms(kv_in) * gain_attn).astype(bf16)
     kv_seg = jnp.where(jnp.arange(routed) < counts[1], kv_marked[:, width].astype(f32), -1.0)
     heavy_q = dot(q_rows, w_hqkv[:, :width]).astype(bf16)
     heavy_kv = dot(kv_rows, w_hqkv[:, width:]).astype(bf16)
     heavy_mixed, heavy_probs = attend(
         heavy_q, heavy_kv, q_seg, kv_seg, H_HEAD, min(routed, 256), 0, f32
     )
-    gate = sigmoid(
+    gate_attn = sigmoid(
         jnp.sum(q_rows.astype(f32) * router_attn.astype(f32), axis=1, keepdims=True)
     )
-    gated = (gate * heavy_mixed).astype(bf16)
+    gated = (gate_attn * heavy_mixed).astype(bf16)
     heavy_rows = dot(gated, w_hout).astype(bf16)
     midway = x_in.astype(f32) + dot(light_mixed, w_lout) + dot_tn(table_q, heavy_rows)
-
     inv_ffn = inv_rms(midway)
     normed_ffn = (midway * inv_ffn * gain_ffn).astype(bf16)
     rows_part = dot(table_f, normed_ffn).astype(bf16)
-    rows_part, normed_ffn, cot_part, *got = fence(
-        rows_part, normed_ffn, cot_part, *got_gate_up, *got_down
-    )
-    got_gate_up, got_down = got[: seq - 1], got[seq - 1 :]
-    gate_up_held = {(): merged(place_seq([gate_up_for(0)] + got_gate_up))}
-    z_down = merged(place_seq([down] + got_down))
-    if z_down.shape == heavy_down.shape:
-        down_held = [{(): jnp.concatenate([z_down, heavy_down], axis=1)}]
-    else:
-        down_held = [{(): z_down}, {(): heavy_down}]
-    ffn_held = [gate_up_held] + down_held
-    for held in ffn_held:
-        wave(held, 0)
-    seq_left = seq_masks()
-    rows_part = sum_hop(rows_part, seq_left.pop(0))
-    rows_part, normed_ffn, cot_part = fence_pieces(
-        [(held, arrived(held, 1)) for held in ffn_held], rows_part, normed_ffn, cot_part
-    )
-    for h in range(1, hops):
-        for held in ffn_held:
-            wave(held, h)
-    for mask in seq_left:
-        rows_part = sum_hop(rows_part, mask)
-    w_lgu, w_hgu = place_dp(gate_up_held, [light_gate_up.shape[1], 2 * dp * unit])
-    w_ldown, w_hdown = sum(
-        [place_dp(held, [width] * (2 // len(down_held))) for held in down_held], []
-    )
-    ffn_rows, cot_part, normed_ffn = fence(rows_part, cot_part, normed_ffn)
-    cot_rows = sum_seq(cot_part)
-
-    by_dp = lambda grad: grad.reshape(dp, -1, grad.shape[1])
+
+    sum_rows = Sum(rows_part, pair=True)
+    sum_cot = Sum(cot_part, rows_part, pair=True)
+    (gu_z,) = place_seq([gate(own_gu, heavy_mixed)] + got_gu)
+    (down_z,) = place([gate(heavy_down, heavy_mixed)] + got_down, seq_order(range(0, seq, 2)) // 2, [width])
+    gu_held, down_held = {(): gu_z}, {(): down_z}
+    wave(gu_held, 0)
+    wave(down_held, 0)
+    w_lgu = light_ffn_all[:, :light_cut]
+    w_ldown = merged(unfold(light_ffn_all[:, light_cut:].reshape(dp * seq, rows, -1), light_unit, width))
+
     light_units = w_ldown.shape[0]
     light_pre = dot(normed_ffn, w_lgu)
     light_gate, light_up = light_pre[:, :light_units], light_pre[:, light_units:]
@@ -568,11 +617,19 @@
     ).astype(bf16)
     grad_lgu = dot_tn(normed_ffn, light_pre_grad).astype(bf16)
     normed_ffn_grad = dot_nt(light_pre_grad, w_lgu)
-    ffn_rows, cot_rows, normed_ffn_grad, grad_ldown, grad_lgu = fence(
-        ffn_rows, cot_rows, normed_ffn_grad, grad_ldown, grad_lgu
-    )
-
-    sum_light = [scatter_dp([by_dp(grad_lgu)]), scatter_dp([by_dp(grad_ldown)])]
+
+    grad_ldown = merged(fold(grad_ldown.reshape(dp * seq, -1, width), rows))
+    light_sum = lax.psum_scatter(
+        jnp.concatenate([grad_lgu, grad_ldown], axis=1), ("dp", "seq"), scatter_dimension=0, tiled=True
+    )
+    for h in range(1, hops):
+        wave(gu_held, h, light_ffn)
+        wave(down_held, h, light_ffn)
+    ffn_rows = sum_rows.finish(normed_ffn_grad, light_ffn)
+    cot_rows = sum_cot.finish(normed_ffn_grad, light_ffn)
+    (w_hgu,) = place_dp(gu_held, [gu_z.shape[1]], ffn_rows)
+    (w_hdown,) = place_dp(down_held, [width], ffn_rows)
+
     heavy_units = w_hdown.shape[0]
     heavy_pre = dot(ffn_rows, w_hgu)
     heavy_gate, heavy_up = heavy_pre[:, :heavy_units], heavy_pre[:, heavy_units:]
@@ -593,128 +650,125 @@
     )
     rows_grad_part = dot_nt(heavy_pre_grad, w_hgu) + ffn_score_grad * router_ffn.astype(f32)
     rows_grad = rows_grad_part.astype(bf16)
-    rows_grad, heavy_hidden, heavy_pre_grad, ffn_score_grad = fence_sums(
-        sum_light, rows_grad, heavy_hidden, heavy_pre_grad, ffn_score_grad
-    )
-    seq_left = seq_masks()
-    rows_grad = sum_hop(rows_grad, seq_left.pop(0))
-    for s in sum_light:
-        s.step()
+    sum_rows = Sum(rows_grad, pair=True)
+    heavy_hidden, heavy_pre_grad, ffn_score_grad = fence(
+        heavy_hidden, heavy_pre_grad, ffn_score_grad, rows_grad
+    )[:3]
     grad_ffn_router = jnp.sum(ffn_rows.astype(f32) * ffn_score_grad, axis=0)
     grad_hdown = dot_tn(heavy_hidden, cot_rows).astype(bf16)
     grad_hgu = dot_tn(ffn_rows, heavy_pre_grad).astype(bf16)
     out_part = dot(heavy_hidden, w_hdown).astype(bf16)
-    rows_grad, grad_hdown, grad_hgu, out_part = fence_sums(
-        sum_light, rows_grad, grad_hdown, grad_hgu, out_part
-    )
-    for mask in seq_left:
-        rows_grad = sum_hop(rows_grad, mask)
-    for s in sum_light:
-        s.step()
+    rows_grad = sum_rows.finish(grad_hdown, grad_hgu, out_part)
     sum_heavy = [scatter_dp([by_dp(grad_hgu)]), scatter_dp([by_dp(grad_hdown)])]
-    rows_grad, out_part = fence_sums(sum_light + sum_heavy, rows_grad, out_part)
-
+
+    sum_out = Sum(out_part, rows_grad, pair=True)
+    normed_ffn_grad = normed_ffn_grad + dot_tn(table_f, rows_grad)
+    midway_grad = cot.astype(f32) + norm_back(midway, inv_ffn, normed_ffn_grad * gain_ffn)
+
+    out_grad = midway_grad.astype(bf16)
     for s in sum_heavy:
-        s.step()
-    out_left = seq_masks()
-    out_part = sum_hop(out_part, out_left.pop(0))
-    lgu_mine = sum_light[0].finish().reshape(seq, rows, -1)
-    ldown_mine = sum_light[1].finish().reshape(seq, -1, width)
-    normed_ffn_grad = normed_ffn_grad + dot_tn(table_f, rows_grad)
-    grad_ffn_gain = jnp.sum(normed_ffn_grad * midway * inv_ffn, axis=0)
-    midway_grad = cot.astype(f32) + norm_back(midway, inv_ffn, normed_ffn_grad * gain_ffn)
-
-    out_grad = midway_grad.astype(bf16)
+        s.step(out_grad)
+    out_grad = gate(out_grad, *[s.keep for s in sum_heavy])
     grad_lout = dot_tn(light_mixed, out_grad).astype(bf16)
     heavy_out_cot = dot(table_q, out_grad).astype(bf16)
     grad_hout = dot_tn(gated, heavy_out_cot).astype(bf16)
     gated_grad = dot_nt(heavy_out_cot, w_hout).astype(bf16).astype(f32)
-    heavy_mixed_grad = (gate * gated_grad).astype(bf16)
-    attn_score_grad = gate * (1.0 - gate) * jnp.sum(gated_grad * heavy_mixed, axis=1, keepdims=True)
+    heavy_mixed_grad = (gate_attn * gated_grad).astype(bf16)
+    attn_score_grad = gate_attn * (1.0 - gate_attn) * jnp.sum(gated_grad * heavy_mixed, axis=1, keepdims=True)
     heavy_q_grad, heavy_kv_grad = attend_back(
         heavy_q, heavy_kv, heavy_probs, heavy_mixed_grad, H_HEAD, min(routed, 256), 0
     )
     grad_hq = dot_tn(q_rows, heavy_q_grad).astype(bf16)
     grad_hkv = dot_tn(kv_rows, heavy_kv_grad).astype(bf16)
     grad_attn_router = jnp.sum(q_rows.astype(f32) * attn_score_grad, axis=0)
+    routers = jnp.pad(
+        jnp.stack([grad_attn_router, grad_ffn_router], axis=1), ((0, 0), (0, LANES - 2))
+    ).astype(bf16)
     q_rows_grad = (
         dot_nt(heavy_q_grad, w_hqkv[:, :width]) + attn_score_grad * router_attn.astype(f32)
     ).astype(bf16)
-    kv_rows_grad = dot_nt(heavy_kv_grad, w_hqkv[:, width:])
+    kv_send = dot_nt(heavy_kv_grad, w_hqkv[:, width:]).astype(bf16)
     mixed_grad = dot_nt(out_grad, w_lout).astype(bf16)
-    mixed_grad, kv_send, out_part, lgu_mine, ldown_mine, *attn_grads = fence_sums(
-        sum_heavy,
-        mixed_grad,
-        kv_rows_grad.astype(bf16),
-        out_part,
-        lgu_mine,
-        ldown_mine,
-        *[by_dp(g) for g in (grad_hq, grad_hkv, grad_lout, grad_hout)],
-    )
-
+    attn_grads = [by_dp(g) for g in (grad_hq, grad_hkv, grad_lout, grad_hout, routers)]
+
+    sum_attn = scatter_dp(attn_grads)
+    sum_kv = Sum(kv_send)
+    out_part = sum_out.finish(kv_send)
     for s in sum_heavy:
-        s.step()
-    sum_attn = scatter_dp(attn_grads)
-    for mask in out_left:
-        out_part = sum_hop(out_part, mask)
-    kv_left = seq_masks()
-    kv_send = sum_hop(kv_send, kv_left.pop(0))
+        s.step(kv_send)
     light_q_grad, light_kv_grad = attend_back(
-        light_q, light_kv, light_probs, mixed_grad, L_HEAD, WINDOW, WINDOW
-    )
-    light_q_grad, light_kv_grad, kv_send, out_part, lgu_mine, ldown_mine = fence_sums(
-        sum_heavy + [sum_attn], light_q_grad, light_kv_grad, kv_send, out_part, lgu_mine, ldown_mine
-    )
-    sum_attn.step()
-    for mask in kv_left:
-        kv_send = sum_hop(kv_send, mask)
-    out_light_down = scatter_seq(ldown_mine)
-    hgu_mine = sum_heavy[0].finish().reshape(seq, rows, -1)
-    out_heavy_down = sum_heavy[1].finish()
-    ext_grad = dot_nt(light_kv_grad, w_lqkv[:, width:])
-
+        light_q,
+        light_kv,
+        light_probs,
+        gate(mixed_grad, sum_attn.keep, kv_send, out_part, *[s.keep for s in sum_heavy]),
+        L_HEAD,
+        WINDOW,
+        WINDOW,
+    )
+
+    sum_attn.step(light_kv_grad)
+    grad_lq = by_dp(dot_tn(normed, light_q_grad).astype(bf16))
+    grad_lkv = by_dp(dot_tn(normed_ext, light_kv_grad).astype(bf16))
+    sum_last = scatter_dp([grad_lq, grad_lkv])
+    heavy_z = by_seq(sum_heavy[0].finish(sum_last.keep)).astype(bf16)
+    down_z = sum_heavy[1].finish(sum_last.keep).astype(bf16).reshape(half, unit, width)
+    sum_kv.add(grad_lkv)
+    got_heavy = [pick_seq(heavy_z)(0)] + send_seq(pick_seq(heavy_z))
+    pick_down = lambda k: lax.dynamic_index_in_dim(down_z, (pos ^ k) // 2, 0, keepdims=False)
+    got_down = [pick_down(0)] + send_seq(pick_down, 2)
+    sum_last.step()
+    ext_grad = dot_nt(gate(light_kv_grad, sum_last.keep), w_lqkv[:, width:])
+    from_right = lax.ppermute(
+        ext_grad[WINDOW + tokens :].astype(bf16), "seq", [(i, i + 1) for i in range(seq - 1)]
+    )
+    from_left = lax.ppermute(
+        ext_grad[:WINDOW].astype(bf16), "seq", [(i + 1, i) for i in range(seq - 1)]
+    )
     own_grad = (
         ext_grad[WINDOW : WINDOW + tokens]
         + dot_nt(light_q_grad, w_lqkv[:, :width])
         + dot_tn(table_q, q_rows_grad)
     )
-    grad_attn_gain = (
-        jnp.sum(own_grad * (ext_in * ext_inv)[WINDOW : WINDOW + tokens], axis=0)
-        + jnp.sum(ext_grad[:WINDOW] * (ext_in * ext_inv)[:WINDOW], axis=0)
-        + jnp.sum(ext_grad[WINDOW + tokens :] * (ext_in * ext_inv)[WINDOW + tokens :], axis=0)
-        + jnp.sum(kv_rows_grad * (kv_in * kv_inv), axis=0)
-    )
-    small_grads = jnp.stack([grad_attn_gain, grad_attn_router, grad_ffn_gain, grad_ffn_router], 1)
-    grad_lqkv = [
-        dot_tn(normed, light_q_grad).astype(bf16),
-        dot_tn(normed_ext, light_kv_grad).astype(bf16),
-        jnp.pad(small_grads, ((0, 0), (0, LANES - 4))).astype(bf16),
-    ]
-    *grad_lqkv, hgu_mine, lgu_mine, out_light_down = fence_sums(
-        [sum_attn], *[by_dp(g) for g in grad_lqkv], hgu_mine, lgu_mine, out_light_down
-    )
-    sum_last = scatter_dp(grad_lqkv)
-    both = jnp.concatenate([lgu_mine.astype(bf16), hgu_mine.astype(bf16)], axis=2)
-    pick = lambda k: lax.dynamic_index_in_dim(both, pos ^ k, 0, keepdims=False)
-    got = [pick(0)] + send_seq(pick)
-    from_right = lax.ppermute(
-        ext_grad[WINDOW + tokens :].astype(bf16), "seq", [(i, i + 1) for i in range(seq - 1)]
-    )
-    from_left = lax.ppermute(
-        ext_grad[:WINDOW].astype(bf16), "seq", [(i + 1, i) for i in range(seq - 1)]
-    )
-    sum_last.step()
-    attn_mine = sum_attn.finish().reshape(seq, rows, -1)
-    attn_mine, kv_total, *got = fence_sums([sum_last], attn_mine, kv_send, *got)
-    sum_last.step()
-    heavy_outs = scatter_seq(attn_mine)
-    light_cut = light_gate_up.shape[1]
-    out_light_gate_up = sum(g[:, :light_cut].astype(f32) for g in got)
-    slices = place_seq(got)[:, :, light_cut:].reshape(seq, rows, 2 * dp, unit)
-    out_heavy_gate_up = slices.transpose(1, 2, 0, 3).astype(f32).reshape(rows, -1)
+    sum_last.step(own_grad)
+    sum_attn.step(own_grad)
+    attn_mine = by_seq(sum_attn.finish(own_grad))
+    light_last = by_seq(sum_last.finish(attn_mine))
+    attn_sent = send_seq(pick_seq(attn_mine.astype(bf16)))
+    light_sent = send_seq(pick_seq(light_last.astype(bf16)))
+    attn_outs = pick_seq(attn_mine)(0) + sum(g.astype(f32) for g in attn_sent)
+    last_mine = light_last
+    light_last = light_sent[0]
+    kv_total = sum_kv.finish(light_last)
+    light_outs = pick_seq(last_mine)(0) + sum(g.astype(f32) for g in light_sent)
+
+    light_sum = gate(light_sum, light_last, ext_grad).astype(f32)
+    out_light_gate_up = light_sum[:, :light_cut]
+    out_light_down = unfold(light_sum[:, light_cut:], light_unit, width)
+    got_heavy = [gate(g, light_last) for g in got_heavy]
+    got_down = [gate(g, light_last) for g in got_down]
+    out_heavy_down = sum(g.astype(f32) for g in got_down)
+    out_heavy_gate_up = join_columns(odd[None], got_heavy, unit)
+    midway, out_part = fence(midway, out_part, light_last)[:2]
     layer_output = (midway + light_ffn + dot_tn(table_f, out_part)).astype(bf16)
-    light_outs = scatter_seq(sum_last.finish().reshape(seq, rows, -1))
-    out_small = light_outs[:, wide : wide + 4].T
+    out_heavy_qkv = attn_outs[:, :wide]
+    out_light_out = attn_outs[:, wide : wide + width]
+    out_heavy_out = attn_outs[:, wide + width : wide + 2 * width]
+    out_attn_router = attn_outs[:, wide + 2 * width]
+    out_ffn_router = attn_outs[:, wide + 2 * width + 1]
+
+    def along(weight, grad):
+        return jnp.sum(weight.astype(f32) * grad, axis=1)
+
+    out_attn_gain = (
+        along(light_qkv, light_outs)
+        + along(heavy_qkv, out_heavy_qkv)
+        + attn_router.astype(f32) * out_attn_router
+    ) / attn_gain.astype(f32)
+    out_ffn_gain = (
+        along(light_gate_up, out_light_gate_up)
+        + along(heavy_gate_up, out_heavy_gate_up)
+        + ffn_router.astype(f32) * out_ffn_router
+    ) / ffn_gain.astype(f32)
     edge = jnp.concatenate(
         [from_right.astype(f32), jnp.zeros((tokens - 2 * WINDOW, width), f32), from_left.astype(f32)]
     )
@@ -727,18 +781,18 @@
     return (
         layer_output[None],
         input_grad.astype(bf16)[None],
-        out_small[0],
-        light_outs[:, :wide],
-        heavy_outs[:, wide : wide + width],
-        heavy_outs[:, :wide],
-        heavy_outs[:, wide + width :],
-        out_small[1],
-        out_small[2],
+        out_attn_gain,
+        light_outs,
+        out_light_out,
+        out_heavy_qkv,
+        out_heavy_out,
+        out_attn_router,
+        out_ffn_gain,
         out_light_gate_up,
         out_light_down,
         out_heavy_gate_up,
         out_heavy_down,
-        out_small[3],
+        out_ffn_router,
     )
 
 

time: 482 us -> 446 us (0.925)
  waiting for transfers between devices: 169 us -> 112 us
  starting transfers between devices: 98.9 us -> 74.5 us
  matrix products: 54.3 us -> 76 us
  other arithmetic: 45.3 us -> 64.5 us
  between operations: 3.33 us -> 16.4 us
  local copies, waits for them, and re-layouts: 43.1 us -> 34.4 us
    ppermute x21 -> x8, waiting for transfers between devices: 97.2 us -> 41.4 us  [send(): self.got = lax.ppermute(self.part, 'seq', pairs)]
    ppermute x21 -> x8, starting transfers between devices: 34.9 us -> 3.27 us  [send(): self.got = lax.ppermute(self.part, 'seq', pairs)]
    dot_general x9, matrix products: 14.3 us -> 23 us  [dot_nt(): lax.dot_general(a, b, (((1,), (1,)), ((), ())), preferred_element_type=f32)]
    add x11 -> x4, other arithmetic: 9.64 us -> 2.12 us  [the longest x1 1.08 us: shards(): attn_outs = pick_seq(attn_mine)(0) + sum((g.astype(f32) for g in attn_sent))]
    convert_element_type x5 -> x4, other arithmetic: 2.11 us -> 9 us  [step(): self.keep = (wide(self.keep[:half]) + wide(self.got[:half])).astype(bf16)]
    dot_general x15, matrix products: 22.1 us -> 28.9 us  [dot_tn(): lax.dot_general(a, b, (((0,), (0,)), ((), ())), preferred_element_type=f32)]
    convert_element_type x15 -> x11, other arithmetic: 5.12 us -> 11.8 us  [the longest x5 6.16 us: add(): self.part = (part.astype(f32) + self.got.astype(f32)).astype(bf16)]
    ppermute x15 -> x20, starting transfers between devices: 26.8 us -> 33.1 us  [send_seq(): lax.ppermute(piece_for(k), 'seq', perm_seq(count, k))]
  transfers between devices with their start and end apart: 86 -> 74, of which waited for: 28 -> 22; matrix products, arithmetic and copies ran while one was open for 16% -> 32% of each run, Pallas kernels for 9% -> 13%
where the time goes in v3:
time: 446 us; the launch traced here: 438 us
  waiting for transfers between devices  112 us (25%)
  matrix products  76 us (17%)
  starting transfers between devices  74.5 us (17%)
  other arithmetic  64.5 us (14%)
  Pallas kernels  61.2 us (14%)
  local copies, waits for them, and re-layouts  34.4 us (8%)
  between operations  16.4 us (4%)
    ppermute x8, waiting for transfers between devices, send(): self.got = lax.ppermute(self.part, 'seq', pairs)  41.4 us
    ppermute x20, starting transfers between devices, send_seq(): lax.ppermute(piece_for(k), 'seq', perm_seq(count, k))  33.1 us
    dot_general x15, matrix products, dot_tn(): lax.dot_general(a, b, (((0,), (0,)), ((), ())), preferred_element_type=f32)  28.9 us
    pallas_call x12, Pallas kernels, dma_moves(): pl.pallas_call(body, out_shape=[jax.ShapeDtypeStruct(s, a) for s, a in ou...  25.9 us
    ppermute x20, waiting for transfers between devices, send_seq(): lax.ppermute(piece_for(k), 'seq', perm_seq(count, k))  24.8 us
    ppermute x12, waiting for transfers between devices, hop(): self.got = lax.ppermute(send, 'dp', perm(count, self.left.pop()))  24.1 us
    dot_general x14, matrix products, dot(): lax.dot_general(a, b, (((1,), (0,)), ((), ())), preferred_element_type=f32)  24 us
    dot_general x9, matrix products, dot_nt(): lax.dot_general(a, b, (((1,), (1,)), ((), ())), preferred_element_type=f32)  23 us
  transfers between devices with their start and end apart: 74, of which 22 were waited for; matrix products, arithmetic and copies ran while one was open for 32% of the time, Pallas kernels for 13%

profile of v3, /device:TPU:0, one launch (start us, length us, event | category | flops | bytes accessed | tf_op | source)
XLA Modules:
  0.0 438.5 jit_solution(11727757119356497601)
XLA Ops:
  12.2 5.1 %collective-permute-start.4 = (bf16[24,2432]{1,0:T(8,128)(2,1)S(1)}, bf16[24,2432]{1,0:T(8,128)(2,1)S(1)}, u32[]{:S(2)}, u32[]{:S(2)}) collective-permute-start(bf16[24,2432]{1,0:T(8,128)(2,1)S(1)} %fusion.110.refs_0_), channel_id=1, source_target_pairs={{0,3},{1,2},{2,1},{3,0},{4,7},{5,6},{6,5},{7,4},{8,11},{9,10},{10,... | collective-permute-start | bytes 350216 | tf_op jit(solution)/shard_map/ppermute | solution.py:144
  20.7 4.0 collective-permute-start
  32.4 7.7 %collective-permute-done.5.refs_1_ = bf16[96,2432]{1,0:T(8,128)(2,1)S(1)} collective-permute-done((bf16[96,2432]{1,0:T(8,128)(2,1)S(1)}, bf16[96,2432]{1,0:T(8,128)(2,1)S(1)}, u32[]{:S(2)}, u32[]{:S(2)}) %collective-permute-start.5) | collective-permute-done | bytes 466976 | tf_op jit(solution)/shard_map/ppermute | solution.py:155
  44.2 3.8 collective-permute-start.14
  63.9 4.1 convolution_convert_fusion.5.kv_ref
  76.8 12.4 %collective-permute-done.15 = bf16[256,896]{1,0:T(8,128)(2,1)} collective-permute-done((bf16[256,896]{1,0:T(8,128)(2,1)}, bf16[256,896]{1,0:T(8,128)(2,1)}, u32[]{:S(2)}, u32[]{:S(2)}) %collective-permute-start.15) | collective-permute-done | bytes 458784 | tf_op jit(solution)/shard_map/ppermute | solution.py:226
  91.2 10.6 %shard_map.275 = (bf16[512,768]{1,0:T(8,128)(2,1)S(1)}, bf16[8,512,384]{2,1,0:T(8,128)(2,1)S(1)}) custom-call(bf16[512,768]{1,0:T(8,128)(2,1)S(1)} %convolution_convert_fusion.15.q_ref, bf16[768,1536]{1,0:T(8,128)(2,1)S(1)} %convolution_convert_fusion.5.kv_ref, f32[512,1]{1,0:T(8,128)S(1)} %copy.62.q_seg_ref, f32[1,768]{1,0:T(1,128)S(1)} %or_select_fusion.k_seg_ref), custom_call_target="tpu_custom_call" | custom-call | flops 603979776 | bytes 7077888 | tf_op jit(solution)/shard_map/pallas_call | solution.py:390
  116.0 18.3 %collective-permute-done.23 = bf16[256,896]{1,0:T(8,128)(2,1)S(1)} collective-permute-done((bf16[256,896]{1,0:T(8,128)(2,1)}, bf16[256,896]{1,0:T(8,128)(2,1)S(1)}, u32[]{:S(2)}, u32[]{:S(2)}) %collective-permute-start.23) | collective-permute-done | bytes 458784 | tf_op jit(solution)/shard_map/ppermute | solution.py:226
  168.4 3.4 fusion.20
  178.8 7.8 %collective-permute-done.36.refs_1_ = bf16[128,768]{1,0:T(8,128)(2,1)S(1)} collective-permute-done((bf16[128,768]{1,0:T(8,128)(2,1)}, bf16[128,768]{1,0:T(8,128)(2,1)S(1)}, u32[]{:S(2)}, u32[]{:S(2)}) %collective-permute-start.36) | collective-permute-done | bytes 196640 | tf_op jit(solution)/shard_map/ppermute | solution.py:144
  192.8 8.0 %collective-permute-done.38.refs_2_ = bf16[256,768]{1,0:T(8,128)(2,1)S(1)} collective-permute-done((bf16[256,768]{1,0:T(8,128)(2,1)S(1)}, bf16[256,768]{1,0:T(8,128)(2,1)S(1)}, u32[]{:S(2)}, u32[]{:S(2)}) %collective-permute-start.38) | collective-permute-done | bytes 393248 | tf_op jit(solution)/shard_map/ppermute | solution.py:155
  202.2 5.0 %fusion = f32[512,768]{1,0:T(8,128)} fusion(bf16[768,3072]{1,0:T(8,128)(2,1)} %all-gather.2.cloned.1.call-done, bf16[512,1024]{0,1:T(8,128)(2,1)S(1)} %copy-done.132, bf16[512,1024]{0,1:T(8,128)(2,1)S(1)} %copy-done.131), kind=kOutput, calls=%fused_computation.17 | convolution fusion | flops 1614807040 | bytes 6815744 | tf_op jit(solution)/shard_map/dot_general | solution.py:328
  221.9 3.8 collective-permute-done.35
  251.7 4.2 collective-permute-done.44
  261.1 4.9 %add_convert_fusion = (bf16[2,96,4096]{2,1,0:T(8,128)(2,1)}, bf16[2,96,4096]{2,1,0:T(8,128)(2,1)}) fusion(bf16[4,96,4096]{2,1,0:T(8,128)(2,1)} %collective-permute-done.45, bf16[4,96,4096]{2,1,0:T(8,128)(2,1)S(1)} %copy-done.11), kind=kLoop, calls=%fused_computation.7 | loop fusion | flops 6291456 | bytes 9437184 | tf_op jit(solution)/shard_map/convert_element_type | solution.py:201
  267.7 4.7 %shard_map.285 = (bf16[256,768]{1,0:T(8,128)(2,1)S(1)}, bf16[256,1536]{1,0:T(8,128)(2,1)S(1)}) custom-call(bf16[256,768]{1,0:T(8,128)(2,1)S(1)} %convolution_convert_fusion.23.q_ref, bf16[256,1536]{1,0:T(8,128)(2,1)S(1)} %copy-done.21, bf16[12,256,256]{2,1,0:T(8,128)(2,1)S(1)} %copy-done.15, bf16[256,768]{1,0:T(8,128)(2,1)S(1)} %get-tuple-element.237.grad_ref), custom_call_target="tpu_custom_call" | custom-call | flops 402653184 | bytes 4325376 | tf_op jit(solution)/shard_map/pallas_call | solution.py:453
  301.5 7.5 %collective-permute-done.48 = bf16[2,96,4096]{2,1,0:T(8,128)(2,1)} collective-permute-done((bf16[2,96,4096]{2,1,0:T(8,128)(2,1)}, bf16[2,96,4096]{2,1,0:T(8,128)(2,1)}, u32[]{:S(2)}, u32[]{:S(2)}) %collective-permute-start.48) | collective-permute-done | bytes 1572896 | tf_op jit(solution)/shard_map/ppermute | solution.py:195
  313.3 13.7 %shard_map.287 = (bf16[512,768]{1,0:T(8,128)(2,1)S(1)}, bf16[768,1536]{1,0:T(8,128)(2,1)S(1)}) custom-call(bf16[512,768]{1,0:T(8,128)(2,1)S(1)} %copy-done.9, bf16[768,1536]{1,0:T(8,128)(2,1)S(1)} %convolution_convert_fusion.5.kv_ref, bf16[8,512,384]{2,1,0:T(8,128)(2,1)S(1)} %copy-done.5, bf16[512,768]{1,0:T(8,128)(2,1)S(1)} %copy-done.19), custom_call_target="tpu_custom_call" | custom-call | flops 1207959552 | bytes 10223616 | tf_op jit(solution)/shard_map/pallas_call | solution.py:453
  336.1 4.2 add_convert_fusion.3
  343.9 3.5 fusion.30
  349.7 4.0 collective-permute-start.57
  370.3 6.0 %collective-permute-done.51 = bf16[2,96,2304]{2,1,0:T(8,128)(2,1)} collective-permute-done((bf16[2,96,2304]{2,1,0:T(8,128)(2,1)}, bf16[2,96,2304]{2,1,0:T(8,128)(2,1)}, u32[]{:S(2)}, u32[]{:S(2)}) %collective-permute-start.51) | collective-permute-done | bytes 884768 | tf_op jit(solution)/shard_map/ppermute | solution.py:195
  381.3 7.6 %collective-permute-done.55 = bf16[1,96,2304]{2,1,0:T(8,128)(2,1)S(1)} collective-permute-done((bf16[1,96,2304]{2,1,0:T(8,128)(2,1)S(1)}, bf16[1,96,2304]{2,1,0:T(8,128)(2,1)S(1)}, u32[]{:S(2)}, u32[]{:S(2)}) %collective-permute-start.55) | collective-permute-done | bytes 442400 | tf_op jit(solution)/shard_map/ppermute | solution.py:195
  418.9 8.5 %collective-permute-done.64 = bf16[24,3968]{1,0:T(8,128)(2,1)S(1)} collective-permute-done((bf16[24,3968]{1,0:T(8,128)(2,1)S(1)}, bf16[24,3968]{1,0:T(8,128)(2,1)S(1)}, u32[]{:S(2)}, u32[]{:S(2)}) %collective-permute-start.64) | collective-permute-done | bytes 190496 | tf_op jit(solution)/shard_map/ppermute | solution.py:144
  (558 shorter events, 259.1 us)
Async XLA Ops:
  7.2 155.1 %all-gather.2.cloned.1.call-start = ((), (), s32[]{:S(2)}) async-start(), calls=%async_computation.1 | async-start | bytes 4866048 | tf_op jit(solution)/shard_map/all_gather | solution.py:524
  10.4 385.7 %reduce-scatter.2.cloned.1.call-start = ((), (), s32[]{:S(2)}) async-start(), calls=%async_computation.2 | async-start | bytes 4866048 | tf_op jit(solution)/shard_map/reduce_scatter | solution.py:622
  20.7 31.3 %collective-permute-start = (bf16[128,896]{1,0:T(8,128)(2,1)}, bf16[128,896]{1,0:T(8,128)(2,1)}, u32[]{:S(2)}, u32[]{:S(2)}) collective-permute-start(bf16[128,896]{1,0:T(8,128)(2,1)} %get-tuple-element.230), channel_id=1, source_target_pairs={{0,1},{1,2},{2,3},{4,5},{5,6},{6,7},{8,9},{9,10},{10,11},{12,13},{... | collective-permute-start | bytes 688136 | tf_op jit(solution)/shard_map/ppermute | solution.py:528
  24.7 27.4 %collective-permute-start.1 = (bf16[128,896]{1,0:T(8,128)(2,1)}, bf16[128,896]{1,0:T(8,128)(2,1)}, u32[]{:S(2)}, u32[]{:S(2)}) collective-permute-start(bf16[128,896]{1,0:T(8,128)(2,1)} %get-tuple-element.231), channel_id=1, source_target_pairs={{1,0},{2,1},{3,2},{5,4},{6,5},{7,6},{9,8},{10,9},{11,10},{13,12},{... | collective-permute-start | bytes 688136 | tf_op jit(solution)/shard_map/ppermute | solution.py:529
  44.2 25.8 %collective-permute-start.14 = (bf16[24,3840]{1,0:T(8,128)(2,1)S(1)}, bf16[24,3840]{1,0:T(8,128)(2,1)S(1)}, u32[]{:S(2)}, u32[]{:S(2)}) collective-permute-start(bf16[24,3840]{1,0:T(8,128)(2,1)S(1)} %constant_dynamic-update-slice_fusion.refs_0_), channel_id=1, source_target_pairs={{0,3},{1,2},{2,1},{3,0},{4,7},{5,6},{6,5},{7,4},{8,11},{9,10},{10,... | collective-permute-start | bytes 552968 | tf_op jit(solution)/shard_map/ppermute | solution.py:144
  58.3 30.9 %collective-permute-start.15 = (bf16[256,896]{1,0:T(8,128)(2,1)}, bf16[256,896]{1,0:T(8,128)(2,1)}, u32[]{:S(2)}, u32[]{:S(2)}) collective-permute-start(bf16[256,896]{1,0:T(8,128)(2,1)} %convolution_convert_fusion.16), channel_id=1, source_target_pairs={{0,1},{1,0},{2,3},{3,2},{4,5},{5,4},{6,7},{7,6},{8,9},{9,8},{10,11... | collective-permute-start | bytes 1376264 | tf_op jit(solution)/shard_map/ppermute | solution.py:226
  73.6 30.7 %collective-permute-start.16 = (bf16[96,3840]{1,0:T(8,128)(2,1)}, bf16[96,3840]{1,0:T(8,128)(2,1)}, u32[]{:S(2)}, u32[]{:S(2)}) collective-permute-start(bf16[96,3840]{1,0:T(8,128)(2,1)} %bitcast.21.refs_0_), channel_id=1, source_target_pairs={{0,8},{4,20},{8,0},{12,28},{16,24},{20,4},{24,16},{28,12},{1,9},{5... | collective-permute-start | bytes 2211848 | tf_op jit(solution)/shard_map/ppermute | solution.py:155
  75.0 39.1 %collective-permute-start.17 = (bf16[96,3840]{1,0:T(8,128)(2,1)}, bf16[96,3840]{1,0:T(8,128)(2,1)}, u32[]{:S(2)}, u32[]{:S(2)}) collective-permute-start(bf16[96,3840]{1,0:T(8,128)(2,1)} %bitcast.21.refs_0_), channel_id=1, source_target_pairs={{0,16},{4,12},{8,24},{12,4},{16,0},{20,28},{24,8},{28,20},{1,17},{... | collective-permute-start | bytes 2211848 | tf_op jit(solution)/shard_map/ppermute | solution.py:155
  109.8 24.4 %collective-permute-start.23 = (bf16[256,896]{1,0:T(8,128)(2,1)}, bf16[256,896]{1,0:T(8,128)(2,1)S(1)}, u32[]{:S(2)}, u32[]{:S(2)}) collective-permute-start(bf16[256,896]{1,0:T(8,128)(2,1)} %add_convert_fusion.15), channel_id=1, source_target_pairs={{0,2},{1,3},{2,0},{3,1},{4,6},{5,7},{6,4},{7,5},{8,10},{9,11},{10,... | collective-permute-start | bytes 1376264 | tf_op jit(solution)/shard_map/ppermute | solution.py:226
  109.8 25.5 %collective-permute-start.19 = (bf16[96,3840]{1,0:T(8,128)(2,1)}, bf16[96,3840]{1,0:T(8,128)(2,1)S(1)}, u32[]{:S(2)}, u32[]{:S(2)}) collective-permute-start(bf16[96,3840]{1,0:T(8,128)(2,1)} %bitcast.21.refs_0_), channel_id=1, source_target_pairs={{0,4},{4,0},{8,12},{12,8},{16,20},{20,16},{24,28},{28,24},{1,5},{5... | collective-permute-start | bytes 2211848 | tf_op jit(solution)/shard_map/ppermute | solution.py:155
  109.9 38.1 %collective-permute-start.27 = (bf16[24,4096]{1,0:T(8,128)(2,1)}, bf16[24,4096]{1,0:T(8,128)(2,1)S(1)}, u32[]{:S(2)}, u32[]{:S(2)}) collective-permute-start(bf16[24,4096]{1,0:T(8,128)(2,1)} %get-tuple-element.126), channel_id=1, source_target_pairs={{0,3},{1,2},{2,1},{3,0},{4,7},{5,6},{6,5},{7,4},{8,11},{9,10},{10,... | collective-permute-start | bytes 589832 | tf_op jit(solution)/shard_map/ppermute | solution.py:144
  150.5 50.5 %collective-permute-start.29 = (bf16[96,4096]{1,0:T(8,128)(2,1)}, bf16[96,4096]{1,0:T(8,128)(2,1)}, u32[]{:S(2)}, u32[]{:S(2)}) collective-permute-start(bf16[96,4096]{1,0:T(8,128)(2,1)} %bitcast.39.refs_0_), channel_id=1, source_target_pairs={{0,16},{4,12},{8,24},{12,4},{16,0},{20,28},{24,8},{28,20},{1,17},{... | collective-permute-start | bytes 2359304 | tf_op jit(solution)/shard_map/ppermute | solution.py:155
  174.0 27.3 %collective-permute-start.30 = (bf16[96,4096]{1,0:T(8,128)(2,1)}, bf16[96,4096]{1,0:T(8,128)(2,1)}, u32[]{:S(2)}, u32[]{:S(2)}) collective-permute-start(bf16[96,4096]{1,0:T(8,128)(2,1)} %collective-permute-done.28.refs_1_), channel_id=1, source_target_pairs={{0,16},{4,12},{8,24},{12,4},{16,0},{20,28},{24,8},{28,20},{1,17},{... | collective-permute-start | bytes 2359304 | tf_op jit(solution)/shard_map/ppermute | solution.py:155
  256.0 38.5 %collective-permute-start.47 = (bf16[256,768]{1,0:T(8,128)(2,1)}, bf16[256,768]{1,0:T(8,128)(2,1)}, u32[]{:S(2)}, u32[]{:S(2)}) collective-permute-start(bf16[256,768]{1,0:T(8,128)(2,1)} %convolution_convert_fusion.19), channel_id=1, source_target_pairs={{0,1},{1,0},{2,3},{3,2},{4,5},{5,4},{6,7},{7,6},{8,9},{9,8},{10,11... | collective-permute-start | bytes 1179656 | tf_op jit(solution)/shard_map/ppermute | solution.py:226
  274.0 57.0 %collective-permute-start.59 = (bf16[256,768]{1,0:T(8,128)(2,1)}, bf16[256,768]{1,0:T(8,128)(2,1)}, u32[]{:S(2)}, u32[]{:S(2)}) collective-permute-start(bf16[256,768]{1,0:T(8,128)(2,1)} %fusion.44), channel_id=1, source_target_pairs={{0,1},{1,0},{2,3},{3,2},{4,5},{5,4},{6,7},{7,6},{8,9},{9,8},{10,11... | collective-permute-start | bytes 1179656 | tf_op jit(solution)/shard_map/ppermute | solution.py:226
  275.7 33.4 %collective-permute-start.48 = (bf16[2,96,4096]{2,1,0:T(8,128)(2,1)}, bf16[2,96,4096]{2,1,0:T(8,128)(2,1)}, u32[]{:S(2)}, u32[]{:S(2)}) collective-permute-start(bf16[2,96,4096]{2,1,0:T(8,128)(2,1)} %get-tuple-element.200), channel_id=1, source_target_pairs={{0,16},{4,12},{8,24},{12,4},{16,0},{20,28},{24,8},{28,20},{1,17},{... | collective-permute-start | bytes 4718600 | tf_op jit(solution)/shard_map/ppermute | solution.py:195
  284.4 48.6 %collective-permute-start.70 = (bf16[1,256,768]{2,1,0:T(8,128)(2,1)}, bf16[1,256,768]{2,1,0:T(8,128)(2,1)}, u32[]{:S(2)}, u32[]{:S(2)}) collective-permute-start(bf16[1,256,768]{2,1,0:T(8,128)(2,1)} %get-tuple-element.220), channel_id=1, source_target_pairs={{0,8},{4,20},{8,0},{12,28},{16,24},{20,4},{24,16},{28,12},{1,9},{5... | collective-permute-start | bytes 1179656 | tf_op jit(solution)/shard_map/ppermute | solution.py:195
  294.5 41.6 %collective-permute-start.52 = (bf16[4,96,3968]{2,1,0:T(8,128)(2,1)}, bf16[4,96,3968]{2,1,0:T(8,128)(2,1)}, u32[]{:S(2)}, u32[]{:S(2)}) collective-permute-start(bf16[4,96,3968]{2,1,0:T(8,128)(2,1)} %get-tuple-element.165), channel_id=1, source_target_pairs={{0,4},{4,0},{8,12},{12,8},{16,20},{20,16},{24,28},{28,24},{1,5},{5... | collective-permute-start | bytes 9142280 | tf_op jit(solution)/shard_map/ppermute | solution.py:195
  311.6 23.4 %collective-permute-start.66 = (bf16[1,96,4096]{2,1,0:T(8,128)(2,1)S(1)}, bf16[1,96,4096]{2,1,0:T(8,128)(2,1)S(1)}, u32[]{:S(2)}, u32[]{:S(2)}) collective-permute-start(bf16[1,96,4096]{2,1,0:T(8,128)(2,1)S(1)} %get-tuple-element.212), channel_id=1, source_target_pairs={{0,8},{4,20},{8,0},{12,28},{16,24},{20,4},{24,16},{28,12},{1,9},{5... | collective-permute-start | bytes 2359304 | tf_op jit(solution)/shard_map/ppermute | solution.py:195
  333.0 63.2 %collective-permute-start.60 = (bf16[256,768]{1,0:T(8,128)(2,1)}, bf16[256,768]{1,0:T(8,128)(2,1)}, u32[]{:S(2)}, u32[]{:S(2)}) collective-permute-start(bf16[256,768]{1,0:T(8,128)(2,1)} %add_convert_fusion.21), channel_id=1, source_target_pairs={{0,2},{1,3},{2,0},{3,1},{4,6},{5,7},{6,4},{7,5},{8,10},{9,11},{10,... | collective-permute-start | bytes 1179656 | tf_op jit(solution)/shard_map/ppermute | solution.py:226
  343.2 33.1 %collective-permute-start.51 = (bf16[2,96,2304]{2,1,0:T(8,128)(2,1)}, bf16[2,96,2304]{2,1,0:T(8,128)(2,1)}, u32[]{:S(2)}, u32[]{:S(2)}) collective-permute-start(bf16[2,96,2304]{2,1,0:T(8,128)(2,1)} %get-tuple-element.211), channel_id=1, source_target_pairs={{0,16},{4,12},{8,24},{12,4},{16,0},{20,28},{24,8},{28,20},{1,17},{... | collective-permute-start | bytes 2654216 | tf_op jit(solution)/shard_map/ppermute | solution.py:195
  365.3 25.6 %collective-permute-start.71 = (bf16[128,768]{1,0:T(8,128)(2,1)S(1)}, bf16[128,768]{1,0:T(8,128)(2,1)S(1)}, u32[]{:S(2)}, u32[]{:S(2)}) collective-permute-start(bf16[128,768]{1,0:T(8,128)(2,1)S(1)} %copy-done.78), channel_id=1, source_target_pairs={{0,2},{1,3},{2,0},{3,1},{4,6},{5,7},{6,4},{7,5},{8,10},{9,11},{10,... | collective-permute-start | bytes 589832 | tf_op jit(solution)/shard_map/ppermute | solution.py:144
  368.5 42.4 %collective-permute-start.69 = (bf16[24,4096]{1,0:T(8,128)(2,1)}, bf16[24,4096]{1,0:T(8,128)(2,1)}, u32[]{:S(2)}, u32[]{:S(2)}) collective-permute-start(bf16[24,4096]{1,0:T(8,128)(2,1)} %get-tuple-element.232), channel_id=1, source_target_pairs={{0,3},{1,2},{2,1},{3,0},{4,7},{5,6},{6,5},{7,4},{8,11},{9,10},{10,... | collective-permute-start | bytes 589832 | tf_op jit(solution)/shard_map/ppermute | solution.py:144
  376.3 36.7 %collective-permute-start.68 = (bf16[24,4096]{1,0:T(8,128)(2,1)}, bf16[24,4096]{1,0:T(8,128)(2,1)}, u32[]{:S(2)}, u32[]{:S(2)}) collective-permute-start(bf16[24,4096]{1,0:T(8,128)(2,1)} %get-tuple-element.233), channel_id=1, source_target_pairs={{0,2},{1,3},{2,0},{3,1},{4,6},{5,7},{6,4},{7,5},{8,10},{9,11},{10,... | collective-permute-start | bytes 589832 | tf_op jit(solution)/shard_map/ppermute | solution.py:144
  (183 other events, 1939.4 us)
Sparse Core Ops, SparseCore 0:
  11.5 77.7 all-gather.1
  244.2 118.8 reduce-scatter.1

commit v4 on v3

--- a/solution.py
+++ b/solution.py
@@ -564,7 +564,7 @@
     wave(second_held, 0)
     sum_kv.add(light_kv)
     light_mixed, light_probs = attend(
-        gate(light_q, second_z, sum_kv.part), light_kv, seg_f, key_seg, L_HEAD, WINDOW, WINDOW, bf16
+        gate(light_q, second_z), light_kv, seg_f, key_seg, L_HEAD, WINDOW, WINDOW, bf16
     )
     q_rows = dot(table_q, normed).astype(bf16)
     q_seg = jnp.sum(table_q.astype(f32) * seg_f[None], axis=1)
@@ -700,7 +700,7 @@
         light_q,
         light_kv,
         light_probs,
-        gate(mixed_grad, sum_attn.keep, kv_send, out_part, *[s.keep for s in sum_heavy]),
+        gate(mixed_grad, sum_attn.keep, kv_send, out_part),
         L_HEAD,
         WINDOW,
         WINDOW,

time: 446 us -> 426 us (0.955)
  waiting for transfers between devices: 112 us -> 93.3 us
  starting transfers between devices: 74.5 us -> 82.7 us
    ppermute x8, waiting for transfers between devices: 41.4 us -> 29.4 us  [send(): self.got = lax.ppermute(self.part, 'seq', pairs)]
    ppermute x20, starting transfers between devices: 33.1 us -> 44.2 us  [send_seq(): lax.ppermute(piece_for(k), 'seq', perm_seq(count, k))]
    ppermute x20, waiting for transfers between devices: 24.8 us -> 18 us  [send_seq(): lax.ppermute(piece_for(k), 'seq', perm_seq(count, k))]
    unnamed x270 -> x280, local copies, waits for them, and re-layouts: 20.2 us -> 17.8 us
    convert_element_type x4 -> x6, other arithmetic: 9 us -> 10.8 us  [step(): self.keep = (wide(self.keep[:half]) + wide(self.got[:half])).astype(bf16)]
  transfers between devices with their start and end apart: 74 -> 74, of which waited for: 22 -> 18; matrix products, arithmetic and copies ran while one was open for 32% -> 32% of each run, Pallas kernels for 13% -> 14%
where the time goes in v4:
time: 426 us; the launch traced here: 420 us
  waiting for transfers between devices  93.3 us (22%)
  starting transfers between devices  82.7 us (19%)
  matrix products  73.1 us (17%)
  other arithmetic  62.4 us (15%)
  Pallas kernels  60.6 us (14%)
  local copies, waits for them, and re-layouts  31.4 us (7%)
  between operations  16.6 us (4%)
    ppermute x20, starting transfers between devices, send_seq(): lax.ppermute(piece_for(k), 'seq', perm_seq(count, k))  44.2 us
    ppermute x8, waiting for transfers between devices, send(): self.got = lax.ppermute(self.part, 'seq', pairs)  29.4 us
    dot_general x14, matrix products, dot(): lax.dot_general(a, b, (((1,), (0,)), ((), ())), preferred_element_type=f32)  25.5 us
    dot_general x15, matrix products, dot_tn(): lax.dot_general(a, b, (((0,), (0,)), ((), ())), preferred_element_type=f32)  25.4 us
    pallas_call x12, Pallas kernels, dma_moves(): pl.pallas_call(body, out_shape=[jax.ShapeDtypeStruct(s, a) for s, a in ou...  25.3 us
    ppermute x28, waiting for transfers between devices, wave(): lax.ppermute(pieces[label], 'dp', perm(count, stages[stage]))  23.8 us
    dot_general x9, matrix products, dot_nt(): lax.dot_general(a, b, (((1,), (1,)), ((), ())), preferred_element_type=f32)  22.2 us
    ppermute x12, waiting for transfers between devices, hop(): self.got = lax.ppermute(send, 'dp', perm(count, self.left.pop()))  21.8 us
  transfers between devices with their start and end apart: 74, of which 18 were waited for; matrix products, arithmetic and copies ran while one was open for 32% of the time, Pallas kernels for 14%

profile of v4, /device:TPU:0, one launch (start us, length us, event | category | flops | bytes accessed | tf_op | source)
XLA Modules:
  0.0 420.1 jit_solution(7436380183118297560)
XLA Ops:
  12.2 5.1 %collective-permute-start.4 = (bf16[24,2432]{1,0:T(8,128)(2,1)S(1)}, bf16[24,2432]{1,0:T(8,128)(2,1)S(1)}, u32[]{:S(2)}, u32[]{:S(2)}) collective-permute-start(bf16[24,2432]{1,0:T(8,128)(2,1)S(1)} %fusion.110.refs_0_), channel_id=1, source_target_pairs={{0,3},{1,2},{2,1},{3,0},{4,7},{5,6},{6,5},{7,4},{8,11},{9,10},{10,... | collective-permute-start | bytes 350216 | tf_op jit(solution)/shard_map/ppermute | solution.py:144
  32.4 7.7 %collective-permute-done.5.refs_1_ = bf16[96,2432]{1,0:T(8,128)(2,1)S(1)} collective-permute-done((bf16[96,2432]{1,0:T(8,128)(2,1)S(1)}, bf16[96,2432]{1,0:T(8,128)(2,1)S(1)}, u32[]{:S(2)}, u32[]{:S(2)}) %collective-permute-start.5) | collective-permute-done | bytes 466976 | tf_op jit(solution)/shard_map/ppermute | solution.py:155
  44.3 3.8 collective-permute-start.14
  63.5 4.2 convolution_convert_fusion.5.kv_ref
  80.1 10.8 %shard_map.275 = (bf16[512,768]{1,0:T(8,128)(2,1)S(1)}, bf16[8,512,384]{2,1,0:T(8,128)(2,1)S(1)}) custom-call(bf16[512,768]{1,0:T(8,128)(2,1)S(1)} %convolution_convert_fusion.15.q_ref, bf16[768,1536]{1,0:T(8,128)(2,1)S(1)} %convolution_convert_fusion.5.kv_ref, f32[512,1]{1,0:T(8,128)S(1)} %copy.62.q_seg_ref, f32[1,768]{1,0:T(1,128)S(1)} %or_select_fusion.k_seg_ref), custom_call_target="tpu_custom_call" | custom-call | flops 603979776 | bytes 7077888 | tf_op jit(solution)/shard_map/pallas_call | solution.py:390
  99.1 3.6 collective-permute-done.17.refs_3_
  102.7 19.2 %collective-permute-done.23 = bf16[256,896]{1,0:T(8,128)(2,1)S(1)} collective-permute-done((bf16[256,896]{1,0:T(8,128)(2,1)S(1)}, bf16[256,896]{1,0:T(8,128)(2,1)S(1)}, u32[]{:S(2)}, u32[]{:S(2)}) %collective-permute-start.23) | collective-permute-done | bytes 458784 | tf_op jit(solution)/shard_map/ppermute | solution.py:226
  131.4 4.3 %collective-permute-done.26.refs_2_ = bf16[24,4096]{1,0:T(8,128)(2,1)S(1)} collective-permute-done((bf16[24,4096]{1,0:T(8,128)(2,1)S(1)}, bf16[24,4096]{1,0:T(8,128)(2,1)S(1)}, u32[]{:S(2)}, u32[]{:S(2)}) %collective-permute-start.26) | collective-permute-done | bytes 196640 | tf_op jit(solution)/shard_map/ppermute | solution.py:144
  154.1 3.6 fusion.20
  165.0 7.1 %collective-permute-done.36.refs_1_ = bf16[128,768]{1,0:T(8,128)(2,1)S(1)} collective-permute-done((bf16[128,768]{1,0:T(8,128)(2,1)}, bf16[128,768]{1,0:T(8,128)(2,1)S(1)}, u32[]{:S(2)}, u32[]{:S(2)}) %collective-permute-start.36) | collective-permute-done | bytes 196640 | tf_op jit(solution)/shard_map/ppermute | solution.py:144
  177.3 8.4 %collective-permute-done.38.refs_2_ = bf16[256,768]{1,0:T(8,128)(2,1)S(1)} collective-permute-done((bf16[256,768]{1,0:T(8,128)(2,1)S(1)}, bf16[256,768]{1,0:T(8,128)(2,1)S(1)}, u32[]{:S(2)}, u32[]{:S(2)}) %collective-permute-start.38) | collective-permute-done | bytes 393248 | tf_op jit(solution)/shard_map/ppermute | solution.py:155
  187.2 5.0 %fusion = f32[512,768]{1,0:T(8,128)} fusion(bf16[768,3072]{1,0:T(8,128)(2,1)} %all-gather.2.cloned.1.call-done, bf16[512,1024]{0,1:T(8,128)(2,1)S(1)} %copy-done.137, bf16[512,1024]{0,1:T(8,128)(2,1)S(1)} %copy-done.136), kind=kOutput, calls=%fused_computation.17 | convolution fusion | flops 1614807040 | bytes 6815744 | tf_op jit(solution)/shard_map/dot_general | solution.py:328
  206.7 4.4 %collective-permute-done.35 = bf16[256,768]{1,0:T(8,128)(2,1)S(1)} collective-permute-done((bf16[256,768]{1,0:T(8,128)(2,1)S(1)}, bf16[256,768]{1,0:T(8,128)(2,1)S(1)}, u32[]{:S(2)}, u32[]{:S(2)}) %collective-permute-start.35) | collective-permute-done | bytes 393248 | tf_op jit(solution)/shard_map/ppermute | solution.py:226
  245.6 4.8 %add_convert_fusion = (bf16[2,96,4096]{2,1,0:T(8,128)(2,1)}, bf16[2,96,4096]{2,1,0:T(8,128)(2,1)}) fusion(bf16[4,96,4096]{2,1,0:T(8,128)(2,1)} %collective-permute-done.45, bf16[4,96,4096]{2,1,0:T(8,128)(2,1)S(1)} %copy-done.10), kind=kLoop, calls=%fused_computation.7 | loop fusion | flops 6291456 | bytes 9437184 | tf_op jit(solution)/shard_map/convert_element_type | solution.py:201
  252.7 4.7 %shard_map.285 = (bf16[256,768]{1,0:T(8,128)(2,1)S(1)}, bf16[256,1536]{1,0:T(8,128)(2,1)S(1)}) custom-call(bf16[256,768]{1,0:T(8,128)(2,1)S(1)} %copy-done.25, bf16[256,1536]{1,0:T(8,128)(2,1)S(1)} %copy-done.19, bf16[12,256,256]{2,1,0:T(8,128)(2,1)S(1)} %copy-done.14, bf16[256,768]{1,0:T(8,128)(2,1)S(1)} %get-tuple-element.237.grad_ref), custom_call_target="tpu_custom_call" | custom-call | flops 402653184 | bytes 4325376 | tf_op jit(solution)/shard_map/pallas_call | solution.py:453
  272.9 3.6 shard_map.286
  281.0 13.7 %shard_map.287 = (bf16[512,768]{1,0:T(8,128)(2,1)S(1)}, bf16[768,1536]{1,0:T(8,128)(2,1)S(1)}) custom-call(bf16[512,768]{1,0:T(8,128)(2,1)S(1)} %copy-done.8, bf16[768,1536]{1,0:T(8,128)(2,1)S(1)} %copy-done.1, bf16[8,512,384]{2,1,0:T(8,128)(2,1)S(1)} %copy-done.4, bf16[512,768]{1,0:T(8,128)(2,1)S(1)} %convolution_convert_fusion.14.grad_ref), custom_call_target="tpu_custom_call" | custom-call | flops 1207959552 | bytes 10223616 | tf_op jit(solution)/shard_map/pallas_call | solution.py:453
  334.9 4.9 %collective-permute-start.71 = (bf16[128,768]{1,0:T(8,128)(2,1)S(1)}, bf16[128,768]{1,0:T(8,128)(2,1)S(1)}, u32[]{:S(2)}, u32[]{:S(2)}) collective-permute-start(bf16[128,768]{1,0:T(8,128)(2,1)S(1)} %copy-done.79), channel_id=1, source_target_pairs={{0,2},{1,3},{2,0},{3,1},{4,6},{5,7},{6,4},{7,5},{8,10},{9,11},{10,... | collective-permute-start | bytes 589832 | tf_op jit(solution)/shard_map/ppermute | solution.py:144
  343.1 3.5 collective-permute-done.51
  348.5 4.1 collective-permute-start.68
  352.6 10.9 %collective-permute-done.49 = bf16[2,96,2304]{2,1,0:T(8,128)(2,1)S(1)} collective-permute-done((bf16[2,96,2304]{2,1,0:T(8,128)(2,1)S(1)}, bf16[2,96,2304]{2,1,0:T(8,128)(2,1)S(1)}, u32[]{:S(2)}, u32[]{:S(2)}) %collective-permute-start.49) | collective-permute-done | bytes 884768 | tf_op jit(solution)/shard_map/ppermute | solution.py:195
  363.5 5.5 %collective-permute-start.67 = (bf16[24,4096]{1,0:T(8,128)(2,1)}, bf16[24,4096]{1,0:T(8,128)(2,1)}, u32[]{:S(2)}, u32[]{:S(2)}) collective-permute-start(bf16[24,4096]{1,0:T(8,128)(2,1)} %get-tuple-element.233), channel_id=1, source_target_pairs={{0,2},{1,3},{2,0},{3,1},{4,6},{5,7},{6,4},{7,5},{8,10},{9,11},{10,... | collective-permute-start | bytes 589832 | tf_op jit(solution)/shard_map/ppermute | solution.py:144
  370.2 7.4 %collective-permute-done.53 = bf16[1,96,2304]{2,1,0:T(8,128)(2,1)S(1)} collective-permute-done((bf16[1,96,2304]{2,1,0:T(8,128)(2,1)S(1)}, bf16[1,96,2304]{2,1,0:T(8,128)(2,1)S(1)}, u32[]{:S(2)}, u32[]{:S(2)}) %collective-permute-start.53) | collective-permute-done | bytes 442400 | tf_op jit(solution)/shard_map/ppermute | solution.py:195
  405.6 3.5 collective-permute-done.62
  (568 shorter events, 249.6 us)
Async XLA Ops:
  7.2 140.9 %all-gather.2.cloned.1.call-start = ((), (), s32[]{:S(2)}) async-start(), calls=%async_computation.1 | async-start | bytes 4866048 | tf_op jit(solution)/shard_map/all_gather | solution.py:524
  10.4 374.6 %reduce-scatter.2.cloned.1.call-start = ((), (), s32[]{:S(2)}) async-start(), calls=%async_computation.2 | async-start | bytes 4866048 | tf_op jit(solution)/shard_map/reduce_scatter | solution.py:622
  20.7 31.4 %collective-permute-start = (bf16[128,896]{1,0:T(8,128)(2,1)}, bf16[128,896]{1,0:T(8,128)(2,1)S(1)}, u32[]{:S(2)}, u32[]{:S(2)}) collective-permute-start(bf16[128,896]{1,0:T(8,128)(2,1)} %get-tuple-element.230), channel_id=1, source_target_pairs={{0,1},{1,2},{2,3},{4,5},{5,6},{6,7},{8,9},{9,10},{10,11},{12,13},{... | collective-permute-start | bytes 688136 | tf_op jit(solution)/shard_map/ppermute | solution.py:528
  24.0 28.1 %collective-permute-start.1 = (bf16[128,896]{1,0:T(8,128)(2,1)}, bf16[128,896]{1,0:T(8,128)(2,1)}, u32[]{:S(2)}, u32[]{:S(2)}) collective-permute-start(bf16[128,896]{1,0:T(8,128)(2,1)} %get-tuple-element.231), channel_id=1, source_target_pairs={{1,0},{2,1},{3,2},{5,4},{6,5},{7,6},{9,8},{10,9},{11,10},{13,12},{... | collective-permute-start | bytes 688136 | tf_op jit(solution)/shard_map/ppermute | solution.py:529
  44.3 26.3 %collective-permute-start.14 = (bf16[24,3840]{1,0:T(8,128)(2,1)S(1)}, bf16[24,3840]{1,0:T(8,128)(2,1)S(1)}, u32[]{:S(2)}, u32[]{:S(2)}) collective-permute-start(bf16[24,3840]{1,0:T(8,128)(2,1)S(1)} %constant_dynamic-update-slice_fusion.refs_0_), channel_id=1, source_target_pairs={{0,3},{1,2},{2,1},{3,0},{4,7},{5,6},{6,5},{7,4},{8,11},{9,10},{10,... | collective-permute-start | bytes 552968 | tf_op jit(solution)/shard_map/ppermute | solution.py:144
  78.5 44.6 %collective-permute-start.18 = (bf16[96,3840]{1,0:T(8,128)(2,1)}, bf16[96,3840]{1,0:T(8,128)(2,1)S(1)}, u32[]{:S(2)}, u32[]{:S(2)}) collective-permute-start(bf16[96,3840]{1,0:T(8,128)(2,1)} %bitcast.21.refs_0_), channel_id=1, source_target_pairs={{0,4},{4,0},{8,12},{12,8},{16,20},{20,16},{24,28},{28,24},{1,5},{5... | collective-permute-start | bytes 2211848 | tf_op jit(solution)/shard_map/ppermute | solution.py:155
  93.5 28.4 %collective-permute-start.23 = (bf16[256,896]{1,0:T(8,128)(2,1)S(1)}, bf16[256,896]{1,0:T(8,128)(2,1)S(1)}, u32[]{:S(2)}, u32[]{:S(2)}) collective-permute-start(bf16[256,896]{1,0:T(8,128)(2,1)S(1)} %add_convert_fusion.15), channel_id=1, source_target_pairs={{0,2},{1,3},{2,0},{3,1},{4,6},{5,7},{6,4},{7,5},{8,10},{9,11},{10,... | collective-permute-start | bytes 1376264 | tf_op jit(solution)/shard_map/ppermute | solution.py:226
  94.8 40.9 %collective-permute-start.27 = (bf16[24,4096]{1,0:T(8,128)(2,1)S(1)}, bf16[24,4096]{1,0:T(8,128)(2,1)S(1)}, u32[]{:S(2)}, u32[]{:S(2)}) collective-permute-start(bf16[24,4096]{1,0:T(8,128)(2,1)S(1)} %copy-done.133), channel_id=1, source_target_pairs={{0,3},{1,2},{2,1},{3,0},{4,7},{5,6},{6,5},{7,4},{8,11},{9,10},{10,... | collective-permute-start | bytes 589832 | tf_op jit(solution)/shard_map/ppermute | solution.py:144
  99.1 24.0 %collective-permute-start.19 = (bf16[96,3840]{1,0:T(8,128)(2,1)}, bf16[96,3840]{1,0:T(8,128)(2,1)S(1)}, u32[]{:S(2)}, u32[]{:S(2)}) collective-permute-start(bf16[96,3840]{1,0:T(8,128)(2,1)} %collective-permute-done.15.refs_1_), channel_id=1, source_target_pairs={{0,4},{4,0},{8,12},{12,8},{16,20},{20,16},{24,28},{28,24},{1,5},{5... | collective-permute-start | bytes 2211848 | tf_op jit(solution)/shard_map/ppermute | solution.py:155
  102.7 21.9 %collective-permute-start.20 = (bf16[96,3840]{1,0:T(8,128)(2,1)S(1)}, bf16[96,3840]{1,0:T(8,128)(2,1)S(1)}, u32[]{:S(2)}, u32[]{:S(2)}) collective-permute-start(bf16[96,3840]{1,0:T(8,128)(2,1)S(1)} %collective-permute-done.16.refs_2_), channel_id=1, source_target_pairs={{0,4},{4,0},{8,12},{12,8},{16,20},{20,16},{24,28},{28,24},{1,5},{5... | collective-permute-start | bytes 2211848 | tf_op jit(solution)/shard_map/ppermute | solution.py:155
  137.3 48.5 %collective-permute-start.29 = (bf16[96,4096]{1,0:T(8,128)(2,1)S(1)}, bf16[96,4096]{1,0:T(8,128)(2,1)S(1)}, u32[]{:S(2)}, u32[]{:S(2)}) collective-permute-start(bf16[96,4096]{1,0:T(8,128)(2,1)S(1)} %bitcast.168), channel_id=1, source_target_pairs={{0,16},{4,12},{8,24},{12,4},{16,0},{20,28},{24,8},{28,20},{1,17},{... | collective-permute-start | bytes 2359304 | tf_op jit(solution)/shard_map/ppermute | solution.py:155
  160.0 26.1 %collective-permute-start.30 = (bf16[96,4096]{1,0:T(8,128)(2,1)}, bf16[96,4096]{1,0:T(8,128)(2,1)}, u32[]{:S(2)}, u32[]{:S(2)}) collective-permute-start(bf16[96,4096]{1,0:T(8,128)(2,1)} %collective-permute-done.28.refs_1_), channel_id=1, source_target_pairs={{0,16},{4,12},{8,24},{12,4},{16,0},{20,28},{24,8},{28,20},{1,17},{... | collective-permute-start | bytes 2359304 | tf_op jit(solution)/shard_map/ppermute | solution.py:155
  240.5 36.9 %collective-permute-start.47 = (bf16[256,768]{1,0:T(8,128)(2,1)}, bf16[256,768]{1,0:T(8,128)(2,1)}, u32[]{:S(2)}, u32[]{:S(2)}) collective-permute-start(bf16[256,768]{1,0:T(8,128)(2,1)} %convolution_convert_fusion.19), channel_id=1, source_target_pairs={{0,1},{1,0},{2,3},{3,2},{4,5},{5,4},{6,7},{7,6},{8,9},{9,8},{10,11... | collective-permute-start | bytes 1179656 | tf_op jit(solution)/shard_map/ppermute | solution.py:226
  259.0 44.9 %collective-permute-start.57 = (bf16[256,768]{1,0:T(8,128)(2,1)}, bf16[256,768]{1,0:T(8,128)(2,1)}, u32[]{:S(2)}, u32[]{:S(2)}) collective-permute-start(bf16[256,768]{1,0:T(8,128)(2,1)} %fusion.44), channel_id=1, source_target_pairs={{0,1},{1,0},{2,3},{3,2},{4,5},{5,4},{6,7},{7,6},{8,9},{9,8},{10,11... | collective-permute-start | bytes 1179656 | tf_op jit(solution)/shard_map/ppermute | solution.py:226
  268.9 37.0 %collective-permute-start.70 = (bf16[1,256,768]{2,1,0:T(8,128)(2,1)}, bf16[1,256,768]{2,1,0:T(8,128)(2,1)}, u32[]{:S(2)}, u32[]{:S(2)}) collective-permute-start(bf16[1,256,768]{2,1,0:T(8,128)(2,1)} %get-tuple-element.221), channel_id=1, source_target_pairs={{0,8},{4,20},{8,0},{12,28},{16,24},{20,4},{24,16},{28,12},{1,9},{5... | collective-permute-start | bytes 1179656 | tf_op jit(solution)/shard_map/ppermute | solution.py:195
  280.5 27.2 %collective-permute-start.64 = (bf16[2,96,4096]{2,1,0:T(8,128)(2,1)}, bf16[2,96,4096]{2,1,0:T(8,128)(2,1)}, u32[]{:S(2)}, u32[]{:S(2)}) collective-permute-start(bf16[2,96,4096]{2,1,0:T(8,128)(2,1)} %get-tuple-element.200), channel_id=1, source_target_pairs={{0,16},{4,12},{8,24},{12,4},{16,0},{20,28},{24,8},{28,20},{1,17},{... | collective-permute-start | bytes 4718600 | tf_op jit(solution)/shard_map/ppermute | solution.py:195
  305.9 79.2 %collective-permute-start.58 = (bf16[256,768]{1,0:T(8,128)(2,1)}, bf16[256,768]{1,0:T(8,128)(2,1)}, u32[]{:S(2)}, u32[]{:S(2)}) collective-permute-start(bf16[256,768]{1,0:T(8,128)(2,1)} %add_convert_fusion.22), channel_id=1, source_target_pairs={{0,2},{1,3},{2,0},{3,1},{4,6},{5,7},{6,4},{7,5},{8,10},{9,11},{10,... | collective-permute-start | bytes 1179656 | tf_op jit(solution)/shard_map/ppermute | solution.py:226
  310.9 30.8 %collective-permute-start.65 = (bf16[1,96,4096]{2,1,0:T(8,128)(2,1)}, bf16[1,96,4096]{2,1,0:T(8,128)(2,1)}, u32[]{:S(2)}, u32[]{:S(2)}) collective-permute-start(bf16[1,96,4096]{2,1,0:T(8,128)(2,1)} %get-tuple-element.215), channel_id=1, source_target_pairs={{0,8},{4,20},{8,0},{12,28},{16,24},{20,4},{24,16},{28,12},{1,9},{5... | collective-permute-start | bytes 2359304 | tf_op jit(solution)/shard_map/ppermute | solution.py:195
  334.9 44.5 %collective-permute-start.71 = (bf16[128,768]{1,0:T(8,128)(2,1)S(1)}, bf16[128,768]{1,0:T(8,128)(2,1)S(1)}, u32[]{:S(2)}, u32[]{:S(2)}) collective-permute-start(bf16[128,768]{1,0:T(8,128)(2,1)S(1)} %copy-done.79), channel_id=1, source_target_pairs={{0,2},{1,3},{2,0},{3,1},{4,6},{5,7},{6,4},{7,5},{8,10},{9,11},{10,... | collective-permute-start | bytes 589832 | tf_op jit(solution)/shard_map/ppermute | solution.py:144
  340.8 22.6 %collective-permute-start.49 = (bf16[2,96,2304]{2,1,0:T(8,128)(2,1)S(1)}, bf16[2,96,2304]{2,1,0:T(8,128)(2,1)S(1)}, u32[]{:S(2)}, u32[]{:S(2)}) collective-permute-start(bf16[2,96,2304]{2,1,0:T(8,128)(2,1)S(1)} %copy-done.62), channel_id=1, source_target_pairs={{0,16},{4,12},{8,24},{12,4},{16,0},{20,28},{24,8},{28,20},{1,17},{... | collective-permute-start | bytes 2654216 | tf_op jit(solution)/shard_map/ppermute | solution.py:195
  347.0 22.3 %collective-permute-start.52 = (bf16[1,96,3968]{2,1,0:T(8,128)(2,1)S(1)}, bf16[1,96,3968]{2,1,0:T(8,128)(2,1)S(1)}, u32[]{:S(2)}, u32[]{:S(2)}) collective-permute-start(bf16[1,96,3968]{2,1,0:T(8,128)(2,1)S(1)} %get-tuple-element.217), channel_id=1, source_target_pairs={{0,8},{4,20},{8,0},{12,28},{16,24},{20,4},{24,16},{28,12},{1,9},{5... | collective-permute-start | bytes 2285576 | tf_op jit(solution)/shard_map/ppermute | solution.py:195
  348.5 50.4 %collective-permute-start.68 = (bf16[24,4096]{1,0:T(8,128)(2,1)}, bf16[24,4096]{1,0:T(8,128)(2,1)}, u32[]{:S(2)}, u32[]{:S(2)}) collective-permute-start(bf16[24,4096]{1,0:T(8,128)(2,1)} %get-tuple-element.232), channel_id=1, source_target_pairs={{0,3},{1,2},{2,1},{3,0},{4,7},{5,6},{6,5},{7,4},{8,11},{9,10},{10,... | collective-permute-start | bytes 589832 | tf_op jit(solution)/shard_map/ppermute | solution.py:144
  363.5 38.4 %collective-permute-start.67 = (bf16[24,4096]{1,0:T(8,128)(2,1)}, bf16[24,4096]{1,0:T(8,128)(2,1)}, u32[]{:S(2)}, u32[]{:S(2)}) collective-permute-start(bf16[24,4096]{1,0:T(8,128)(2,1)} %get-tuple-element.233), channel_id=1, source_target_pairs={{0,2},{1,3},{2,0},{3,1},{4,6},{5,7},{6,4},{7,5},{8,10},{9,11},{10,... | collective-permute-start | bytes 589832 | tf_op jit(solution)/shard_map/ppermute | solution.py:144
  380.0 21.9 %collective-permute-start.66 = (bf16[24,4096]{1,0:T(8,128)(2,1)}, bf16[24,4096]{1,0:T(8,128)(2,1)}, u32[]{:S(2)}, u32[]{:S(2)}) collective-permute-start(bf16[24,4096]{1,0:T(8,128)(2,1)} %get-tuple-element.234), channel_id=1, source_target_pairs={{0,1},{1,0},{2,3},{3,2},{4,5},{5,4},{6,7},{7,6},{8,9},{9,8},{10,11... | collective-permute-start | bytes 589832 | tf_op jit(solution)/shard_map/ppermute | solution.py:144
  (188 other events, 1842.5 us)
Sparse Core Ops, SparseCore 0:
  11.5 74.3 all-gather.1
  228.7 120.3 reduce-scatter.1

commit v5 on v4

--- a/solution.py
+++ b/solution.py
@@ -562,7 +562,7 @@
     (second_z,) = place_seq([gate(second, light_kv, light_q)] + got_second)
     second_held = {(): second_z}
     wave(second_held, 0)
-    sum_kv.add(light_kv)
+    sum_kv.add()
     light_mixed, light_probs = attend(
         gate(light_q, second_z), light_kv, seg_f, key_seg, L_HEAD, WINDOW, WINDOW, bf16
     )
@@ -619,13 +619,12 @@
     normed_ffn_grad = dot_nt(light_pre_grad, w_lgu)
 
     grad_ldown = merged(fold(grad_ldown.reshape(dp * seq, -1, width), rows))
-    light_sum = lax.psum_scatter(
-        jnp.concatenate([grad_lgu, grad_ldown], axis=1), ("dp", "seq"), scatter_dimension=0, tiled=True
-    )
+    light_grads = jnp.concatenate([grad_lgu, grad_ldown], axis=1)
+    light_sum = lax.psum_scatter(light_grads, ("dp", "seq"), scatter_dimension=0, tiled=True)
     for h in range(1, hops):
         wave(gu_held, h, light_ffn)
         wave(down_held, h, light_ffn)
-    ffn_rows = sum_rows.finish(normed_ffn_grad, light_ffn)
+    ffn_rows = sum_rows.finish(normed_ffn_grad, light_ffn, light_grads)
     cot_rows = sum_cot.finish(normed_ffn_grad, light_ffn)
     (w_hgu,) = place_dp(gu_held, [gu_z.shape[1]], ffn_rows)
     (w_hdown,) = place_dp(down_held, [width], ffn_rows)
@@ -700,7 +699,7 @@
         light_q,
         light_kv,
         light_probs,
-        gate(mixed_grad, sum_attn.keep, kv_send, out_part),
+        gate(mixed_grad, sum_attn.keep),
         L_HEAD,
         WINDOW,
         WINDOW,

time: 426 us -> 416 us (0.977)
  waiting for transfers between devices: 93.3 us -> 76.7 us
    ppermute x8, waiting for transfers between devices: 29.4 us -> 15.7 us  [send(): self.got = lax.ppermute(self.part, 'seq', pairs)]
    ppermute x20, starting transfers between devices: 44.2 us -> 39.5 us  [send_seq(): lax.ppermute(piece_for(k), 'seq', perm_seq(count, k))]
    unnamed x280 -> x274, local copies, waits for them, and re-layouts: 17.8 us -> 22.3 us
  transfers between devices with their start and end apart: 74 -> 74, of which waited for: 18 -> 17; matrix products, arithmetic and copies ran while one was open for 32% -> 32% of each run, Pallas kernels for 14% -> 14%
where the time goes in v5:
time: 416 us; the launch traced here: 409 us
  starting transfers between devices  84.4 us (20%)
  waiting for transfers between devices  76.7 us (18%)
  matrix products  73.4 us (18%)
  Pallas kernels  61.7 us (15%)
  other arithmetic  60.5 us (15%)
  local copies, waits for them, and re-layouts  35.6 us (9%)
  between operations  16.6 us (4%)
    ppermute x20, starting transfers between devices, send_seq(): lax.ppermute(piece_for(k), 'seq', perm_seq(count, k))  39.5 us
    dot_general x15, matrix products, dot_tn(): lax.dot_general(a, b, (((0,), (0,)), ((), ())), preferred_element_type=f32)  29.3 us
    pallas_call x12, Pallas kernels, dma_moves(): pl.pallas_call(body, out_shape=[jax.ShapeDtypeStruct(s, a) for s, a in ou...  26.4 us
    dot_general x14, matrix products, dot(): lax.dot_general(a, b, (((1,), (0,)), ((), ())), preferred_element_type=f32)  23.8 us
    unnamed x274, local copies, waits for them, and re-layouts  22.3 us
    ppermute x28, waiting for transfers between devices, wave(): lax.ppermute(pieces[label], 'dp', perm(count, stages[stage]))  21.4 us
    dot_general x9, matrix products, dot_nt(): lax.dot_general(a, b, (((1,), (1,)), ((), ())), preferred_element_type=f32)  20.3 us
    ppermute x12, waiting for transfers between devices, hop(): self.got = lax.ppermute(send, 'dp', perm(count, self.left.pop()))  20.1 us
  transfers between devices with their start and end apart: 74, of which 17 were waited for; matrix products, arithmetic and copies ran while one was open for 32% of the time, Pallas kernels for 14%

profile of v5, /device:TPU:0, one launch (start us, length us, event | category | flops | bytes accessed | tf_op | source)
XLA Modules:
  0.0 408.8 jit_solution(15721215206271487608)
XLA Ops:
  12.2 5.1 %collective-permute-start.4 = (bf16[24,2432]{1,0:T(8,128)(2,1)S(1)}, bf16[24,2432]{1,0:T(8,128)(2,1)S(1)}, u32[]{:S(2)}, u32[]{:S(2)}) collective-permute-start(bf16[24,2432]{1,0:T(8,128)(2,1)S(1)} %fusion.110.refs_0_), channel_id=1, source_target_pairs={{0,3},{1,2},{2,1},{3,0},{4,7},{5,6},{6,5},{7,4},{8,11},{9,10},{10,... | collective-permute-start | bytes 350216 | tf_op jit(solution)/shard_map/ppermute | solution.py:144
  20.7 4.0 collective-permute-start
  33.0 8.5 %collective-permute-done.5.refs_1_ = bf16[96,2432]{1,0:T(8,128)(2,1)S(1)} collective-permute-done((bf16[96,2432]{1,0:T(8,128)(2,1)S(1)}, bf16[96,2432]{1,0:T(8,128)(2,1)S(1)}, u32[]{:S(2)}, u32[]{:S(2)}) %collective-permute-start.5) | collective-permute-done | bytes 466976 | tf_op jit(solution)/shard_map/ppermute | solution.py:155
  45.8 5.0 %collective-permute-start.14 = (bf16[24,3840]{1,0:T(8,128)(2,1)S(1)}, bf16[24,3840]{1,0:T(8,128)(2,1)S(1)}, u32[]{:S(2)}, u32[]{:S(2)}) collective-permute-start(bf16[24,3840]{1,0:T(8,128)(2,1)S(1)} %constant_dynamic-update-slice_fusion.refs_0_), channel_id=1, source_target_pairs={{0,3},{1,2},{2,1},{3,0},{4,7},{5,6},{6,5},{7,4},{8,11},{9,10},{10,... | collective-permute-start | bytes 552968 | tf_op jit(solution)/shard_map/ppermute | solution.py:144
  64.5 4.1 convolution_convert_fusion.5.kv_ref
  80.3 9.4 %collective-permute-done.22 = bf16[256,896]{1,0:T(8,128)(2,1)} collective-permute-done((bf16[256,896]{1,0:T(8,128)(2,1)}, bf16[256,896]{1,0:T(8,128)(2,1)}, u32[]{:S(2)}, u32[]{:S(2)}) %collective-permute-start.22) | collective-permute-done | bytes 458784 | tf_op jit(solution)/shard_map/ppermute | solution.py:226
  95.9 10.8 %shard_map.275 = (bf16[512,768]{1,0:T(8,128)(2,1)S(1)}, bf16[8,512,384]{2,1,0:T(8,128)(2,1)S(1)}) custom-call(bf16[512,768]{1,0:T(8,128)(2,1)S(1)} %convolution_convert_fusion.15.q_ref, bf16[768,1536]{1,0:T(8,128)(2,1)S(1)} %convolution_convert_fusion.5.kv_ref, f32[512,1]{1,0:T(8,128)S(1)} %copy.62.q_seg_ref, f32[1,768]{1,0:T(1,128)S(1)} %or_select_fusion.k_seg_ref), custom_call_target="tpu_custom_call" | custom-call | flops 603979776 | bytes 7077888 | tf_op jit(solution)/shard_map/pallas_call | solution.py:390
  113.5 5.0 %collective-permute-done.17.refs_3_ = bf16[96,3840]{1,0:T(8,128)(2,1)S(1)} collective-permute-done((bf16[96,3840]{1,0:T(8,128)(2,1)}, bf16[96,3840]{1,0:T(8,128)(2,1)S(1)}, u32[]{:S(2)}, u32[]{:S(2)}) %collective-permute-start.17) | collective-permute-done | bytes 737312 | tf_op jit(solution)/shard_map/ppermute | solution.py:155
  133.9 8.6 %collective-permute-done.36.refs_1_ = bf16[128,768]{1,0:T(8,128)(2,1)S(1)} collective-permute-done((bf16[128,768]{1,0:T(8,128)(2,1)S(1)}, bf16[128,768]{1,0:T(8,128)(2,1)S(1)}, u32[]{:S(2)}, u32[]{:S(2)}) %collective-permute-start.36) | collective-permute-done | bytes 196640 | tf_op jit(solution)/shard_map/ppermute | solution.py:144
  179.7 5.4 %collective-permute-done.30.refs_3_ = bf16[96,4096]{1,0:T(8,128)(2,1)} collective-permute-done((bf16[96,4096]{1,0:T(8,128)(2,1)}, bf16[96,4096]{1,0:T(8,128)(2,1)}, u32[]{:S(2)}, u32[]{:S(2)}) %collective-permute-start.30) | collective-permute-done | bytes 786464 | tf_op jit(solution)/shard_map/ppermute | solution.py:155
  200.2 3.9 shard_map.280
  229.9 3.6 collective-permute-done.44
  239.6 4.9 %add_convert_fusion = (bf16[2,96,4096]{2,1,0:T(8,128)(2,1)}, bf16[2,96,4096]{2,1,0:T(8,128)(2,1)}) fusion(bf16[4,96,4096]{2,1,0:T(8,128)(2,1)} %collective-permute-done.45, bf16[4,96,4096]{2,1,0:T(8,128)(2,1)S(1)} %copy-done.10), kind=kLoop, calls=%fused_computation.7 | loop fusion | flops 6291456 | bytes 9437184 | tf_op jit(solution)/shard_map/convert_element_type | solution.py:201
  250.9 4.7 %shard_map.285 = (bf16[256,768]{1,0:T(8,128)(2,1)S(1)}, bf16[256,1536]{1,0:T(8,128)(2,1)S(1)}) custom-call(bf16[256,768]{1,0:T(8,128)(2,1)S(1)} %copy-done.27, bf16[256,1536]{1,0:T(8,128)(2,1)S(1)} %copy-done.20, bf16[12,256,256]{2,1,0:T(8,128)(2,1)S(1)} %copy-done.14, bf16[256,768]{1,0:T(8,128)(2,1)S(1)} %get-tuple-element.235.grad_ref), custom_call_target="tpu_custom_call" | custom-call | flops 402653184 | bytes 4325376 | tf_op jit(solution)/shard_map/pallas_call | solution.py:453
  261.6 3.6 fusion.49
  271.0 3.4 shard_map.286
  277.1 13.7 %shard_map.287 = (bf16[512,768]{1,0:T(8,128)(2,1)S(1)}, bf16[768,1536]{1,0:T(8,128)(2,1)S(1)}) custom-call(bf16[512,768]{1,0:T(8,128)(2,1)S(1)} %copy-done.8, bf16[768,1536]{1,0:T(8,128)(2,1)S(1)} %convolution_convert_fusion.5.kv_ref, bf16[8,512,384]{2,1,0:T(8,128)(2,1)S(1)} %copy-done.4, bf16[512,768]{1,0:T(8,128)(2,1)S(1)} %copy-done.18), custom_call_target="tpu_custom_call" | custom-call | flops 1207959552 | bytes 10223616 | tf_op jit(solution)/shard_map/pallas_call | solution.py:453
  306.5 3.5 fusion.30
  322.4 3.3 fusion.39
  325.9 6.1 %collective-permute-start.71 = (bf16[128,768]{1,0:T(8,128)(2,1)S(1)}, bf16[128,768]{1,0:T(8,128)(2,1)S(1)}, u32[]{:S(2)}, u32[]{:S(2)}) collective-permute-start(bf16[128,768]{1,0:T(8,128)(2,1)S(1)} %copy-done.84), channel_id=1, source_target_pairs={{0,2},{1,3},{2,0},{3,1},{4,6},{5,7},{6,4},{7,5},{8,10},{9,11},{10,... | collective-permute-start | bytes 589832 | tf_op jit(solution)/shard_map/ppermute | solution.py:144
  342.3 11.1 %collective-permute-done.49 = bf16[2,96,2304]{2,1,0:T(8,128)(2,1)S(1)} collective-permute-done((bf16[2,96,2304]{2,1,0:T(8,128)(2,1)S(1)}, bf16[2,96,2304]{2,1,0:T(8,128)(2,1)S(1)}, u32[]{:S(2)}, u32[]{:S(2)}) %collective-permute-start.49) | collective-permute-done | bytes 884768 | tf_op jit(solution)/shard_map/ppermute | solution.py:195
  356.8 7.3 %collective-permute-done.53 = bf16[1,96,2304]{2,1,0:T(8,128)(2,1)S(1)} collective-permute-done((bf16[1,96,2304]{2,1,0:T(8,128)(2,1)S(1)}, bf16[1,96,2304]{2,1,0:T(8,128)(2,1)S(1)}, u32[]{:S(2)}, u32[]{:S(2)}) %collective-permute-start.53) | collective-permute-done | bytes 442400 | tf_op jit(solution)/shard_map/ppermute | solution.py:195
  368.5 3.6 collective-permute-done.54
  391.5 6.2 %collective-permute-done.62 = bf16[24,3968]{1,0:T(8,128)(2,1)S(1)} collective-permute-done((bf16[24,3968]{1,0:T(8,128)(2,1)S(1)}, bf16[24,3968]{1,0:T(8,128)(2,1)S(1)}, u32[]{:S(2)}, u32[]{:S(2)}) %collective-permute-start.62) | collective-permute-done | bytes 190496 | tf_op jit(solution)/shard_map/ppermute | solution.py:144
  (562 shorter events, 247.5 us)
Async XLA Ops:
  7.3 153.4 %all-gather.2.cloned.1.call-start = ((), (), s32[]{:S(2)}) async-start(), calls=%async_computation.1 | async-start | bytes 4866048 | tf_op jit(solution)/shard_map/all_gather | solution.py:524
  10.5 361.6 %reduce-scatter.2.cloned.1.call-start = ((), (), s32[]{:S(2)}) async-start(), calls=%async_computation.2 | async-start | bytes 4866048 | tf_op jit(solution)/shard_map/reduce_scatter | solution.py:623
  20.7 31.5 %collective-permute-start = (bf16[128,896]{1,0:T(8,128)(2,1)}, bf16[128,896]{1,0:T(8,128)(2,1)}, u32[]{:S(2)}, u32[]{:S(2)}) collective-permute-start(bf16[128,896]{1,0:T(8,128)(2,1)} %get-tuple-element.228), channel_id=1, source_target_pairs={{0,1},{1,2},{2,3},{4,5},{5,6},{6,7},{8,9},{9,10},{10,11},{12,13},{... | collective-permute-start | bytes 688136 | tf_op jit(solution)/shard_map/ppermute | solution.py:528
  24.7 27.5 %collective-permute-start.1 = (bf16[128,896]{1,0:T(8,128)(2,1)}, bf16[128,896]{1,0:T(8,128)(2,1)}, u32[]{:S(2)}, u32[]{:S(2)}) collective-permute-start(bf16[128,896]{1,0:T(8,128)(2,1)} %get-tuple-element.229), channel_id=1, source_target_pairs={{1,0},{2,1},{3,2},{5,4},{6,5},{7,6},{9,8},{10,9},{11,10},{13,12},{... | collective-permute-start | bytes 688136 | tf_op jit(solution)/shard_map/ppermute | solution.py:529
  45.8 24.9 %collective-permute-start.14 = (bf16[24,3840]{1,0:T(8,128)(2,1)S(1)}, bf16[24,3840]{1,0:T(8,128)(2,1)S(1)}, u32[]{:S(2)}, u32[]{:S(2)}) collective-permute-start(bf16[24,3840]{1,0:T(8,128)(2,1)S(1)} %constant_dynamic-update-slice_fusion.refs_0_), channel_id=1, source_target_pairs={{0,3},{1,2},{2,1},{3,0},{4,7},{5,6},{6,5},{7,4},{8,11},{9,10},{10,... | collective-permute-start | bytes 552968 | tf_op jit(solution)/shard_map/ppermute | solution.py:144
  58.3 31.4 %collective-permute-start.22 = (bf16[256,896]{1,0:T(8,128)(2,1)}, bf16[256,896]{1,0:T(8,128)(2,1)}, u32[]{:S(2)}, u32[]{:S(2)}) collective-permute-start(bf16[256,896]{1,0:T(8,128)(2,1)} %convolution_convert_fusion.16), channel_id=1, source_target_pairs={{0,1},{1,0},{2,3},{3,2},{4,5},{5,4},{6,7},{7,6},{8,9},{9,8},{10,11... | collective-permute-start | bytes 1376264 | tf_op jit(solution)/shard_map/ppermute | solution.py:226
  74.2 32.5 %collective-permute-start.15 = (bf16[96,3840]{1,0:T(8,128)(2,1)}, bf16[96,3840]{1,0:T(8,128)(2,1)}, u32[]{:S(2)}, u32[]{:S(2)}) collective-permute-start(bf16[96,3840]{1,0:T(8,128)(2,1)} %bitcast.21.refs_0_), channel_id=1, source_target_pairs={{0,8},{4,20},{8,0},{12,28},{16,24},{20,4},{24,16},{28,12},{1,9},{5... | collective-permute-start | bytes 2211848 | tf_op jit(solution)/shard_map/ppermute | solution.py:155
  107.4 39.2 %collective-permute-start.27 = (bf16[24,4096]{1,0:T(8,128)(2,1)S(1)}, bf16[24,4096]{1,0:T(8,128)(2,1)S(1)}, u32[]{:S(2)}, u32[]{:S(2)}) collective-permute-start(bf16[24,4096]{1,0:T(8,128)(2,1)S(1)} %copy-done.134), channel_id=1, source_target_pairs={{0,3},{1,2},{2,1},{3,0},{4,7},{5,6},{6,5},{7,4},{8,11},{9,10},{10,... | collective-permute-start | bytes 589832 | tf_op jit(solution)/shard_map/ppermute | solution.py:144
  119.8 26.8 %collective-permute-start.25 = (bf16[24,4096]{1,0:T(8,128)(2,1)S(1)}, bf16[24,4096]{1,0:T(8,128)(2,1)S(1)}, u32[]{:S(2)}, u32[]{:S(2)}) collective-permute-start(bf16[24,4096]{1,0:T(8,128)(2,1)S(1)} %copy-done.134), channel_id=1, source_target_pairs={{0,1},{1,0},{2,3},{3,2},{4,5},{5,4},{6,7},{7,6},{8,9},{9,8},{10,11... | collective-permute-start | bytes 589832 | tf_op jit(solution)/shard_map/ppermute | solution.py:144
  121.9 22.4 %collective-permute-start.26 = (bf16[24,4096]{1,0:T(8,128)(2,1)S(1)}, bf16[24,4096]{1,0:T(8,128)(2,1)S(1)}, u32[]{:S(2)}, u32[]{:S(2)}) collective-permute-start(bf16[24,4096]{1,0:T(8,128)(2,1)S(1)} %copy-done.34), channel_id=1, source_target_pairs={{0,2},{1,3},{2,0},{3,1},{4,6},{5,7},{6,4},{7,5},{8,10},{9,11},{10,... | collective-permute-start | bytes 589832 | tf_op jit(solution)/shard_map/ppermute | solution.py:144
  143.6 42.6 %collective-permute-start.40 = (bf16[256,768]{1,0:T(8,128)(2,1)S(1)}, bf16[256,768]{1,0:T(8,128)(2,1)}, u32[]{:S(2)}, u32[]{:S(2)}) collective-permute-start(bf16[256,768]{1,0:T(8,128)(2,1)S(1)} %bitcast.175), channel_id=1, source_target_pairs={{0,4},{4,0},{8,12},{12,8},{16,20},{20,16},{24,28},{28,24},{1,5},{5... | collective-permute-start | bytes 1179656 | tf_op jit(solution)/shard_map/ppermute | solution.py:155
  143.7 28.0 %collective-permute-start.38 = (bf16[256,768]{1,0:T(8,128)(2,1)S(1)}, bf16[256,768]{1,0:T(8,128)(2,1)}, u32[]{:S(2)}, u32[]{:S(2)}) collective-permute-start(bf16[256,768]{1,0:T(8,128)(2,1)S(1)} %bitcast.176), channel_id=1, source_target_pairs={{0,16},{4,12},{8,24},{12,4},{16,0},{20,28},{24,8},{28,20},{1,17},{... | collective-permute-start | bytes 1179656 | tf_op jit(solution)/shard_map/ppermute | solution.py:155
  144.3 27.4 %collective-permute-start.37 = (bf16[256,768]{1,0:T(8,128)(2,1)S(1)}, bf16[256,768]{1,0:T(8,128)(2,1)}, u32[]{:S(2)}, u32[]{:S(2)}) collective-permute-start(bf16[256,768]{1,0:T(8,128)(2,1)S(1)} %bitcast.177), channel_id=1, source_target_pairs={{0,8},{4,20},{8,0},{12,28},{16,24},{20,4},{24,16},{28,12},{1,9},{5... | collective-permute-start | bytes 1179656 | tf_op jit(solution)/shard_map/ppermute | solution.py:155
  149.1 29.1 %collective-permute-start.29 = (bf16[96,4096]{1,0:T(8,128)(2,1)}, bf16[96,4096]{1,0:T(8,128)(2,1)}, u32[]{:S(2)}, u32[]{:S(2)}) collective-permute-start(bf16[96,4096]{1,0:T(8,128)(2,1)} %bitcast.41.refs_0_), channel_id=1, source_target_pairs={{0,16},{4,12},{8,24},{12,4},{16,0},{20,28},{24,8},{28,20},{1,17},{... | collective-permute-start | bytes 2359304 | tf_op jit(solution)/shard_map/ppermute | solution.py:155
  233.7 61.2 %collective-permute-start.47 = (bf16[256,768]{1,0:T(8,128)(2,1)}, bf16[256,768]{1,0:T(8,128)(2,1)}, u32[]{:S(2)}, u32[]{:S(2)}) collective-permute-start(bf16[256,768]{1,0:T(8,128)(2,1)} %convolution_convert_fusion.19), channel_id=1, source_target_pairs={{0,1},{1,0},{2,3},{3,2},{4,5},{5,4},{6,7},{7,6},{8,9},{9,8},{10,11... | collective-permute-start | bytes 1179656 | tf_op jit(solution)/shard_map/ppermute | solution.py:226
  238.6 28.8 %collective-permute-start.69 = (bf16[2,256,768]{2,1,0:T(8,128)(2,1)}, bf16[2,256,768]{2,1,0:T(8,128)(2,1)}, u32[]{:S(2)}, u32[]{:S(2)}) collective-permute-start(bf16[2,256,768]{2,1,0:T(8,128)(2,1)} %get-tuple-element.210), channel_id=1, source_target_pairs={{0,16},{4,12},{8,24},{12,4},{16,0},{20,28},{24,8},{28,20},{1,17},{... | collective-permute-start | bytes 2359304 | tf_op jit(solution)/shard_map/ppermute | solution.py:195
  257.2 40.1 %collective-permute-start.57 = (bf16[256,768]{1,0:T(8,128)(2,1)}, bf16[256,768]{1,0:T(8,128)(2,1)}, u32[]{:S(2)}, u32[]{:S(2)}) collective-permute-start(bf16[256,768]{1,0:T(8,128)(2,1)} %fusion.44), channel_id=1, source_target_pairs={{0,1},{1,0},{2,3},{3,2},{4,5},{5,4},{6,7},{7,6},{8,9},{9,8},{10,11... | collective-permute-start | bytes 1179656 | tf_op jit(solution)/shard_map/ppermute | solution.py:226
  268.9 32.2 %collective-permute-start.70 = (bf16[1,256,768]{2,1,0:T(8,128)(2,1)S(1)}, bf16[1,256,768]{2,1,0:T(8,128)(2,1)S(1)}, u32[]{:S(2)}, u32[]{:S(2)}) collective-permute-start(bf16[1,256,768]{2,1,0:T(8,128)(2,1)S(1)} %get-tuple-element.219), channel_id=1, source_target_pairs={{0,8},{4,20},{8,0},{12,28},{16,24},{20,4},{24,16},{28,12},{1,9},{5... | collective-permute-start | bytes 1179656 | tf_op jit(solution)/shard_map/ppermute | solution.py:195
  276.0 26.0 %collective-permute-start.64 = (bf16[2,96,4096]{2,1,0:T(8,128)(2,1)S(1)}, bf16[2,96,4096]{2,1,0:T(8,128)(2,1)S(1)}, u32[]{:S(2)}, u32[]{:S(2)}) collective-permute-start(bf16[2,96,4096]{2,1,0:T(8,128)(2,1)S(1)} %copy-done.56), channel_id=1, source_target_pairs={{0,16},{4,12},{8,24},{12,4},{16,0},{20,28},{24,8},{28,20},{1,17},{... | collective-permute-start | bytes 4718600 | tf_op jit(solution)/shard_map/ppermute | solution.py:195
  299.3 72.8 %collective-permute-start.58 = (bf16[256,768]{1,0:T(8,128)(2,1)}, bf16[256,768]{1,0:T(8,128)(2,1)}, u32[]{:S(2)}, u32[]{:S(2)}) collective-permute-start(bf16[256,768]{1,0:T(8,128)(2,1)} %add_convert_fusion.22), channel_id=1, source_target_pairs={{0,2},{1,3},{2,0},{3,1},{4,6},{5,7},{6,4},{7,5},{8,10},{9,11},{10,... | collective-permute-start | bytes 1179656 | tf_op jit(solution)/shard_map/ppermute | solution.py:226
  303.6 30.9 %collective-permute-start.65 = (bf16[1,96,4096]{2,1,0:T(8,128)(2,1)}, bf16[1,96,4096]{2,1,0:T(8,128)(2,1)}, u32[]{:S(2)}, u32[]{:S(2)}) collective-permute-start(bf16[1,96,4096]{2,1,0:T(8,128)(2,1)} %get-tuple-element.213), channel_id=1, source_target_pairs={{0,8},{4,20},{8,0},{12,28},{16,24},{20,4},{24,16},{28,12},{1,9},{5... | collective-permute-start | bytes 2359304 | tf_op jit(solution)/shard_map/ppermute | solution.py:195
  325.9 41.0 %collective-permute-start.71 = (bf16[128,768]{1,0:T(8,128)(2,1)S(1)}, bf16[128,768]{1,0:T(8,128)(2,1)S(1)}, u32[]{:S(2)}, u32[]{:S(2)}) collective-permute-start(bf16[128,768]{1,0:T(8,128)(2,1)S(1)} %copy-done.84), channel_id=1, source_target_pairs={{0,2},{1,3},{2,0},{3,1},{4,6},{5,7},{6,4},{7,5},{8,10},{9,11},{10,... | collective-permute-start | bytes 589832 | tf_op jit(solution)/shard_map/ppermute | solution.py:144
  340.7 45.2 %collective-permute-start.68 = (bf16[24,4096]{1,0:T(8,128)(2,1)}, bf16[24,4096]{1,0:T(8,128)(2,1)}, u32[]{:S(2)}, u32[]{:S(2)}) collective-permute-start(bf16[24,4096]{1,0:T(8,128)(2,1)} %get-tuple-element.230), channel_id=1, source_target_pairs={{0,3},{1,2},{2,1},{3,0},{4,7},{5,6},{6,5},{7,4},{8,11},{9,10},{10,... | collective-permute-start | bytes 589832 | tf_op jit(solution)/shard_map/ppermute | solution.py:144
  353.4 34.4 %collective-permute-start.67 = (bf16[24,4096]{1,0:T(8,128)(2,1)}, bf16[24,4096]{1,0:T(8,128)(2,1)}, u32[]{:S(2)}, u32[]{:S(2)}) collective-permute-start(bf16[24,4096]{1,0:T(8,128)(2,1)} %get-tuple-element.231), channel_id=1, source_target_pairs={{0,2},{1,3},{2,0},{3,1},{4,6},{5,7},{6,4},{7,5},{8,10},{9,11},{10,... | collective-permute-start | bytes 589832 | tf_op jit(solution)/shard_map/ppermute | solution.py:144
  (185 other events, 1857.8 us)
Sparse Core Ops, SparseCore 0:
  11.5 77.7 all-gather.1
  221.8 129.4 reduce-scatter.1
